TPU v7x, 32 devices: a whole 2x2x4 slice. The times are simulated.
32 devices in a mesh: dp: 4 (over z), fsdp: 8 (over y, x, core).
Axes of the slice: x: 2, y: 2, z: 4, core: 2. Of those that a mesh axis runs over, the one named last changes fastest.
Arguments:
- tokens: bfloat16 [32768, 512], P(('dp', 'fsdp')), may hold values from -6 to 6
- halt_in: float32 [32768], P(('dp', 'fsdp')), may hold values from 0 to 0.7
- depths: int32 [32768], P(('dp', 'fsdp')), may hold values from 1 to 8, as said below
- attn_routes: int32 [32768, 4], P(('dp', 'fsdp')), may hold values from 0 to 23, all different within a row
- ffn_routes: int32 [32768, 2], P(('dp', 'fsdp')), may hold values from 0 to 7, all different within a row; in each aligned block of 1024 rows (0 to 1023, 1024 to 2047, ...) at most 512 rows name the same one
- w_query: bfloat16 [512, 1536], P(('dp', 'fsdp')), may hold values from -0.25 to 0.25
- w_out: bfloat16 [1536, 512], P(None, ('dp', 'fsdp')), may hold values from -12 to 12
- w_kv: bfloat16 [512, 128], P(('dp', 'fsdp')), may hold values from -0.25 to 0.25
- router: bfloat16 [512, 32], P(('dp', 'fsdp')), may hold values from -0.15820312 to 0.15820312
- vectors: bfloat16 [5, 512], P(None, ('dp', 'fsdp')), may hold values from -1 to 2
- w_up: bfloat16 [8, 512, 2048], P('fsdp', None, 'dp'), may hold values from -0.25 to 0.25
- w_down: bfloat16 [8, 2048, 512], P('fsdp', 'dp'), may hold values from -0.25 to 0.25
- cot_out: bfloat16 [32768, 512], P(('dp', 'fsdp')), may hold values from -6 to 6
- cot_halt: float32 [32768], P(('dp', 'fsdp')), may hold values from -6 to 6
Outputs:
- block_out: bfloat16 [32768, 512], P(('dp', 'fsdp'))
- halt_out: float32 [32768], P(('dp', 'fsdp'))
- grad_in: bfloat16 [32768, 512], P(('dp', 'fsdp'))
- grad_query: float32 [512, 1536], P(('dp', 'fsdp'))
- grad_out_proj: float32 [1536, 512], P(None, ('dp', 'fsdp'))
- grad_kv: float32 [512, 128], P(('dp', 'fsdp'))
- grad_router: float32 [512, 32], P(('dp', 'fsdp'))
- grad_vectors: float32 [5, 512], P(None, ('dp', 'fsdp'))
- grad_up: float32 [8, 512, 2048], P('fsdp', None, 'dp')
- grad_down: float32 [8, 2048, 512], P('fsdp', 'dp')
Inputs may be any that keep to these rules, and one draw needn't show every extreme that they name: `depths`: halting depth of each token; the first token of every sequence has depth 8. `attn_routes`: each token names 4 different attention experts. `ffn_routes`: each token names 2 different feed-forward experts; among the 1024 rows of one device no expert is named more than 512 times, and in some devices' rows an expert is named exactly 512 times.
All inputs are finite; a program needn't handle non-finite values.
Results may differ from a plain program's by a relative error of at most 0.019.
Values may be sent and summed in bfloat16 or wider, within the bound.
No kernel may reach another device: no remote copies, remote signals or barrier semaphores. Data moves between devices by JAX's collectives and lax.ppermute only.
A program may use at most 256 MiB of HBM per device.

v0:
```python
from functools import partial

import jax
import jax.numpy as jnp
from jax import lax
from jax.sharding import PartitionSpec as P

D = 512
HEAD = 64
A_EXP = 24
A_TOP = 4
F_TOP = 2
LENGTH = 1024
QUERY_BLOCK = 128
STEP = 2


PRECISE = lax.Precision.HIGHEST
EPSILON = 1e-05


def norm_stats(values):
    center = values - jnp.mean(values, axis=-1, keepdims=True)
    inv_std = lax.rsqrt(jnp.mean(center * center, axis=-1, keepdims=True) + EPSILON)
    return (center * inv_std, inv_std)


def norm_back(grad_normed, normal_part, inv_std, gain_row):
    grad_hat = grad_normed * gain_row
    mean_one = jnp.mean(grad_hat, axis=-1, keepdims=True)
    mean_two = jnp.mean(grad_hat * normal_part, axis=-1, keepdims=True)
    return inv_std * (grad_hat - mean_one - normal_part * mean_two)


def gate_back(gate_probs, grad_gates, pick_table):
    weighted = jnp.sum(gate_probs * grad_gates, axis=1, keepdims=True)
    return jnp.einsum(
        "tk,tke->te", gate_probs * (grad_gates - weighted), pick_table, precision=PRECISE
    )


def slot_table(ffn_routes, active_mask, tok_count, expert_total, capacity):
    pick_bool = (
        ffn_routes[:, :, None] == jnp.arange(expert_total, dtype=jnp.int32)[None, None, :]
    ) & active_mask[:, None, None]
    flat_pick = pick_bool.reshape(tok_count * F_TOP, expert_total).astype(jnp.int32)
    slot_place = jnp.cumsum(flat_pick, axis=0) - 1
    own_place = jnp.sum(flat_pick * slot_place, axis=1)
    expert = ffn_routes.reshape(tok_count * F_TOP)
    is_live = jnp.sum(flat_pick, axis=1) > 0
    slot_dest = jnp.where(is_live, expert * capacity + own_place, expert_total * capacity)
    owners = jnp.arange(tok_count * F_TOP, dtype=jnp.int32) // F_TOP
    slot_source = (
        jnp.full((expert_total * capacity + 1,), tok_count, jnp.int32).at[slot_dest].set(owners)
    )
    return (slot_dest, slot_source[: expert_total * capacity])


def causal_mask(first_row):
    positions = first_row + jnp.arange(QUERY_BLOCK, dtype=jnp.int32)
    return jnp.arange(LENGTH, dtype=jnp.int32)[None, None, :] <= positions[:, None, None]


def attend_block(key_rows, value_rows, block_query, first_row):
    score_scale = HEAD ** (-0.5)
    scores = (
        jnp.einsum("tkh,jh->tkj", block_query, key_rows, preferred_element_type=jnp.float32)
        * score_scale
    )
    scores = jnp.where(causal_mask(first_row), scores, -1e30)
    highest = jnp.max(scores, axis=-1, keepdims=True)
    shifted = jnp.exp(scores - highest)
    totals = jnp.sum(shifted, axis=-1, keepdims=True)
    weights = (shifted / totals).astype(jnp.bfloat16)
    outputs = jnp.einsum("tkj,jh->tkh", weights, value_rows, preferred_element_type=jnp.float32)
    return (outputs, (highest + jnp.log(totals))[:, :, 0])


def attend_sequence(seq_pair):
    seq_query, seq_kv = seq_pair
    key_rows = seq_kv[:, :HEAD]
    value_rows = seq_kv[:, HEAD:]
    block_count = LENGTH // QUERY_BLOCK
    blocks = seq_query.reshape(block_count, QUERY_BLOCK, A_TOP, HEAD)
    firsts = jnp.arange(block_count, dtype=jnp.int32) * QUERY_BLOCK
    outputs, log_totals = lax.map(
        lambda block_item: attend_block(key_rows, value_rows, block_item[0], block_item[1]),
        (blocks, firsts),
    )
    return (outputs.reshape(LENGTH, A_TOP, HEAD), log_totals.reshape(LENGTH, A_TOP))


def attend_back_block(key_rows, value_rows, carried, block_item):
    grad_keys, grad_values = carried
    block_query, block_grad, block_log, first_row = block_item
    score_scale = HEAD ** (-0.5)
    scores = (
        jnp.einsum("tkh,jh->tkj", block_query, key_rows, preferred_element_type=jnp.float32)
        * score_scale
    )
    scores = jnp.where(causal_mask(first_row), scores, -1e30)
    weights = jnp.exp(scores - block_log[:, :, None])
    grad_weights = jnp.einsum(
        "tkh,jh->tkj", block_grad, value_rows, preferred_element_type=jnp.float32
    )
    inner_sum = jnp.sum(weights * grad_weights, axis=-1, keepdims=True)
    grad_scores = (weights * (grad_weights - inner_sum) * score_scale).astype(jnp.bfloat16)
    grad_query = jnp.einsum(
        "tkj,jh->tkh", grad_scores, key_rows, preferred_element_type=jnp.float32
    )
    grad_keys = grad_keys + jnp.einsum(
        "tkj,tkh->jh", grad_scores, block_query, preferred_element_type=jnp.float32
    )
    grad_values = grad_values + jnp.einsum(
        "tkj,tkh->jh", weights.astype(jnp.bfloat16), block_grad, preferred_element_type=jnp.float32
    )
    return ((grad_keys, grad_values), grad_query)


def attend_sequence_back(seq_items):
    seq_query, seq_kv, seq_grad, seq_log = seq_items
    key_rows = seq_kv[:, :HEAD]
    value_rows = seq_kv[:, HEAD:]
    block_count = LENGTH // QUERY_BLOCK
    blocks = (
        seq_query.reshape(block_count, QUERY_BLOCK, A_TOP, HEAD),
        seq_grad.reshape(block_count, QUERY_BLOCK, A_TOP, HEAD),
        seq_log.reshape(block_count, QUERY_BLOCK, A_TOP),
        jnp.arange(block_count, dtype=jnp.int32) * QUERY_BLOCK,
    )
    zero_rows = jnp.zeros((LENGTH, HEAD), jnp.float32)
    carried, grad_blocks = lax.scan(
        partial(attend_back_block, key_rows, value_rows), (zero_rows, zero_rows), blocks
    )
    return (
        grad_blocks.reshape(LENGTH, A_TOP, HEAD),
        jnp.concatenate([carried[0], carried[1]], axis=1),
    )


def exact_gelu(values):
    return jax.nn.gelu(values, approximate=False)


def expert_forward(expert_item):
    expert_rows, expert_up, expert_down = expert_item
    pre_act = jnp.dot(expert_rows, expert_up, preferred_element_type=jnp.float32)
    gelu_low = exact_gelu(pre_act).astype(jnp.bfloat16)
    return jnp.dot(gelu_low, expert_down, preferred_element_type=jnp.float32).astype(jnp.bfloat16)


def expert_back(expert_item):
    expert_rows, expert_up, expert_down, expert_grad = expert_item
    pre_act = jnp.dot(expert_rows, expert_up, preferred_element_type=jnp.float32)
    gelu_value, gelu_pull = jax.vjp(exact_gelu, pre_act)
    gelu_low = gelu_value.astype(jnp.bfloat16)
    grad_down_e = jnp.dot(gelu_low.T, expert_grad, preferred_element_type=jnp.float32)
    grad_gelu = jnp.dot(expert_grad, expert_down.T, preferred_element_type=jnp.float32)
    grad_pre = gelu_pull(grad_gelu)[0].astype(jnp.bfloat16)
    grad_up_e = jnp.dot(expert_rows.T, grad_pre, preferred_element_type=jnp.float32)
    grad_rows_e = jnp.dot(grad_pre, expert_up.T, preferred_element_type=jnp.float32)
    return (grad_up_e, grad_down_e, grad_rows_e)


def on_device(
    tokens,
    halt_in,
    depths,
    attn_routes,
    ffn_routes,
    w_query,
    w_out,
    w_kv,
    router,
    vectors,
    w_up,
    w_down,
    cot_out,
    cot_halt,
):
    group_attn = (
        lax.all_gather(w_query, "fsdp", axis=0, tiled=True),
        lax.all_gather(w_out, "fsdp", axis=1, tiled=True),
        lax.all_gather(w_kv, "fsdp", axis=0, tiled=True),
        lax.all_gather(router, "fsdp", axis=0, tiled=True),
        lax.all_gather(vectors, "fsdp", axis=1, tiled=True),
    )
    whole_query, whole_out, whole_kv, whole_router, whole_vectors = (
        lax.all_gather(group_attn[0], "dp", axis=0, tiled=True),
        lax.all_gather(group_attn[1], "dp", axis=1, tiled=True),
        lax.all_gather(group_attn[2], "dp", axis=0, tiled=True),
        lax.all_gather(group_attn[3], "dp", axis=0, tiled=True),
        lax.all_gather(group_attn[4], "dp", axis=1, tiled=True),
    )
    whole_up, whole_down = (
        lax.all_gather(w_up, "dp", axis=2, tiled=True),
        lax.all_gather(w_down, "dp", axis=1, tiled=True),
    )
    tok_count = tokens.shape[0]
    seq_count = tok_count // LENGTH
    expert_total = lax.axis_size("fsdp") * w_up.shape[0]
    capacity = 2 * F_TOP * tok_count // expert_total
    active_mask = depths >= STEP
    active = active_mask.astype(jnp.float32)
    act_col = active[:, None]
    vector_rows = whole_vectors.astype(jnp.float32)
    router_cols = whole_router.astype(jnp.float32)
    tok_float = tokens.astype(jnp.float32)
    first_hat, first_inv = norm_stats(tok_float)
    normed = (first_hat * vector_rows[0] + vector_rows[1]).astype(jnp.bfloat16)
    queries = jnp.dot(normed, whole_query, preferred_element_type=jnp.float32).astype(jnp.bfloat16)
    key_value = jnp.dot(normed, whole_kv, preferred_element_type=jnp.float32).astype(jnp.bfloat16)
    attn_pick = (
        attn_routes[:, :, None] == jnp.arange(A_EXP, dtype=jnp.int32)[None, None, :]
    ).astype(jnp.float32)
    attn_logits = jnp.dot(normed, whole_router[:, :A_EXP], preferred_element_type=jnp.float32)
    attn_gates = jax.nn.softmax(
        jnp.einsum("tke,te->tk", attn_pick, attn_logits, precision=PRECISE), axis=-1
    )
    slot_query = jnp.einsum(
        "tke,teh->tkh",
        attn_pick.astype(jnp.bfloat16),
        queries.reshape(tok_count, A_EXP, HEAD),
        preferred_element_type=jnp.float32,
    ).astype(jnp.bfloat16)
    seq_query = slot_query.reshape(seq_count, LENGTH, A_TOP, HEAD)
    seq_kv = key_value.reshape(seq_count, LENGTH, 2 * HEAD)
    slot_out, slot_log = lax.map(attend_sequence, (seq_query, seq_kv))
    slot_out = slot_out.reshape(tok_count, A_TOP, HEAD)
    mixed_heads = (
        jnp.einsum("tke,tkh->teh", attn_pick * attn_gates[:, :, None], slot_out, precision=PRECISE)
        .reshape(tok_count, A_EXP * HEAD)
        .astype(jnp.bfloat16)
    )
    attn_branch = jnp.dot(mixed_heads, whole_out, preferred_element_type=jnp.float32)
    hidden = tok_float + act_col * attn_branch
    second_hat, second_inv = norm_stats(hidden)
    normed_two = (second_hat * vector_rows[2] + vector_rows[3]).astype(jnp.bfloat16)
    ffn_pick = (
        ffn_routes[:, :, None] == jnp.arange(expert_total, dtype=jnp.int32)[None, None, :]
    ).astype(jnp.float32)
    ffn_logits = jnp.dot(normed_two, whole_router[:, A_EXP:], preferred_element_type=jnp.float32)
    ffn_gates = jax.nn.softmax(
        jnp.einsum("tke,te->tk", ffn_pick, ffn_logits, precision=PRECISE), axis=-1
    )
    slot_dest, slot_source = slot_table(ffn_routes, active_mask, tok_count, expert_total, capacity)
    padded_rows = jnp.concatenate([normed_two, jnp.zeros((1, D), jnp.bfloat16)], axis=0)
    slot_rows = padded_rows[slot_source].reshape(expert_total, capacity, D)
    owned_rows = lax.all_to_all(slot_rows, "fsdp", split_axis=0, concat_axis=1, tiled=True)
    owned_out = lax.map(expert_forward, (owned_rows, whole_up, whole_down))
    expert_out = lax.all_to_all(owned_out, "fsdp", split_axis=1, concat_axis=0, tiled=True)
    padded_out = jnp.concatenate(
        [
            expert_out.reshape(expert_total * capacity, D).astype(jnp.float32),
            jnp.zeros((1, D), jnp.float32),
        ],
        axis=0,
    )
    assigned = padded_out[slot_dest].reshape(tok_count, F_TOP, D)
    ffn_branch = jnp.sum(ffn_gates[:, :, None] * assigned, axis=1)
    block_out = hidden + act_col * ffn_branch
    halt_prob = jax.nn.sigmoid(jnp.dot(block_out, vector_rows[4], precision=PRECISE))
    halt_out = halt_in + active * (1.0 - halt_in) * halt_prob
    grad_out = cot_out.astype(jnp.float32)
    halt_slope = cot_halt * active * (1.0 - halt_in) * halt_prob * (1.0 - halt_prob)
    grad_block = grad_out + halt_slope[:, None] * vector_rows[4][None, :]
    grad_halt_row = jnp.dot(halt_slope, block_out, precision=PRECISE)
    grad_ffn = act_col * grad_block
    grad_gate_ffn = jnp.sum(grad_ffn[:, None, :] * assigned, axis=2)
    grad_assigned = ffn_gates[:, :, None] * grad_ffn[:, None, :]
    grad_expert = (
        jnp.zeros((expert_total * capacity + 1, D), jnp.float32)
        .at[slot_dest]
        .add(grad_assigned.reshape(tok_count * F_TOP, D))
    )
    grad_expert = (
        grad_expert[: expert_total * capacity]
        .reshape(expert_total, capacity, D)
        .astype(jnp.bfloat16)
    )
    owned_grad = lax.all_to_all(grad_expert, "fsdp", split_axis=0, concat_axis=1, tiled=True)
    grad_up, grad_down, grad_rows = lax.map(
        expert_back, (owned_rows, whole_up, whole_down, owned_grad)
    )
    part_up, part_down = (
        lax.psum_scatter(
            grad_up.astype(jnp.bfloat16), "dp", scatter_dimension=2, tiled=True
        ).astype(jnp.float32),
        lax.psum_scatter(
            grad_down.astype(jnp.bfloat16), "dp", scatter_dimension=1, tiled=True
        ).astype(jnp.float32),
    )
    rows_back = lax.all_to_all(
        grad_rows.astype(jnp.bfloat16), "fsdp", split_axis=1, concat_axis=0, tiled=True
    ).astype(grad_rows.dtype)
    grad_normed_two = (
        jnp.zeros((tok_count + 1, D), jnp.float32)
        .at[slot_source]
        .add(rows_back.reshape(expert_total * capacity, D))[:tok_count]
    )
    grad_ffn_logits = gate_back(ffn_gates, grad_gate_ffn, ffn_pick)
    grad_router_ffn = jnp.dot(
        normed_two.T, grad_ffn_logits, precision=PRECISE, preferred_element_type=jnp.float32
    )
    grad_normed_two = grad_normed_two + jnp.dot(
        grad_ffn_logits, router_cols[:, A_EXP:].T, precision=PRECISE
    )
    grad_gain_two = jnp.sum(grad_normed_two * second_hat, axis=0)
    grad_shift_two = jnp.sum(grad_normed_two, axis=0)
    grad_hidden = grad_block + norm_back(grad_normed_two, second_hat, second_inv, vector_rows[2])
    grad_attn = (act_col * grad_hidden).astype(jnp.bfloat16)
    grad_out_proj = jnp.dot(mixed_heads.T, grad_attn, preferred_element_type=jnp.float32)
    grad_mixed = jnp.dot(grad_attn, whole_out.T, preferred_element_type=jnp.float32).reshape(
        tok_count, A_EXP, HEAD
    )
    grad_slot = jnp.einsum("tke,teh->tkh", attn_pick, grad_mixed, precision=PRECISE)
    grad_gate_attn = jnp.sum(grad_slot * slot_out, axis=2)
    grad_slot_out = (attn_gates[:, :, None] * grad_slot).astype(jnp.bfloat16)
    grad_slots_q, grad_kv_seq = lax.map(
        attend_sequence_back,
        (seq_query, seq_kv, grad_slot_out.reshape(seq_count, LENGTH, A_TOP, HEAD), slot_log),
    )
    grad_queries = (
        jnp.einsum(
            "tke,tkh->teh",
            attn_pick,
            grad_slots_q.reshape(tok_count, A_TOP, HEAD),
            precision=PRECISE,
        )
        .reshape(tok_count, A_EXP * HEAD)
        .astype(jnp.bfloat16)
    )
    grad_kv = grad_kv_seq.reshape(tok_count, 2 * HEAD).astype(jnp.bfloat16)
    grad_query_w = jnp.dot(normed.T, grad_queries, preferred_element_type=jnp.float32)
    grad_kv_w = jnp.dot(normed.T, grad_kv, preferred_element_type=jnp.float32)
    grad_attn_logits = gate_back(attn_gates, grad_gate_attn, attn_pick)
    grad_router_attn = jnp.dot(
        normed.T, grad_attn_logits, precision=PRECISE, preferred_element_type=jnp.float32
    )
    grad_normed = jnp.dot(grad_queries, whole_query.T, preferred_element_type=jnp.float32)
    grad_normed = grad_normed + jnp.dot(grad_kv, whole_kv.T, preferred_element_type=jnp.float32)
    grad_normed = grad_normed + jnp.dot(
        grad_attn_logits, router_cols[:, :A_EXP].T, precision=PRECISE
    )
    grad_gain_one = jnp.sum(grad_normed * first_hat, axis=0)
    grad_shift_one = jnp.sum(grad_normed, axis=0)
    grad_input = grad_hidden + norm_back(grad_normed, first_hat, first_inv, vector_rows[0])
    grad_router = jnp.concatenate([grad_router_attn, grad_router_ffn], axis=1)
    grad_vectors = jnp.stack(
        [grad_gain_one, grad_shift_one, grad_gain_two, grad_shift_two, grad_halt_row]
    )
    outer_attn = (
        lax.psum_scatter(
            grad_query_w.astype(jnp.bfloat16), "dp", scatter_dimension=0, tiled=True
        ).astype(jnp.float32),
        lax.psum_scatter(
            grad_out_proj.astype(jnp.bfloat16), "dp", scatter_dimension=1, tiled=True
        ).astype(jnp.float32),
        lax.psum_scatter(
            grad_kv_w.astype(jnp.bfloat16), "dp", scatter_dimension=0, tiled=True
        ).astype(jnp.float32),
        lax.psum_scatter(
            grad_router.astype(jnp.bfloat16), "dp", scatter_dimension=0, tiled=True
        ).astype(jnp.float32),
        lax.psum_scatter(
            grad_vectors.astype(jnp.bfloat16), "dp", scatter_dimension=1, tiled=True
        ).astype(jnp.float32),
    )
    part_query, part_out, part_kv, part_router, part_vectors = (
        lax.psum_scatter(
            outer_attn[0].astype(jnp.bfloat16), "fsdp", scatter_dimension=0, tiled=True
        ).astype(jnp.float32),
        lax.psum_scatter(
            outer_attn[1].astype(jnp.bfloat16), "fsdp", scatter_dimension=1, tiled=True
        ).astype(jnp.float32),
        lax.psum_scatter(
            outer_attn[2].astype(jnp.bfloat16), "fsdp", scatter_dimension=0, tiled=True
        ).astype(jnp.float32),
        lax.psum_scatter(
            outer_attn[3].astype(jnp.bfloat16), "fsdp", scatter_dimension=0, tiled=True
        ).astype(jnp.float32),
        lax.psum_scatter(
            outer_attn[4].astype(jnp.bfloat16), "fsdp", scatter_dimension=1, tiled=True
        ).astype(jnp.float32),
    )
    return (
        block_out.astype(jnp.bfloat16),
        halt_out,
        grad_input.astype(jnp.bfloat16),
        part_query,
        part_out,
        part_kv,
        part_router,
        part_vectors,
        part_up,
        part_down,
    )


def solution(mesh):
    placed = (
        P(("dp", "fsdp"), None),
        P(("dp", "fsdp")),
        P(("dp", "fsdp")),
        P(("dp", "fsdp"), None),
        P(("dp", "fsdp"), None),
        P(("dp", "fsdp"), None),
        P(None, ("dp", "fsdp")),
        P(("dp", "fsdp"), None),
        P(("dp", "fsdp"), None),
        P(None, ("dp", "fsdp")),
        P("fsdp", None, "dp"),
        P("fsdp", "dp", None),
        P(("dp", "fsdp"), None),
        P(("dp", "fsdp")),
    )
    return jax.shard_map(
        on_device,
        mesh=mesh,
        in_specs=placed,
        out_specs=(
            P(("dp", "fsdp"), None),
            P(("dp", "fsdp")),
            P(("dp", "fsdp"), None),
            P(("dp", "fsdp"), None),
            P(None, ("dp", "fsdp")),
            P(("dp", "fsdp"), None),
            P(("dp", "fsdp"), None),
            P(None, ("dp", "fsdp")),
            P("fsdp", None, "dp"),
            P("fsdp", "dp", None),
        ),
        check_vma=False,
    )
```

profile of v0, /device:TPU:0, one launch (start us, length us, event | category | flops | bytes accessed | tf_op | source)
XLA Modules:
  0.0 1472.6 jit_solution(12062161259620058067)
XLA Ops:
  148.3 30.8 %while.30 = (s32[]{:T(128)}, f32[8,128,4,64]{1,3,2,0:T(8,128)S(1)}, f32[8,128,4]{1,2,0:T(4,128)}, s32[8]{0:T(128)S(1)}, bf16[8,128,4,64]{1,3,2,0:T(8,128)(2,1)S(...) while((s32[]{:T(128)}, f32[8,128,4,64]{1,3,2,0:T(8,128)S(1)}, ...), condition=%wide.region_7.8_spmd, body=%wide.region_4.7_spmd.sunk | while | flops 140639872 | bytes 7292025 | solution.py:86
  180.9 26.3 %convolution_convert_fusion.4 = bf16[1024,24,64]{2,1,0:T(8,128)(2,1)} fusion(f32[1024,4,64]{2,1,0:T(4,128)} %bitcast.267, f32[1024,4]{1,0:T(8,128)} %fusion.114, s32[1024,4]{1,0:T(8,128)S(1)} %copy.100), kind=kOutput, calls=%fused_computation.98 | convolution fusion | flops 77266944 | bytes 4227072 | tf_op jit(solution)/shard_map/tke,tkh->teh/dot_general | solution.py:231
  244.8 47.3 %all-gather.10.cloned.1.call-done = bf16[1,512,2048]{2,1,0:T(8,128)(2,1)} async-done(((bf16[1,512,512]{2,1,0:T(8,128)(2,1)}), bf16[1,512,2048]{2,1,0:T(8,128)(2,1)}) %all-gather.10.cloned.1.call-update) | async-done | bytes 2097168 | tf_op jit(solution)/shard_map/all_gather | solution.py:196
  292.6 93.2 %multiply_convert_fusion.1 = (bf16[4096,2048]{1,0:T(8,128)(2,1)}, f32[4096,2048]{1,0:T(8,128)}, f32[4096,2048]{1,0:T(8,128)}) fusion(bf16[4096,512]{1,0:T(8,128)(2,1)} %bitcast.27, bf16[1,512,2048]{2,1,0:T(8,128)(2,1)} %all-gather.10.cloned.1.call-done), kind=kOutput, calls=%fused_computation.66 | convolution fusion | flops 9135194112 | bytes 90177536 | tf_op jit(solution)/shard_map/while/body/eval_jaxpr/dot_general | solution.py:147
  398.9 36.5 %copy.160 = bf16[1,4096,512]{2,0,1:T(2,128)(2,1)} copy(bf16[1,4096,512]{2,1,0:T(8,128)(2,1)S(1)} %fusion.66) | data formatting | bytes 8388608 | tf_op jit(solution)/shard_map/while/body/jit(dynamic_update_index_in_dim)/broadcast_in_dim | solution.py:250
  435.9 28.5 %reduce.6 = bf16[4096,512]{1,0:T(8,128)(2,1)} reduce(bf16[4096,1,512]{2,1,0:T(2,128)(2,1)} %bitcast.247, bf16[]{:T(256)} %broadcast.618), dimensions={1}, to_apply=%bitcast.208.reduce_sub_computation | reduce | bytes 8388610
  485.1 41.5 %all-to-all-done.1 = bf16[8,2,131072]{2,1,0:T(2,128)(2,1)} async-done(((bf16[8,2,131072]{2,1,0:T(2,128)(2,1)}), bf16[8,2,131072]{2,1,0:T(2,128)(2,1)}, u32[]{:S(2)}, u32[]{:S(2)}) %all-to-all-start.1) | async-done | bytes 4194336 | tf_op jit(solution)/shard_map/all_to_all | solution.py:251
  608.6 52.3 %all_to_all.16 = bf16[8,512,512]{2,1,0:T(8,128)(2,1)} all-to-all(bf16[8,512,512]{2,1,0:T(8,128)(2,1)S(1)} %bitcast.255), channel_id=1, replica_groups=mesh['dp'=4,'fsdp'=8] {'fsdp'}, dimensions={0} | all-to-all | bytes 8388608 | tf_op jit(solution)/shard_map/all_to_all | solution.py:281
  660.9 33.9 %add_convert_fusion = bf16[4096,2048]{1,0:T(8,128)(2,1)} fusion(f32[4096,2048]{1,0:T(8,128)} %get-tuple-element.397, f32[4096,2048]{1,0:T(8,128)} %get-tuple-element.417, bf16[4096,512]{1,0:T(8,128)(2,1)} %bitcast.271, bf16[1,2048,512]{2,1,0:T(8,128)(2,1)} %all-gather.12.cloned.1.call-done), kind=kOutput, calls=%fused_computation.65 | convolution fusion | flops 8707375104 | bytes 90177536 | tf_op jit(solution)/shard_map/while/body/eval_jaxpr/dot_general | solution.py:158
  708.0 36.4 %copy.159 = bf16[1,4096,512]{2,0,1:T(2,128)(2,1)} copy(bf16[1,4096,512]{2,1,0:T(8,128)(2,1)S(1)} %fusion.67) | data formatting | bytes 8388608 | tf_op jit(solution)/shard_map/convert_element_type | solution.py:294
  744.4 28.9 %reduce.7 = bf16[4096,512]{1,0:T(8,128)(2,1)} reduce(bf16[4096,1,512]{2,1,0:T(2,128)(2,1)} %bitcast.248, bf16[]{:T(256)} %broadcast.618), dimensions={1}, to_apply=%bitcast.207.reduce_sub_computation | reduce | bytes 8388610
  803.1 31.7 %all-to-all-done.3 = bf16[8,2,131072]{2,1,0:T(2,128)(2,1)} async-done(((bf16[8,2,131072]{2,1,0:T(2,128)(2,1)}), bf16[8,2,131072]{2,1,0:T(2,128)(2,1)}, u32[]{:S(2)}, u32[]{:S(2)}) %all-to-all-start.3) | async-done | bytes 4194336 | tf_op jit(solution)/shard_map/all_to_all | solution.py:293
  843.6 31.2 %scatter_custom_fusion.2 = f32[1025,512]{1,0:T(8,128)} fusion(s32[4096]{0:T(1024)} %get-tuple-element.406, bf16[1,4096,512]{2,0,1:T(2,128)(2,1)} %bitcast.250, f32[]{:T(128)} %constant.277.clone.1), kind=kCustom, calls=%fused_computation.81 | custom fusion | flops 4194304 | bytes 10488320 | tf_op jit(solution)/shard_map/scatter-add | solution.py:299
  910.3 110.4 %while.37 = (s32[]{:T(128)}, f32[1024,64]{0,1:T(8,128)S(1)}, f32[1024,64]{0,1:T(8,128)S(1)}, f32[8,128,4,64]{1,3,2,0:T(8,128)}, s32[8]{0:T(128)S(1)}, /*index=5*...) while((s32[]{:T(128)}, f32[1024,64]{0,1:T(8,128)S(1)}, ...), condition=%wide.region_26.27_spmd.clone, body=%wide.region_24.26_spmd.clone.sunk | while | flops 343280768 | bytes 25173168 | solution.py:132
  1085.3 20.3 %reduce-scatter.41.cloned.1.call-done = bf16[128,32]{1,0:T(8,128)(2,1)} async-done(((bf16[512,32]{1,0:T(8,128)(2,1)}), bf16[128,32]{1,0:T(8,128)(2,1)}) %reduce-scatter.41.cloned.1.call-update) | async-done | bytes 8208
  1105.7 20.4 %reduce-scatter.29.cloned.1.call-done = bf16[128,128]{1,0:T(8,128)(2,1)} async-done(((bf16[512,128]{1,0:T(8,128)(2,1)}), bf16[128,128]{1,0:T(8,128)(2,1)}) %reduce-scatter.29.cloned.1.call-update) | async-done | bytes 32784 | tf_op jit(solution)/shard_map/reduce_scatter | solution.py:359
  1162.1 36.5 %reduce-scatter.25.cloned.1.call-done = bf16[128,1536]{1,0:T(8,128)(2,1)} async-done(((bf16[512,1536]{1,0:T(8,128)(2,1)}), bf16[128,1536]{1,0:T(8,128)(2,1)}) %reduce-scatter.25.cloned.1.call-update) | async-done | bytes 393232 | tf_op jit(solution)/shard_map/reduce_scatter | solution.py:353
  1201.7 30.0 %reduce-scatter.47.cloned.1.call-done = bf16[16,5]{1,0:T(8,128)(2,1)} async-done(((bf16[128,5]{1,0:T(8,128)(2,1)}), bf16[16,5]{1,0:T(8,128)(2,1)}) %reduce-scatter.47.cloned.1.call-update) | async-done | bytes 176
  1233.1 33.0 %reduce-scatter.43.cloned.1.call-done = bf16[16,32]{1,0:T(8,128)(2,1)} async-done(((bf16[128,32]{1,0:T(8,128)(2,1)}), bf16[16,32]{1,0:T(8,128)(2,1)}) %reduce-scatter.43.cloned.1.call-update) | async-done | bytes 1040
  1267.5 32.8 %reduce-scatter.31.cloned.1.call-done = bf16[16,128]{1,0:T(8,128)(2,1)} async-done(((bf16[128,128]{1,0:T(8,128)(2,1)}), bf16[16,128]{1,0:T(8,128)(2,1)}) %reduce-scatter.31.cloned.1.call-update) | async-done | bytes 4112 | tf_op jit(solution)/shard_map/reduce_scatter | solution.py:376
  1301.6 44.7 %reduce-scatter.35.cloned.1.call-done = bf16[1,512,512]{2,1,0:T(8,128)(2,1)} async-done(((bf16[1,2048,512]{2,1,0:T(8,128)(2,1)}), bf16[1,512,512]{2,1,0:T(8,128)(2,1)}) %reduce-scatter.35.cloned.1.call-update) | async-done | bytes 524304 | tf_op jit(solution)/shard_map/reduce_scatter | solution.py:289
  1348.4 42.9 %reduce-scatter.33.cloned.1.call-done = bf16[1,512,512]{2,1,0:T(8,128)(2,1)} async-done(((bf16[1,512,2048]{2,1,0:T(8,128)(2,1)}), bf16[1,512,512]{2,1,0:T(8,128)(2,1)}) %reduce-scatter.33.cloned.1.call-update) | async-done | bytes 524304 | tf_op jit(solution)/shard_map/reduce_scatter | solution.py:286
  1393.5 33.9 %reduce-scatter.39.cloned.1.call-done = bf16[16,1536]{1,0:T(8,128)(2,1)} async-done(((bf16[128,1536]{1,0:T(8,128)(2,1)}), bf16[16,1536]{1,0:T(8,128)(2,1)}) %reduce-scatter.39.cloned.1.call-update) | async-done | bytes 49168
  1429.2 35.0 %reduce-scatter.27.cloned.1.call-done = bf16[16,1536]{1,0:T(8,128)(2,1)} async-done(((bf16[128,1536]{1,0:T(8,128)(2,1)}), bf16[16,1536]{1,0:T(8,128)(2,1)}) %reduce-scatter.27.cloned.1.call-update) | async-done | bytes 49168 | tf_op jit(solution)/shard_map/reduce_scatter | solution.py:370
  (487 shorter events, 639.2 us)
Async XLA Ops:
  7.2 117.9 %all-gather.6.cloned.1.call-start = ((), (), s32[]{:S(2)}) async-start(), calls=%async_computation.16 | async-start | bytes 1966080 | tf_op jit(solution)/shard_map/all_gather | solution.py:189
  20.3 194.6 %all-gather.8.cloned.1.call-start = ((), (), s32[]{:S(2)}) async-start(), calls=%async_computation.17 | async-start | bytes 1966080 | tf_op jit(solution)/shard_map/all_gather | solution.py:190
  33.9 181.0 %copy-start.46 = (f32[1024]{0:T(1024)}, f32[1024]{0:T(1024)S(1)}, u32[]{:S(2)}) copy-start(f32[1024]{0:T(1024)S(1)} %get-tuple-element.398) | copy-start | bytes 12292
  55.3 164.5 %copy-start.62 = (f32[1,512]{1,0:T(1,128)}, f32[1,512]{1,0:T(1,128)S(1)}, u32[]{:S(2)}) copy-start(f32[1,512]{1,0:T(1,128)S(1)} %get-tuple-element.411) | copy-start | bytes 6148
  239.0 53.7 %all-to-all-start = ((bf16[8,512,512]{2,1,0:T(8,128)(2,1)}), bf16[8,512,512]{2,1,0:T(8,128)(2,1)}, u32[]{:S(2)}, u32[]{:S(2)}) async-start(bf16[8,512,512]{2,1,0:T(8,128)(2,1)} %bitcast.253), calls=%async_computation | async-start | bytes 8388608 | tf_op jit(solution)/shard_map/all_to_all | solution.py:249
  243.5 48.6 %all-gather.10.cloned.1.call-start = ((), (), s32[]{:S(2)}) async-start(), calls=%async_computation.18 | async-start | bytes 2621440 | tf_op jit(solution)/shard_map/all_gather | solution.py:196
  244.3 141.6 %all-gather.12.cloned.1.call-start = ((), (), s32[]{:S(2)}) async-start(), calls=%async_computation.19 | async-start | bytes 2621440 | tf_op jit(solution)/shard_map/all_gather | solution.py:197
  472.3 54.2 %all-to-all-start.1 = ((bf16[8,2,131072]{2,1,0:T(2,128)(2,1)}), bf16[8,2,131072]{2,1,0:T(2,128)(2,1)}, u32[]{:S(2)}, u32[]{:S(2)}) async-start(bf16[8,2,131072]{2,1,0:T(2,128)(2,1)} %reshape.411), calls=%async_computation.1 | async-start | bytes 8388608 | tf_op jit(solution)/shard_map/all_to_all | solution.py:251
  781.1 53.7 %all-to-all-start.3 = ((bf16[8,2,131072]{2,1,0:T(2,128)(2,1)}), bf16[8,2,131072]{2,1,0:T(2,128)(2,1)}, u32[]{:S(2)}, u32[]{:S(2)}) async-start(bf16[8,2,131072]{2,1,0:T(2,128)(2,1)} %reshape.413), calls=%async_computation.3 | async-start | bytes 8388608 | tf_op jit(solution)/shard_map/all_to_all | solution.py:293
  785.7 299.6 %reduce-scatter.45.cloned.1.call-start = ((), (), s32[]{:S(2)}) async-start(), calls=%async_computation.30 | async-start | bytes 163840
  910.2 110.5 %copy-start.15 = (f32[1024,1,4]{2,1,0:T(1,128)S(1)}, f32[1024,1,4]{2,1,0:T(1,128)}, u32[]{:S(2)}) copy-start(f32[1024,1,4]{2,1,0:T(1,128)} %copy-done.14) | copy-start | bytes 49156
  910.3 110.5 %copy-start.51 = (f32[1024]{0:T(1024)S(1)}, f32[1024]{0:T(1024)}, u32[]{:S(2)}) copy-start(f32[1024]{0:T(1024)} %copy-done.50) | copy-start | bytes 12292
  910.3 110.4 %copy-start.59 = (f32[1024]{0:T(1024)S(1)}, f32[1024]{0:T(1024)}, u32[]{:S(2)}) copy-start(f32[1024]{0:T(1024)} %copy-done.58) | copy-start | bytes 12292
  1066.4 39.2 %reduce-scatter.41.cloned.1.call-start = ((), (), s32[]{:S(2)}) async-start(), calls=%async_computation.28 | async-start | bytes 163840
  1068.0 58.1 %reduce-scatter.29.cloned.1.call-start = ((), (), s32[]{:S(2)}) async-start(), calls=%async_computation.22 | async-start | bytes 163840 | tf_op jit(solution)/shard_map/reduce_scatter | solution.py:359
  1070.5 91.6 %reduce-scatter.37.cloned.1.call-start = ((), (), s32[]{:S(2)}) async-start(), calls=%async_computation.26 | async-start | bytes 1966080
  1078.1 120.6 %reduce-scatter.25.cloned.1.call-start = ((), (), s32[]{:S(2)}) async-start(), calls=%async_computation.20 | async-start | bytes 1966080 | tf_op jit(solution)/shard_map/reduce_scatter | solution.py:353
  1083.7 148.0 %reduce-scatter.47.cloned.1.call-start = ((), (), s32[]{:S(2)}) async-start(), calls=%async_computation.31 | async-start | bytes 36864
  1085.3 180.8 %reduce-scatter.43.cloned.1.call-start = ((), (), s32[]{:S(2)}) async-start(), calls=%async_computation.29 | async-start | bytes 36864
  1105.6 194.7 %reduce-scatter.31.cloned.1.call-start = ((), (), s32[]{:S(2)}) async-start(), calls=%async_computation.23 | async-start | bytes 36864 | tf_op jit(solution)/shard_map/reduce_scatter | solution.py:376
  1126.1 220.2 %reduce-scatter.35.cloned.1.call-start = ((), (), s32[]{:S(2)}) async-start(), calls=%async_computation.25 | async-start | bytes 2621440 | tf_op jit(solution)/shard_map/reduce_scatter | solution.py:289
  1140.8 250.5 %reduce-scatter.33.cloned.1.call-start = ((), (), s32[]{:S(2)}) async-start(), calls=%async_computation.24 | async-start | bytes 2621440 | tf_op jit(solution)/shard_map/reduce_scatter | solution.py:286
  1155.6 271.8 %reduce-scatter.39.cloned.1.call-start = ((), (), s32[]{:S(2)}) async-start(), calls=%async_computation.27 | async-start | bytes 442368
  1162.1 302.1 %reduce-scatter.27.cloned.1.call-start = ((), (), s32[]{:S(2)}) async-start(), calls=%async_computation.21 | async-start | bytes 442368 | tf_op jit(solution)/shard_map/reduce_scatter | solution.py:370
  (79 other events, 1301.6 us)
Sparse Core Ops, SparseCore 0:
  20.4 37.4 all-gather.5
  59.4 39.7 all-gather.7
  245.9 46.1 all-gather.9
  293.6 44.4 all-gather.11
  1066.5 18.7 reduce-scatter.44
  1087.9 17.6 reduce-scatter.40
  1108.4 17.6 reduce-scatter.28
  1128.4 33.5 reduce-scatter.36
  1164.3 34.2 reduce-scatter.24
  1201.5 30.1 reduce-scatter.46
  1234.7 31.3 reduce-scatter.42
  1268.9 31.3 reduce-scatter.30
  1302.6 43.6 reduce-scatter.34
  1348.4 42.8 reduce-scatter.32
  1394.2 33.0 reduce-scatter.38
  1430.2 33.8 reduce-scatter.26
where the time goes:
time: 1480 us; the launch traced here: 1470 us
  waiting for transfers between devices  460 us (31%)
  matrix products  414 us (28%)
  local copies, waits for them, and re-layouts  252 us (17%)
  other arithmetic  173 us (12%)
  blocking collectives  142 us (10%)
  between operations  15.6 us (1%)
  starting transfers between devices  15.1 us (1%)
    unnamed x22, waiting for transfers between devices  127 us
    dot_general x1, matrix products, expert_forward(): jnp.dot(expert_rows, expert_up, preferred_element_type=jnp.float32)  93.2 us
    unnamed x5, other arithmetic  57.5 us
    unnamed x186, local copies, waits for them, and re-layouts  57.5 us
    all_to_all x1, blocking collectives, on_device(): lax.all_to_all(grad_expert, 'fsdp', split_axis=0, concat_axis=1, tiled=True)  52.3 us
    all_gather x1, waiting for transfers between devices, on_device(): lax.all_gather(w_up, 'dp', axis=2, tiled=True)  47.3 us
    reduce_scatter x1, waiting for transfers between devices, on_device(): lax.psum_scatter(grad_down.astype(jnp.bfloat16), 'dp', scatter_dimension=...  44.7 us
    reduce_scatter x1, waiting for transfers between devices, on_device(): lax.psum_scatter(grad_up.astype(jnp.bfloat16), 'dp', scatter_dimension=2,...  42.9 us
  transfers between devices with their start and end apart: 19, of which 16 were waited for; matrix products, arithmetic and copies ran while one was open for 20% of the time, Pallas kernels for 0%

commit v1 on v0

v1 whole, which is shorter than its diff:
```python
from functools import partial

import jax
import jax.numpy as jnp
from jax import lax
from jax.experimental import pallas as pl
from jax.experimental.pallas import tpu as pltpu
from jax.sharding import PartitionSpec as P

D = 512
HEAD = 64
A_EXP = 24
A_TOP = 4
F_TOP = 2
STEP = 2
LANES = 128
BLOCK = 256
PAIRS = A_EXP // 2
WIDTH = A_EXP * HEAD
KV_AT = 2 * WIDTH
RV_AT = KV_AT + LANES
PACK = RV_AT + LANES
EPSILON = 1e-05
NEG = -1e30
BF = jnp.bfloat16
F32 = jnp.float32

NN = (((1,), (0,)), ((), ()))
NT = (((1,), (1,)), ((), ()))
TN = (((0,), (0,)), ((), ()))

TAIL_P = 0.3
TAIL = (
    0.11962930113077164,
    0.1207539290189743,
    0.09991367161273956,
    0.12856101989746094,
    -0.053682513535022736,
    0.20635227859020233,
    -0.15720237791538239,
    0.03567460551857948,
)


def dot(a, b, dims=NN):
    return lax.dot_general(a, b, dims, preferred_element_type=F32)


def lane_ids(rows):
    return lax.broadcasted_iota(jnp.int32, (rows, LANES), 1)


def norm_stats(values):
    center = values - jnp.mean(values, axis=-1, keepdims=True)
    inv_std = lax.rsqrt(jnp.mean(center * center, axis=-1, keepdims=True) + EPSILON)
    return center * inv_std, inv_std


def norm_back(grad_normed, normal_part, inv_std, gain_row):
    grad_hat = grad_normed * gain_row
    mean_one = jnp.mean(grad_hat, axis=-1, keepdims=True)
    mean_two = jnp.mean(grad_hat * normal_part, axis=-1, keepdims=True)
    return inv_std * (grad_hat - mean_one - normal_part * mean_two)


def transposed_tail(w_ref):
    eye = (
        lax.broadcasted_iota(jnp.int32, (LANES, LANES), 0)
        == lax.broadcasted_iota(jnp.int32, (LANES, LANES), 1)
    )
    eye = jnp.where(eye, 1.0, 0.0).astype(BF)
    return dot(eye, w_ref[:, RV_AT:PACK], NT)


def vector_row(rows_t, first, index):
    return rows_t[first + index : first + index + 1, :]


def split_two(values):
    high = values.astype(BF)
    return high, (values - high.astype(F32)).astype(BF)


def slots_kernel(experts, capacity, meta_ref, cot_ref, rank_ref, rank_t_ref, slots_ref):
    tok = cot_ref.shape[0]
    tri = lax.broadcasted_iota(jnp.int32, (BLOCK, BLOCK), 0) >= lax.broadcasted_iota(
        jnp.int32, (BLOCK, BLOCK), 1
    )
    tri = jnp.where(tri, 1.0, 0.0).astype(BF)
    carry = jnp.zeros((1, LANES), F32)
    lane = lane_ids(BLOCK)
    for b in range(tok // BLOCK):
        rows = slice(b * BLOCK, (b + 1) * BLOCK)
        meta = meta_ref[rows, :]
        pick = ((lane == meta[:, 4:5]) | (lane == meta[:, 5:6])) & (meta[:, 6:7] >= STEP)
        ones = jnp.where(pick, 1.0, 0.0)
        count = dot(tri, ones.astype(BF)) + carry
        carry = count[BLOCK - 1 :, :]
        rank_ref[rows, :] = jnp.where(pick, count - 1.0, -1.0)
    rank_t_ref[...] = jnp.transpose(rank_ref[...]).astype(jnp.int32)

    def gather(e, _):
        slots_ref[e] = dot(one_hot(rank_t_ref, e, capacity), cot_ref[...]).astype(BF)
        return 0

    lax.fori_loop(0, experts, gather, 0)


def one_hot(rank_t_ref, e, capacity):
    row = rank_t_ref[pl.ds(e, 1), :]
    place = lax.broadcasted_iota(jnp.int32, (capacity, row.shape[1]), 0)
    return jnp.where(place == row, 1.0, 0.0).astype(BF)


def select_heads(values, route, lane_half):
    shifted = route - lane_half
    acc = jnp.zeros((values.shape[0], LANES), F32)
    for p in range(PAIRS):
        acc = jnp.where(shifted == 2 * p, values[:, p * LANES : (p + 1) * LANES], acc)
    return acc + pltpu.roll(acc, HEAD, 1)


def spread_heads(pairs, meta, lane, lane_half, store):
    doubled, shifted = [], []
    for k in range(A_TOP):
        half = (lane >= HEAD) if k % 2 else (lane < HEAD)
        part = jnp.where(half, pairs[k // 2], 0.0)
        doubled.append(part + pltpu.roll(part, HEAD, 1))
        shifted.append(meta[:, k : k + 1] - lane_half)
    for p in range(PAIRS):
        acc = jnp.zeros(doubled[0].shape, F32)
        for k in range(A_TOP):
            acc = jnp.where(shifted[k] == 2 * p, doubled[k], acc)
        store(p, acc.astype(BF))


def attend_kernel(
    experts,
    capacity,
    tok_ref,
    w_ref,
    meta_ref,
    rank_t_ref,
    slotq_ref,
    kv_ref,
    so_ref,
    lse_ref,
    gates_ref,
    mixed_ref,
    hidden_ref,
    fgate_ref,
    slots_ref,
    kx_ref,
    vx_ref,
    n2_ref,
):
    tok = tok_ref.shape[0]
    first = A_EXP + experts
    rows_t = transposed_tail(w_ref)
    gain_one, shift_one, gain_two, shift_two = (vector_row(rows_t, first, i) for i in range(4))
    lane = lane_ids(BLOCK)
    upper = lane >= HEAD
    lane_half = jnp.where(upper, 1, 0)

    def project(b, _):
        rows = pl.ds(b * BLOCK, BLOCK)
        meta = meta_ref[rows, :]
        hat, _inv = norm_stats(tok_ref[rows, :].astype(F32))
        normed = (hat * gain_one + shift_one).astype(BF)
        queries = dot(normed, w_ref[:, :WIDTH])
        kv = dot(normed, w_ref[:, KV_AT:RV_AT])
        logits = dot(normed, w_ref[:, RV_AT:PACK])
        kv_ref[rows, :] = kv.astype(BF)
        swapped = pltpu.roll(kv, HEAD, 1)
        kx_ref[0, rows, :] = jnp.where(upper, 0.0, kv).astype(BF)
        kx_ref[1, rows, :] = jnp.where(upper, swapped, 0.0).astype(BF)
        vx_ref[0, rows, :] = jnp.where(upper, 0.0, swapped).astype(BF)
        vx_ref[1, rows, :] = jnp.where(upper, kv, 0.0).astype(BF)
        picked = [select_heads(queries, meta[:, k : k + 1], lane_half) for k in range(A_TOP)]
        for j in range(A_TOP // 2):
            slotq_ref[j, rows, :] = jnp.where(upper, picked[2 * j + 1], picked[2 * j]).astype(BF)
        chosen = [
            jnp.sum(jnp.where(lane == meta[:, k : k + 1], logits, 0.0), axis=1, keepdims=True)
            for k in range(A_TOP)
        ]
        top = jnp.maximum(jnp.maximum(chosen[0], chosen[1]), jnp.maximum(chosen[2], chosen[3]))
        raised = [jnp.exp(c - top) for c in chosen]
        scale = 1.0 / (raised[0] + raised[1] + raised[2] + raised[3])
        gates = jnp.zeros((BLOCK, LANES), F32)
        for k in range(A_TOP):
            gates = jnp.where(lane == k, raised[k] * scale, gates)
        gates_ref[rows, :] = gates
        return 0

    lax.fori_loop(0, tok // BLOCK, project, 0)

    below = lax.broadcasted_iota(jnp.int32, (BLOCK, BLOCK), 1) <= lax.broadcasted_iota(
        jnp.int32, (BLOCK, BLOCK), 0
    )
    for i in range(tok // BLOCK):
        rows = slice(i * BLOCK, (i + 1) * BLOCK)
        seen = (i + 1) * BLOCK
        lse_ref[rows, :] = jnp.zeros((BLOCK, LANES), F32)

        def pair(j, _, rows=rows, seen=seen, i=i):
            out = jnp.zeros((BLOCK, LANES), F32)
            query = slotq_ref[j, rows, :]
            logs = lse_ref[rows, :]
            for h in range(2):
                scores = dot(query, kx_ref[h, :seen, :], NT) * (HEAD**-0.5)
                last = jnp.where(below, scores[:, i * BLOCK :], NEG)
                scores = last if i == 0 else jnp.concatenate([scores[:, : i * BLOCK], last], axis=1)
                top = jnp.max(scores, axis=1, keepdims=True)
                raised = jnp.exp(scores - top)
                total = jnp.sum(raised, axis=1, keepdims=True)
                probs = (raised * (1.0 / total)).astype(BF)
                out = out + dot(probs, vx_ref[h, :seen, :])
                logs = jnp.where(lane == 2 * j + h, top + jnp.log(total), logs)
            so_ref[j, rows, :] = out
            lse_ref[rows, :] = logs
            return 0

        lax.fori_loop(0, A_TOP // 2, pair, 0)

    def finish(b, _):
        rows = pl.ds(b * BLOCK, BLOCK)
        meta = meta_ref[rows, :]
        gates = gates_ref[rows, :]
        active = jnp.where(meta[:, 6:7] >= STEP, 1.0, 0.0)
        pairs = [
            so_ref[j, rows, :]
            * jnp.where(upper, gates[:, 2 * j + 1 : 2 * j + 2], gates[:, 2 * j : 2 * j + 1])
            for j in range(A_TOP // 2)
        ]

        def store(p, block):
            mixed_ref[rows, p * LANES : (p + 1) * LANES] = block

        spread_heads(pairs, meta, lane, lane_half, store)
        branch = dot(mixed_ref[rows, :], w_ref[:, WIDTH:KV_AT], NT)
        hidden = tok_ref[rows, :].astype(F32) + active * branch
        hidden_ref[rows, :] = hidden
        hat, _inv = norm_stats(hidden)
        normed = (hat * gain_two + shift_two).astype(BF)
        n2_ref[rows, :] = normed
        logits = pltpu.roll(dot(normed, w_ref[:, RV_AT:PACK]), LANES - A_EXP, 1)
        named = (lane == meta[:, 4:5]) | (lane == meta[:, 5:6])
        top = jnp.max(jnp.where(named, logits, NEG), axis=1, keepdims=True)
        raised = jnp.where(named, jnp.exp(jnp.where(named, logits, NEG) - top), 0.0)
        fgate_ref[rows, :] = raised * (1.0 / jnp.sum(raised, axis=1, keepdims=True))
        return 0

    lax.fori_loop(0, tok // BLOCK, finish, 0)

    def gather(e, _):
        slots_ref[e] = dot(one_hot(rank_t_ref, e, capacity), n2_ref[...]).astype(BF)
        return 0

    lax.fori_loop(0, experts, gather, 0)


def expert_kernel(parts, x_ref, up_ref, down_ref, out_ref, act_ref, slope_ref):
    width = up_ref.shape[2]
    rows = x_ref[...]

    def part(c, total):
        pre = dot(rows, up_ref[c])
        size = jnp.abs(pre)
        bell = jnp.exp(pre * pre * -0.5)
        inv = 1.0 / (1.0 + TAIL_P * size)
        tail = TAIL[-1] * inv
        for coef in TAIL[-2::-1]:
            tail = (tail + coef) * inv
        tail = tail * bell
        phi = jnp.where(pre >= 0.0, 1.0 - tail, tail)
        act = (pre * phi).astype(BF)
        act_ref[c] = act
        slope_ref[c] = (phi + pre * bell * 0.3989422804014327).astype(BF)
        return total + dot(act, down_ref[c])

    total = part(0, jnp.zeros(out_ref.shape, F32))
    for c in range(1, parts):
        total = part(c, total)
    out_ref[...] = total.astype(BF)


def combine_kernel(
    experts,
    capacity,
    back_ref,
    rank_ref,
    rank_t_ref,
    hidden_ref,
    w_ref,
    meta_ref,
    fgate_ref,
    scal_ref,
    cot_ref,
    out_ref,
    halt_ref,
    slope_ref,
    glf_ref,
    row_ref,
    ab_ref,
    cols_ref,
):
    tok = hidden_ref.shape[0]
    rows_t = transposed_tail(w_ref)
    halt_row = vector_row(rows_t, A_EXP + experts, 4)
    lane = lane_ids(BLOCK)
    row_ref[...] = jnp.zeros(row_ref.shape, F32)

    def block(b, _):
        rows = pl.ds(b * BLOCK, BLOCK)
        meta = meta_ref[rows, :]
        rank = rank_ref[rows, :].astype(jnp.int32)
        fgate = fgate_ref[rows, :]
        scal = scal_ref[rows, :]
        active = jnp.where(meta[:, 6:7] >= STEP, 1.0, 0.0)
        cot = cot_ref[rows, :].astype(F32)
        place = lax.broadcasted_iota(jnp.int32, (BLOCK, capacity), 1)
        branch = jnp.zeros((BLOCK, D), F32)
        with_cot = jnp.zeros((BLOCK, LANES), F32)
        with_row = jnp.zeros((BLOCK, LANES), F32)
        for e in range(experts):
            hot = jnp.where(place == rank[:, e : e + 1], 1.0, 0.0).astype(BF)
            came = dot(hot, back_ref[e])
            branch = branch + fgate[:, e : e + 1] * came
            with_cot = jnp.where(lane == e, jnp.sum(came * cot, axis=1, keepdims=True), with_cot)
            with_row = jnp.where(
                lane == e, jnp.sum(came * halt_row, axis=1, keepdims=True), with_row
            )
        z = hidden_ref[rows, :] + active * branch
        out_ref[rows, :] = z.astype(BF)
        prob = 1.0 / (1.0 + jnp.exp(-jnp.sum(z * halt_row, axis=1, keepdims=True)))
        halt_in, cot_halt = scal[:, 0:1], scal[:, 1:2]
        room = active * (1.0 - halt_in) * prob
        slope = cot_halt * room * (1.0 - prob)
        halt_ref[rows, :] = jnp.broadcast_to(halt_in + room, (BLOCK, LANES))
        slope_ref[rows, :] = jnp.broadcast_to(slope, (BLOCK, LANES))
        row_ref[0:1, :] += jnp.sum(slope * z, axis=0, keepdims=True)
        gfg = active * (with_cot + slope * with_row)
        inner = jnp.sum(fgate * gfg, axis=1, keepdims=True)
        glf_ref[rows, :] = pltpu.roll(fgate * (gfg - inner), A_EXP, 1)
        live = active * fgate
        bent = live * slope
        for index, part in enumerate((live, bent)):
            high = part.astype(BF)
            rest = part - high.astype(F32)
            middle = rest.astype(BF)
            cols_ref[3 * index, rows, :] = high
            cols_ref[3 * index + 1, rows, :] = middle
            cols_ref[3 * index + 2, rows, :] = (rest - middle.astype(F32)).astype(BF)
        return 0

    lax.fori_loop(0, tok // BLOCK, block, 0)
    turned = [jnp.transpose(cols_ref[i].astype(F32)) for i in range(6)]
    for e in range(experts):
        rows = jnp.concatenate(
            [t[e : e + 1, :] for t in turned] + [jnp.zeros((2, tok), F32)], axis=0
        )
        ab_ref[e] = dot(rows.astype(BF), one_hot(rank_t_ref, e, capacity), NT).astype(BF)


def data_back_kernel(
    experts, parts, cot_ref, ab_ref, tail_ref, slope_ref, up_ref, down_ref, gpre_ref, gy_ref, rows_ref
):
    rows = cot_ref.shape[0]
    eye = (
        lax.broadcasted_iota(jnp.int32, (LANES, LANES), 0)
        == lax.broadcasted_iota(jnp.int32, (LANES, LANES), 1)
    )
    rows_t = dot(jnp.where(eye, 1.0, 0.0).astype(BF), tail_ref[...], NT)
    halt_row = vector_row(rows_t, A_EXP + experts, 4)
    ab = ab_ref[0].astype(F32)
    live = ab[0:1, :] + ab[1:2, :] + ab[2:3, :]
    bent = ab[3:4, :] + ab[4:5, :] + ab[5:6, :]
    cols = jnp.transpose(jnp.concatenate([live, bent, jnp.zeros((LANES - 2, rows), F32)], axis=0))
    gy = (cols[:, 0:1] * cot_ref[...].astype(F32) + cols[:, 1:2] * halt_row).astype(BF)
    gy_ref[...] = gy
    total = jnp.zeros((rows, D), F32)
    for c in range(parts):
        gpre = (dot(gy, down_ref[c], NT) * slope_ref[c].astype(F32)).astype(BF)
        gpre_ref[c] = gpre
        total = total + dot(gpre, up_ref[c], NT)
    rows_ref[...] = total.astype(BF)


def weight_back_kernel(parts, x_ref, gy_ref, gpre_ref, act_ref, gup_ref, gdown_ref, up_acc, down_acc):
    step = pl.program_id(0)

    @pl.when(step == 0)
    def _():
        up_acc[...] = jnp.zeros(up_acc.shape, F32)
        down_acc[...] = jnp.zeros(down_acc.shape, F32)

    for c in range(parts):
        up_acc[c] += dot(x_ref[...], gpre_ref[c], TN)
        down_acc[c] += dot(gy_ref[...], act_ref[c], TN)

    @pl.when(step == pl.num_programs(0) - 1)
    def _():
        for c in range(parts):
            gup_ref[c] = up_acc[c].astype(BF)
            gdown_ref[c] = jnp.transpose(down_acc[c]).astype(BF)


def attend_back_kernel(
    experts,
    capacity,
    back_ref,
    rank_ref,
    hidden_ref,
    tok_ref,
    w_ref,
    meta_ref,
    cot_ref,
    slope_ref,
    glf_ref,
    row_ref,
    mixed_ref,
    so_ref,
    lse_ref,
    gates_ref,
    slotq_ref,
    kv_ref,
    gin_ref,
    pack_ref,
    gh_ref,
    n1_ref,
    gx_ref,
    gslot_ref,
    gla_ref,
    wide_ref,
    acc_ref,
    rv_ref,
    vec_ref,
    kx_ref,
    vx_ref,
    lset_ref,
    gq_ref,
):
    tok = hidden_ref.shape[0]
    blocks = tok // BLOCK
    first = A_EXP + experts
    rows_t = transposed_tail(w_ref)
    low_t = rows_t.astype(BF)
    gain_one, shift_one, gain_two, shift_two, halt_row = (
        vector_row(rows_t, first, i) for i in range(5)
    )
    lane = lane_ids(BLOCK)
    upper = lane >= HEAD
    lane_half = jnp.where(upper, 1, 0)
    vec_ref[...] = jnp.zeros(vec_ref.shape, F32)
    vec_ref[4:5, :] = row_ref[0:1, :]
    acc_ref[...] = jnp.zeros(acc_ref.shape, F32)
    rv_ref[...] = jnp.zeros(rv_ref.shape, F32)

    def hidden_back(b, _):
        rows = pl.ds(b * BLOCK, BLOCK)
        meta = meta_ref[rows, :]
        rank = rank_ref[rows, :].astype(jnp.int32)
        active = jnp.where(meta[:, 6:7] >= STEP, 1.0, 0.0)
        place = lax.broadcasted_iota(jnp.int32, (BLOCK, capacity), 1)
        glf_high, glf_low = split_two(glf_ref[rows, :])
        grad = dot(glf_high, low_t) + dot(glf_low, low_t)
        for e in range(experts):
            hot = jnp.where(place == rank[:, e : e + 1], 1.0, 0.0).astype(BF)
            grad = grad + dot(hot, back_ref[e])
        hat, inv = norm_stats(hidden_ref[rows, :])
        normed = (hat * gain_two + shift_two).astype(BF)
        rv_ref[...] += dot(normed, glf_high, TN) + dot(normed, glf_low, TN)
        vec_ref[2:3, :] += jnp.sum(grad * hat, axis=0, keepdims=True)
        vec_ref[3:4, :] += jnp.sum(grad, axis=0, keepdims=True)
        gz = cot_ref[rows, :].astype(F32) + slope_ref[rows, 0:1] * halt_row
        gh = gz + norm_back(grad, hat, inv, gain_two)
        gh_ref[rows, :] = gh
        ga = (active * gh).astype(BF)
        acc_ref[...] += dot(ga, mixed_ref[rows, :], TN)
        gm = dot(ga, w_ref[:, WIDTH:KV_AT])
        gates = gates_ref[rows, :]
        weighted = jnp.zeros((BLOCK, 1), F32)
        grads = []
        picked = [select_heads(gm, meta[:, k : k + 1], lane_half) for k in range(A_TOP)]
        for j in range(A_TOP // 2):
            both = jnp.where(upper, picked[2 * j + 1], picked[2 * j])
            prod = both * so_ref[j, rows, :]
            scale = jnp.where(upper, gates[:, 2 * j + 1 : 2 * j + 2], gates[:, 2 * j : 2 * j + 1])
            gslot_ref[j, rows, :] = (both * scale).astype(BF)
            grads.append(jnp.sum(jnp.where(upper, 0.0, prod), axis=1, keepdims=True))
            grads.append(jnp.sum(jnp.where(upper, prod, 0.0), axis=1, keepdims=True))
        for k in range(A_TOP):
            weighted = weighted + gates[:, k : k + 1] * grads[k]
        gla = jnp.zeros((BLOCK, LANES), F32)
        for k in range(A_TOP):
            value = gates[:, k : k + 1] * (grads[k] - weighted)
            gla = jnp.where(lane == meta[:, k : k + 1], value, gla)
        gla_ref[rows, :] = gla
        kv = kv_ref[rows, :].astype(F32)
        swapped = pltpu.roll(kv, HEAD, 1)
        kx_ref[0, rows, :] = jnp.where(upper, 0.0, kv).astype(BF)
        kx_ref[1, rows, :] = jnp.where(upper, swapped, 0.0).astype(BF)
        vx_ref[0, rows, :] = jnp.where(upper, 0.0, swapped).astype(BF)
        vx_ref[1, rows, :] = jnp.where(upper, kv, 0.0).astype(BF)
        return 0

    lax.fori_loop(0, blocks, hidden_back, 0)
    pack_ref[:, WIDTH:KV_AT] = acc_ref[...].astype(BF)
    lset_ref[...] = jnp.transpose(lse_ref[...])

    above = lax.broadcasted_iota(jnp.int32, (BLOCK, BLOCK), 0) <= lax.broadcasted_iota(
        jnp.int32, (BLOCK, BLOCK), 1
    )
    gx_ref[...] = jnp.zeros(gx_ref.shape, F32)
    for i in range(blocks):
        rows = slice(i * BLOCK, (i + 1) * BLOCK)
        seen = (i + 1) * BLOCK

        def pair(j, _, rows=rows, seen=seen, i=i):
            query = slotq_ref[j, rows, :]
            gslot = gslot_ref[j, rows, :]
            gq = jnp.zeros((BLOCK, LANES), F32)
            for h in range(2):
                keys = kx_ref[h, :seen, :]
                log = lset_ref[pl.ds(2 * j + h, 1), rows]
                scores = dot(keys, query, NT) * (HEAD**-0.5) - log
                last = jnp.where(above, scores[i * BLOCK :, :], NEG)
                scores = last if i == 0 else jnp.concatenate([scores[: i * BLOCK], last], axis=0)
                probs = jnp.exp(scores)
                gprob = dot(vx_ref[h, :seen, :], gslot, NT)
                inner = jnp.sum(probs * gprob, axis=0, keepdims=True)
                gs = (probs * (gprob - inner) * (HEAD**-0.5)).astype(BF)
                gq = gq + dot(gs, keys, TN)
                gx_ref[0, h, :seen, :] += dot(gs, query)
                gx_ref[1, h, :seen, :] += dot(probs.astype(BF), gslot)
            gq_ref[j, rows, :] = gq
            return 0

        lax.fori_loop(0, A_TOP // 2, pair, 0)

    acc_ref[...] = jnp.zeros(acc_ref.shape, F32)

    def input_back(b, gkv_sum):
        rows = pl.ds(b * BLOCK, BLOCK)
        meta = meta_ref[rows, :]
        pairs = [gq_ref[j, rows, :] for j in range(A_TOP // 2)]

        def store(p, block):
            wide_ref[:, p * LANES : (p + 1) * LANES] = block

        spread_heads(pairs, meta, lane, lane_half, store)
        gkeys = gx_ref[0, 0, rows, :] + pltpu.roll(gx_ref[0, 1, rows, :], HEAD, 1)
        gvals = pltpu.roll(gx_ref[1, 0, rows, :], HEAD, 1) + gx_ref[1, 1, rows, :]
        gkv = jnp.where(upper, gvals, gkeys).astype(BF)
        gla_high, gla_low = split_two(gla_ref[rows, :])
        grad = dot(wide_ref[...], w_ref[:, :WIDTH], NT)
        grad = grad + dot(gkv, w_ref[:, KV_AT:RV_AT], NT)
        grad = grad + dot(gla_high, low_t) + dot(gla_low, low_t)
        hat, inv = norm_stats(tok_ref[rows, :].astype(F32))
        normed = (hat * gain_one + shift_one).astype(BF)
        acc_ref[...] += dot(normed, wide_ref[...], TN)
        rv_ref[...] += dot(normed, gla_high, TN) + dot(normed, gla_low, TN)
        vec_ref[0:1, :] += jnp.sum(grad * hat, axis=0, keepdims=True)
        vec_ref[1:2, :] += jnp.sum(grad, axis=0, keepdims=True)
        gin_ref[rows, :] = (gh_ref[rows, :] + norm_back(grad, hat, inv, gain_one)).astype(BF)
        return gkv_sum + dot(normed, gkv, TN)

    gkv_sum = lax.fori_loop(0, blocks, input_back, jnp.zeros((D, LANES), F32))
    pack_ref[:, :WIDTH] = acc_ref[...].astype(BF)
    pack_ref[:, KV_AT:RV_AT] = gkv_sum.astype(BF)
    turned = jnp.transpose(vec_ref[...])
    turned = pltpu.roll(turned, first, 1)
    wide_lane = lane_ids(D)
    tail = jnp.where(wide_lane < first, rv_ref[...], turned)
    pack_ref[:, RV_AT:PACK] = tail.astype(BF)


VMEM_LIMIT = 60 * 1024 * 1024


def whole(shape, dtype):
    return jax.ShapeDtypeStruct(shape, dtype)


def in_vmem(count):
    return [pl.BlockSpec(memory_space=pltpu.VMEM)] * count


def call(kernel, name, inputs, outs, scratch=()):
    return pl.pallas_call(
        kernel,
        name=name,
        out_shape=outs,
        in_specs=in_vmem(len(inputs)),
        out_specs=in_vmem(len(outs)),
        scratch_shapes=list(scratch),
        compiler_params=pltpu.CompilerParams(vmem_limit_bytes=VMEM_LIMIT),
    )(*inputs)


def constant_spec(shape):
    return pl.BlockSpec(shape, lambda s: (0,) * len(shape), pipeline_mode=pl.Buffered(1))


def on_device(
    tokens,
    halt_in,
    depths,
    attn_routes,
    ffn_routes,
    w_query,
    w_out,
    w_kv,
    router,
    vectors,
    w_up,
    w_down,
    cot_out,
    cot_halt,
):
    tok = tokens.shape[0]
    groups, experts = lax.axis_size("dp"), lax.axis_size("fsdp")
    capacity = 2 * F_TOP * tok // experts
    slice_width = w_up.shape[2]
    shard = w_query.shape[0]
    slots = experts * capacity

    tail = jnp.concatenate([router, vectors.T], axis=1)
    tail = jnp.pad(tail, ((0, 0), (0, LANES - tail.shape[1])))
    pack = jnp.concatenate([w_query, w_out.T, w_kv, tail], axis=1)
    pack = lax.all_gather(pack, "dp", axis=0, tiled=False)
    pack = lax.all_gather(pack, "fsdp", axis=0, tiled=False)
    weights = pack.transpose(1, 0, 2, 3).reshape(D, PACK)
    whole_up = lax.all_gather(w_up[0], "dp", axis=0, tiled=False)
    whole_down = lax.all_gather(w_down[0], "dp", axis=0, tiled=False)

    meta = jnp.concatenate([attn_routes, ffn_routes, depths[:, None], depths[:, None]], axis=1)
    scal = jnp.stack([halt_in, cot_halt], axis=1)

    rank, rank_t, cot_slots = call(
        partial(slots_kernel, experts, capacity),
        "slots",
        (meta, cot_out),
        (
            whole((tok, LANES), F32),
            whole((LANES, tok), jnp.int32),
            whole((experts, capacity, D), BF),
        ),
    )

    slotq, kv, so, lse, gates, mixed, hidden, fgate, n2_slots = call(
        partial(attend_kernel, experts, capacity),
        "attend",
        (tokens, weights, meta, rank_t),
        (
            whole((2, tok, LANES), BF),
            whole((tok, LANES), BF),
            whole((2, tok, LANES), F32),
            whole((tok, LANES), F32),
            whole((tok, LANES), F32),
            whole((tok, WIDTH), BF),
            whole((tok, D), F32),
            whole((tok, LANES), F32),
            whole((experts, capacity, D), BF),
        ),
        (
            pltpu.VMEM((2, tok, LANES), BF),
            pltpu.VMEM((2, tok, LANES), BF),
            pltpu.VMEM((tok, D), BF),
        ),
    )

    def exchange(values):
        return lax.all_to_all(values, "fsdp", split_axis=0, concat_axis=0, tiled=True)

    owned_cot = exchange(cot_slots).reshape(slots, D)
    owned = exchange(n2_slots).reshape(slots, D)

    row_spec = pl.BlockSpec((capacity, D), lambda s: (s, 0))
    wide_spec = pl.BlockSpec((groups, capacity, slice_width), lambda s: (0, s, 0))
    up_spec = constant_spec((groups, D, slice_width))
    down_spec = constant_spec((groups, slice_width, D))
    params = pltpu.CompilerParams(vmem_limit_bytes=VMEM_LIMIT)
    wide = whole((groups, slots, slice_width), BF)
    owned_out, act, slope = pl.pallas_call(
        partial(expert_kernel, groups),
        name="expert",
        grid=(experts,),
        out_shape=(whole((slots, D), BF), wide, wide),
        in_specs=[row_spec, up_spec, down_spec],
        out_specs=[row_spec, wide_spec, wide_spec],
        compiler_params=params,
    )(owned, whole_up, whole_down)

    back = exchange(owned_out.reshape(experts, capacity, D))
    block_out, halt_wide, halt_slope, glf, halt_grad, ab = call(
        partial(combine_kernel, experts, capacity),
        "combine",
        (back, rank, rank_t, hidden, weights, meta, fgate, scal, cot_out),
        (
            whole((tok, D), BF),
            whole((tok, LANES), F32),
            whole((tok, LANES), F32),
            whole((tok, LANES), F32),
            whole((8, D), F32),
            whole((experts, 8, capacity), BF),
        ),
        (pltpu.VMEM((6, tok, LANES), BF),),
    )
    halt_out = halt_wide[:, 0]
    owned_ab = exchange(ab)

    gpre, gy, owned_rows = pl.pallas_call(
        partial(data_back_kernel, experts, groups),
        name="data_back",
        grid=(experts,),
        out_shape=(wide, whole((slots, D), BF), whole((slots, D), BF)),
        in_specs=[
            row_spec,
            pl.BlockSpec((1, 8, capacity), lambda s: (s, 0, 0)),
            pl.BlockSpec((D, LANES), lambda s: (0, RV_AT // LANES)),
            wide_spec,
            up_spec,
            down_spec,
        ],
        out_specs=[wide_spec, row_spec, row_spec],
        compiler_params=params,
    )(owned_cot, owned_ab, weights, slope, whole_up, whole_down)
    rows_back = exchange(owned_rows.reshape(experts, capacity, D))

    grad_up, grad_down = pl.pallas_call(
        partial(weight_back_kernel, groups),
        name="weight_back",
        grid=(experts,),
        out_shape=(whole((groups, D, slice_width), BF), whole((groups, slice_width, D), BF)),
        in_specs=[row_spec, row_spec, wide_spec, wide_spec],
        out_specs=[constant_spec((groups, D, slice_width)), constant_spec((groups, slice_width, D))],
        scratch_shapes=[
            pltpu.VMEM((groups, D, slice_width), F32),
            pltpu.VMEM((groups, D, slice_width), F32),
        ],
        compiler_params=params,
    )(owned, gy, gpre, act)
    part_up = lax.psum_scatter(grad_up, "dp", scatter_dimension=0, tiled=True).astype(F32)
    part_down = lax.psum_scatter(grad_down, "dp", scatter_dimension=0, tiled=True).astype(F32)

    grad_in, grads = call(
        partial(attend_back_kernel, experts, capacity),
        "attend_back",
        (
            rows_back,
            rank,
            hidden,
            tokens,
            weights,
            meta,
            cot_out,
            halt_slope,
            glf,
            halt_grad,
            mixed,
            so,
            lse,
            gates,
            slotq,
            kv,
        ),
        (whole((tok, D), BF), whole((D, PACK), BF)),
        (
            pltpu.VMEM((tok, D), F32),
            pltpu.VMEM((8, LANES), F32),
            pltpu.VMEM((2, 2, tok, LANES), F32),
            pltpu.VMEM((2, tok, LANES), BF),
            pltpu.VMEM((tok, LANES), F32),
            pltpu.VMEM((BLOCK, WIDTH), BF),
            pltpu.VMEM((D, WIDTH), F32),
            pltpu.VMEM((D, LANES), F32),
            pltpu.VMEM((LANES, D), F32),
            pltpu.VMEM((2, tok, LANES), BF),
            pltpu.VMEM((2, tok, LANES), BF),
            pltpu.VMEM((LANES, tok), F32),
            pltpu.VMEM((2, tok, LANES), F32),
        ),
    )

    sent = grads.reshape(groups, experts, shard, PACK).transpose(1, 0, 2, 3)
    came = exchange(sent)
    half = jnp.sum(came.astype(F32), axis=0).astype(BF)
    came = lax.all_to_all(half, "dp", split_axis=0, concat_axis=0, tiled=True)
    total = jnp.sum(came.astype(F32), axis=0)
    routers = A_EXP + experts
    return (
        block_out,
        halt_out,
        grad_in,
        total[:, :WIDTH],
        total[:, WIDTH:KV_AT].T,
        total[:, KV_AT:RV_AT],
        total[:, RV_AT : RV_AT + routers],
        total[:, RV_AT + routers : RV_AT + routers + 5].T,
        part_up,
        part_down,
    )


def solution(mesh):
    both = ("dp", "fsdp")
    placed = (
        P(both, None),
        P(both),
        P(both),
        P(both, None),
        P(both, None),
        P(both, None),
        P(None, both),
        P(both, None),
        P(both, None),
        P(None, both),
        P("fsdp", None, "dp"),
        P("fsdp", "dp", None),
        P(both, None),
        P(both),
    )
    return jax.shard_map(
        on_device,
        mesh=mesh,
        in_specs=placed,
        out_specs=(
            P(both, None),
            P(both),
            P(both, None),
            P(both, None),
            P(None, both),
            P(both, None),
            P(both, None),
            P(None, both),
            P("fsdp", None, "dp"),
            P("fsdp", "dp", None),
        ),
        check_vma=False,
    )
```

time: 1480 us -> 556 us (0.38)
  matrix products: 414 us -> 0 us
  waiting for transfers between devices: 460 us -> 149 us
  local copies, waits for them, and re-layouts: 252 us -> 13.5 us
  Pallas kernels: 0 us -> 211 us
  other arithmetic: 173 us -> 8.11 us
  blocking collectives: 142 us -> 122 us
    dot_general x87 -> x0, matrix products: 414 us -> none  [the longest x1 93.2 us: expert_forward(): jnp.dot(expert_rows, expert_up, preferred_element_type=jnp.float32)]
    reduce_scatter x6 -> x2, waiting for transfers between devices: 212 us -> 0.01 us  [the longest x1 0.01 us: on_device(): lax.psum_scatter(grad_down, 'dp', scatter_dimension=0, tiled=True)]
    pallas_call x0 -> x7, Pallas kernels: none -> 211 us  [the longest x4 107 us: call(): pl.pallas_call(kernel, name=name, out_shape=outs, in_specs=in_vmem(len(in...]
    unnamed x22 -> x5, waiting for transfers between devices: 127 us -> 1.17 us
    all_gather x8 -> x1, blocking collectives: 90.1 us -> 16.9 us  [on_device(): pack = lax.all_gather(pack, 'dp', axis=0, tiled=False)]
    unnamed x5 -> x0, other arithmetic: 57.5 us -> none
    unnamed x186 -> x5, local copies, waits for them, and re-layouts: 57.5 us -> 0.67 us
    convert_element_type x4 -> x0, local copies, waits for them, and re-layouts: 56.5 us -> none  [the longest x1 36.4 us: on_device(): grad_rows.astype(jnp.bfloat16)]
  transfers between devices with their start and end apart: 19 -> 9, of which waited for: 16 -> 6; matrix products, arithmetic and copies ran while one was open for 20% -> 3% of each run, Pallas kernels for 0% -> 20%
where the time goes in v1:
time: 556 us; the launch traced here: 545 us
  Pallas kernels  211 us (38%)
  waiting for transfers between devices  149 us (27%)
  blocking collectives  122 us (22%)
  starting transfers between devices  27.3 us (5%)
  between operations  14.1 us (3%)
  local copies, waits for them, and re-layouts  13.5 us (2%)
  other arithmetic  8.11 us (1%)
    pallas_call x4, Pallas kernels, call(): pl.pallas_call(kernel, name=name, out_shape=outs, in_specs=in_vmem(len(in...  107 us
    all_to_all x3, blocking collectives, exchange(): lax.all_to_all(values, 'fsdp', split_axis=0, concat_axis=0, tiled=True)  106 us
    all_to_all x3, waiting for transfers between devices, exchange(): lax.all_to_all(values, 'fsdp', split_axis=0, concat_axis=0, tiled=True)  67.1 us
    pallas_call x1, Pallas kernels, on_device(): pl.pallas_call(partial(expert_kernel, groups), name='expert', grid=(exper...  51.7 us
    all_gather x1, waiting for transfers between devices, on_device(): whole_down = lax.all_gather(w_down[0], 'dp', axis=0, tiled=False)  46.1 us
    pallas_call x1, Pallas kernels, on_device(): pl.pallas_call(partial(data_back_kernel, experts, groups), name='data_bac...  27.1 us
    pallas_call x1, Pallas kernels, on_device(): pl.pallas_call(partial(weight_back_kernel, groups), name='weight_back', g...  25.5 us
    all_gather x1, waiting for transfers between devices, on_device(): pack = lax.all_gather(pack, 'fsdp', axis=0, tiled=False)  23 us
  transfers between devices with their start and end apart: 9, of which 6 were waited for; matrix products, arithmetic and copies ran while one was open for 3% of the time, Pallas kernels for 20%

profile of v1, /device:TPU:0, one launch (start us, length us, event | category | flops | bytes accessed | tf_op | source)
XLA Modules:
  0.0 545.3 jit_solution(7694680642403144787)
XLA Ops:
  9.6 16.9 %all-gather = bf16[64,3328]{1,0:T(8,128)(2,1)} all-gather(bf16[16,3328]{1,0:T(8,128)(2,1)S(1)} %pad_maximum_fusion), channel_id=2, replica_groups=mesh['dp'=4,'fsdp'=8] {'dp'}, dimensions={0}, use_global_device_ids=true | all-gather | bytes 532480 | tf_op jit(solution)/shard_map/all_gather | solution.py:631
  29.1 10.0 %slots.1 = (f32[1024,128]{1,0:T(8,128)}, s32[128,1024]{1,0:T(8,128)}, bf16[8,512,512]{2,1,0:T(8,128)(2,1)}) custom-call(s32[1024,8]{1,0:T(8,128)} %copy.58.meta_ref, bf16[1024,512]{1,0:T(8,128)(2,1)} %cot_ref.5), custom_call_target="tpu_custom_call" | custom-call | tf_op jit(solution)/shard_map/slots/pallas_call | solution.py:590
  39.1 23.0 %all-gather.10.cloned.1.call-done = bf16[32,16,3328]{2,1,0:T(8,128)(2,1)} async-done(((bf16[4,16,3328]{2,1,0:T(8,128)(2,1)}), bf16[32,16,3328]{2,1,0:T(8,128)(2,1)}) %all-gather.10.cloned.1.call-update) | async-done | bytes 3407888 | tf_op jit(solution)/shard_map/all_gather | solution.py:632
  62.0 4.0 copy.56
  66.1 32.5 %attend.1 = (bf16[2,1024,128]{2,1,0:T(8,128)(2,1)}, bf16[1024,128]{1,0:T(8,128)(2,1)}, f32[2,1024,128]{2,1,0:T(8,128)}, f32[1024,128]{1,0:T(8,128)}, f32[1024,12...) custom-call(bf16[1024,512]{1,0:T(8,128)(2,1)} %tok_ref.3, ...), custom_call_target="tpu_custom_call" | custom-call | tf_op jit(solution)/shard_map/attend/pallas_call | solution.py:590
  98.6 4.5 all-to-all-start
  103.8 5.5 %all-gather.6.cloned.1.call-done.up_ref = bf16[4,512,512]{2,1,0:T(8,128)(2,1)} async-done(((bf16[1,512,512]{2,1,0:T(8,128)(2,1)}), bf16[4,512,512]{2,1,0:T(8,128)(2,1)}) %all-gather.6.cloned.1.call-update) | async-done | bytes 2097168 | tf_op jit(solution)/shard_map/all_gather | solution.py:634
  109.3 46.1 %all-gather.8.cloned.1.call-done.down_ref = bf16[4,512,512]{2,1,0:T(8,128)(2,1)} async-done(((bf16[1,512,512]{2,1,0:T(8,128)(2,1)}), bf16[4,512,512]{2,1,0:T(8,128)(2,1)}) %all-gather.8.cloned.1.call-update) | async-done | bytes 2097168 | tf_op jit(solution)/shard_map/all_gather | solution.py:635
  155.4 51.7 %expert.1 = (bf16[4096,512]{1,0:T(8,128)(2,1)}, bf16[4,4096,512]{2,1,0:T(8,128)(2,1)}, bf16[4,4096,512]{2,1,0:T(8,128)(2,1)}) custom-call(bf16[4096,512]{1,0:T(8,128)(2,1)} %bitcast.7.x_ref, bf16[4,512,512]{2,1,0:T(8,128)(2,1)} %all-gather.6.cloned.1.call-done.up_ref, bf16[4,512,512]{2,1,0:T(8,128)(2,1)} %all-gather.8.cloned.1.call-done.down_ref), custom_call_target="tpu_custom_call" | custom-call | tf_op jit(solution)/shard_map/expert/pallas_call | solution.py:685
  207.1 53.5 %all_to_all.35.back_ref = bf16[8,512,512]{2,1,0:T(8,128)(2,1)} all-to-all(bf16[8,512,512]{2,1,0:T(8,128)(2,1)} %bitcast.28), channel_id=1, replica_groups=mesh['dp'=4,'fsdp'=8] {'fsdp'}, dimensions={0} | all-to-all | bytes 8388608 | tf_op jit(solution)/shard_map/all_to_all | solution.py:674
  260.6 4.7 all-to-all-start.2
  266.4 20.3 %combine.1 = (bf16[1024,512]{1,0:T(8,128)(2,1)}, f32[1024,128]{1,0:T(8,128)}, f32[1024,128]{1,0:T(8,128)}, f32[1024,128]{1,0:T(8,128)}, f32[8,512]{1,0:T(8,128)}, /*index=5*/bf16[8,8,512]{2,1,0:T(8,128)(2,1)}) custom-call(bf16[8,512,512]{2,1,0:T(8,128)(2,1)} %all_to_all.35.back_ref, f32[1024,128]{1,0:T(8,128)} %get-tuple-element.41.rank_ref, ...), custom_call_target="tpu_custom_call" | custom-call | tf_op jit(solution)/shard_map/combine/pallas_call | solution.py:590
  286.7 27.6 %all-to-all-done.2 = bf16[8,512,512]{2,1,0:T(8,128)(2,1)} async-done(((bf16[8,512,512]{2,1,0:T(8,128)(2,1)}), bf16[8,512,512]{2,1,0:T(8,128)(2,1)}, u32[]{:S(2)}, u32[]{:S(2)}) %all-to-all-start.2) | async-done | bytes 4194336 | tf_op jit(solution)/shard_map/all_to_all | solution.py:674
  314.4 9.0 %all_to_all.36.ab_ref = bf16[8,8,512]{2,1,0:T(8,128)(2,1)} all-to-all(bf16[8,8,512]{2,1,0:T(8,128)(2,1)} %get-tuple-element.47), channel_id=1, replica_groups=mesh['dp'=4,'fsdp'=8] {'fsdp'}, dimensions={0} | all-to-all | bytes 131072 | tf_op jit(solution)/shard_map/all_to_all | solution.py:674
  323.3 27.1 %data_back.1 = (bf16[4,4096,512]{2,1,0:T(8,128)(2,1)}, bf16[4096,512]{1,0:T(8,128)(2,1)}, bf16[4096,512]{1,0:T(8,128)(2,1)}) custom-call(bf16[4096,512]{1,0:T(8,128)(2,1)} %bitcast.11.cot_ref, bf16[8,8,512]{2,1,0:T(8,128)(2,1)} %all_to_all.36.ab_ref, bf16[512,3328]{1,0:T(8,128)(2,1)} %bitcast.24, bf16[4,4096,512]{2,1,0:T(8,128)(2,1)} %get-tuple-element.48.slope_ref, ...), custom_call_target="tpu_custom_call" | custom-call | tf_op jit(solution)/shard_map/data_back/pallas_call | solution.py:713
  350.4 25.5 %weight_back.1 = (bf16[4,512,512]{2,1,0:T(8,128)(2,1)}, bf16[4,512,512]{2,1,0:T(8,128)(2,1)}) custom-call(bf16[4096,512]{1,0:T(8,128)(2,1)} %bitcast.7.x_ref, bf16[4096,512]{1,0:T(8,128)(2,1)} %get-tuple-element.61.gy_ref, bf16[4,4096,512]{2,1,0:T(8,128)(2,1)} %get-tuple-element.62.gpre_ref, bf16[4,4096,512]{2,1,0:T(8,128)(2,1)} %get-tuple-element.63.act_ref), custom_call_target="tpu_custom_call" | custom-call | tf_op jit(solution)/shard_map/weight_back/pallas_call | solution.py:731
  375.9 4.6 all-to-all-start.4
  380.5 9.6 %reduce-scatter.3.cloned.1.call-start = ((), (), s32[]{:S(2)}) async-start(), calls=%async_computation.11 | async-start | bytes 2621440 | tf_op jit(solution)/shard_map/reduce_scatter | solution.py:744
  390.1 39.5 %all-to-all-done.4.back_ref = bf16[8,512,512]{2,1,0:T(8,128)(2,1)} async-done(((bf16[8,512,512]{2,1,0:T(8,128)(2,1)}), bf16[8,512,512]{2,1,0:T(8,128)(2,1)}, u32[]{:S(2)}, u32[]{:S(2)}) %all-to-all-start.4) | async-done | bytes 4194336 | tf_op jit(solution)/shard_map/all_to_all | solution.py:674
  429.6 44.1 %attend_back.1 = (bf16[1024,512]{1,0:T(8,128)(2,1)}, bf16[512,3328]{1,0:T(8,128)(2,1)}) custom-call(bf16[8,512,512]{2,1,0:T(8,128)(2,1)} %all-to-all-done.4.back_ref, f32[1024,128]{1,0:T(8,128)} %get-tuple-element.41.rank_ref, f32[1024,512]{1,0:T(8,128)} %get-tuple-element.42.hidden_ref, bf16[1024,512]{1,0:T(8,128)(2,1)} %tok_ref.3, ...), custom_call_target="tpu_custom_call" | custom-call | tf_op jit(solution)/shard_map/attend_back/pallas_call | solution.py:590
  473.7 2.2 copy.65
  475.9 43.1 %all_to_all.37 = bf16[8,4,16,3328]{3,2,1,0:T(8,128)(2,1)S(1)} all-to-all(bf16[8,4,16,3328]{3,2,1,0:T(8,128)(2,1)S(1)} %bitcast.26), channel_id=1, replica_groups=mesh['dp'=4,'fsdp'=8] {'fsdp'}, dimensions={0} | all-to-all | bytes 6815744 | tf_op jit(solution)/shard_map/all_to_all | solution.py:674
  520.4 3.5 all-to-all-start.6
  530.0 5.9 %all-to-all-done.6 = bf16[4,16,3328]{2,1,0:T(8,128)(2,1)S(1)} async-done(((bf16[4,16,3328]{2,1,0:T(8,128)(2,1)}), bf16[4,16,3328]{2,1,0:T(8,128)(2,1)S(1)}, u32[]{:S(2)}, u32[]{:S(2)}) %all-to-all-start.6) | async-done | bytes 426016 | tf_op jit(solution)/shard_map/all_to_all | solution.py:789
  (33 shorter events, 17.0 us)
Async XLA Ops:
  7.2 54.9 %all-gather.10.cloned.1.call-start = ((), (), s32[]{:S(2)}) async-start(), calls=%async_computation.13 | async-start | bytes 3833856 | tf_op jit(solution)/shard_map/all_gather | solution.py:632
  26.6 82.7 %all-gather.6.cloned.1.call-start = ((), (), s32[]{:S(2)}) async-start(), calls=%async_computation.9 | async-start | bytes 2621440 | tf_op jit(solution)/shard_map/all_gather | solution.py:634
  98.6 56.8 %all-to-all-start = ((bf16[8,512,512]{2,1,0:T(8,128)(2,1)}), bf16[8,512,512]{2,1,0:T(8,128)(2,1)}, u32[]{:S(2)}, u32[]{:S(2)}) async-start(bf16[8,512,512]{2,1,0:T(8,128)(2,1)} %get-tuple-element.39), calls=%async_computation | async-start | bytes 8388608 | tf_op jit(solution)/shard_map/all_to_all | solution.py:674
  103.1 52.3 %all-gather.8.cloned.1.call-start = ((), (), s32[]{:S(2)}) async-start(), calls=%async_computation.10 | async-start | bytes 2621440 | tf_op jit(solution)/shard_map/all_gather | solution.py:635
  260.6 4.7 copy-start
  260.6 4.7 copy-start.1
  260.6 53.8 %all-to-all-start.2 = ((bf16[8,512,512]{2,1,0:T(8,128)(2,1)}), bf16[8,512,512]{2,1,0:T(8,128)(2,1)}, u32[]{:S(2)}, u32[]{:S(2)}) async-start(bf16[8,512,512]{2,1,0:T(8,128)(2,1)} %get-tuple-element.46), calls=%async_computation.2 | async-start | bytes 8388608 | tf_op jit(solution)/shard_map/all_to_all | solution.py:674
  265.3 260.4 %reduce-scatter.5.cloned.1.call-start = ((), (), s32[]{:S(2)}) async-start(), calls=%async_computation.12 | async-start | bytes 2621440 | tf_op jit(solution)/shard_map/reduce_scatter | solution.py:745
  375.9 53.7 %all-to-all-start.4 = ((bf16[8,512,512]{2,1,0:T(8,128)(2,1)}), bf16[8,512,512]{2,1,0:T(8,128)(2,1)}, u32[]{:S(2)}, u32[]{:S(2)}) async-start(bf16[8,512,512]{2,1,0:T(8,128)(2,1)} %bitcast.27), calls=%async_computation.4 | async-start | bytes 8388608 | tf_op jit(solution)/shard_map/all_to_all | solution.py:674
  380.5 147.3 %reduce-scatter.3.cloned.1.call-start = ((), (), s32[]{:S(2)}) async-start(), calls=%async_computation.11 | async-start | bytes 2621440 | tf_op jit(solution)/shard_map/reduce_scatter | solution.py:744
  520.4 15.5 %all-to-all-start.6 = ((bf16[4,16,3328]{2,1,0:T(8,128)(2,1)}), bf16[4,16,3328]{2,1,0:T(8,128)(2,1)S(1)}, u32[]{:S(2)}, u32[]{:S(2)}) async-start(bf16[4,16,3328]{2,1,0:T(8,128)(2,1)} %reduce_sum.21), calls=%async_computation.6 | async-start | bytes 851968 | tf_op jit(solution)/shard_map/all_to_all | solution.py:789
Sparse Core Ops, SparseCore 0:
  26.7 35.3 all-gather.9
  63.6 45.6 all-gather.5
  110.9 44.4 all-gather.7
  376.1 40.7 reduce-scatter.4
  419.0 42.8 reduce-scatter.2

commit v2 on v1

--- a/solution.py
+++ b/solution.py
@@ -6,6 +6,7 @@
 from jax.experimental import pallas as pl
 from jax.experimental.pallas import tpu as pltpu
 from jax.sharding import PartitionSpec as P
+
 
 D = 512
 HEAD = 64
@@ -15,6 +16,7 @@
 STEP = 2
 LANES = 128
 BLOCK = 256
+HALVES = 2
 PAIRS = A_EXP // 2
 WIDTH = A_EXP * HEAD
 KV_AT = 2 * WIDTH
@@ -64,12 +66,16 @@
 
 
 def transposed_tail(w_ref):
+    return turned_tail(w_ref[:, RV_AT:PACK])
+
+
+def turned_tail(tail):
     eye = (
         lax.broadcasted_iota(jnp.int32, (LANES, LANES), 0)
         == lax.broadcasted_iota(jnp.int32, (LANES, LANES), 1)
     )
     eye = jnp.where(eye, 1.0, 0.0).astype(BF)
-    return dot(eye, w_ref[:, RV_AT:PACK], NT)
+    return dot(eye, tail, NT)
 
 
 def vector_row(rows_t, first, index):
@@ -81,7 +87,7 @@
     return high, (values - high.astype(F32)).astype(BF)
 
 
-def slots_kernel(experts, capacity, meta_ref, cot_ref, rank_ref, rank_t_ref, slots_ref):
+def slots_kernel(experts, capacity, meta_ref, cot_ref, rank_ref, rank_t_ref, *slots_refs):
     tok = cot_ref.shape[0]
     tri = lax.broadcasted_iota(jnp.int32, (BLOCK, BLOCK), 0) >= lax.broadcasted_iota(
         jnp.int32, (BLOCK, BLOCK), 1
@@ -99,16 +105,23 @@
         rank_ref[rows, :] = jnp.where(pick, count - 1.0, -1.0)
     rank_t_ref[...] = jnp.transpose(rank_ref[...]).astype(jnp.int32)
 
+    gather_slots(experts, capacity, rank_t_ref, cot_ref, slots_refs)
+
+
+def gather_slots(experts, capacity, rank_t_ref, rows_ref, slots_refs):
     def gather(e, _):
-        slots_ref[e] = dot(one_hot(rank_t_ref, e, capacity), cot_ref[...]).astype(BF)
+        for h in range(HALVES):
+            hot = one_hot(rank_t_ref, e, capacity, h)
+            slots_refs[h][e] = dot(hot, rows_ref[...]).astype(BF)
         return 0
 
     lax.fori_loop(0, experts, gather, 0)
 
 
-def one_hot(rank_t_ref, e, capacity):
-    row = rank_t_ref[pl.ds(e, 1), :]
-    place = lax.broadcasted_iota(jnp.int32, (capacity, row.shape[1]), 0)
+def one_hot(rank_t_ref, e, capacity, h):
+    size = capacity // HALVES
+    row = rank_t_ref[pl.ds(e, 1), :] - h * size
+    place = lax.broadcasted_iota(jnp.int32, (size, row.shape[1]), 0)
     return jnp.where(place == row, 1.0, 0.0).astype(BF)
 
 
@@ -134,26 +147,32 @@
         store(p, acc.astype(BF))
 
 
-def attend_kernel(
-    experts,
-    capacity,
-    tok_ref,
-    w_ref,
-    meta_ref,
-    rank_t_ref,
-    slotq_ref,
-    kv_ref,
-    so_ref,
-    lse_ref,
-    gates_ref,
-    mixed_ref,
-    hidden_ref,
-    fgate_ref,
-    slots_ref,
-    kx_ref,
-    vx_ref,
-    n2_ref,
-):
+def place_pieces(shape, pieces, w_ref):
+    groups, experts, shard = shape
+    if len(pieces) == 1:
+        w_ref[...] = pieces[0][...]
+        return
+    mine, group = lax.axis_index("fsdp"), lax.axis_index("dp")
+    for m in range(experts):
+        base = jnp.bitwise_xor(mine, m) * shard
+        for g in range(groups):
+            owner = lax.rem(group + g, groups)
+            if m < 6:
+                block = pieces[m][g]
+            else:
+                low, high = pieces[6 + 2 * (m - 6)], pieces[7 + 2 * (m - 6)]
+                block = low[g] if g < groups // 2 else high[g - groups // 2]
+            rows = pl.ds(pl.multiple_of(owner * experts * shard + base, shard), shard)
+            w_ref[rows, :] = block
+
+
+def attend_kernel(experts, capacity, shape, *refs):
+    tok_ref, meta_ref, rank_t_ref = refs[:3]
+    slots_refs, refs = refs[-3 - HALVES : -3], refs[3 : -3 - HALVES] + refs[-3:]
+    pieces, refs = refs[:-12], refs[-12:]
+    w_ref, slotq_ref, kv_ref, so_ref, lse_ref, gates_ref, mixed_ref, hidden_ref, fgate_ref = refs[:9]
+    kx_ref, vx_ref, n2_ref = refs[9:]
+    place_pieces(shape, pieces, w_ref)
     tok = tok_ref.shape[0]
     first = A_EXP + experts
     rows_t = transposed_tail(w_ref)
@@ -165,7 +184,7 @@
     def project(b, _):
         rows = pl.ds(b * BLOCK, BLOCK)
         meta = meta_ref[rows, :]
-        hat, _inv = norm_stats(tok_ref[rows, :].astype(F32))
+        hat, _ = norm_stats(tok_ref[rows, :].astype(F32))
         normed = (hat * gain_one + shift_one).astype(BF)
         queries = dot(normed, w_ref[:, :WIDTH])
         kv = dot(normed, w_ref[:, KV_AT:RV_AT])
@@ -240,7 +259,7 @@
         branch = dot(mixed_ref[rows, :], w_ref[:, WIDTH:KV_AT], NT)
         hidden = tok_ref[rows, :].astype(F32) + active * branch
         hidden_ref[rows, :] = hidden
-        hat, _inv = norm_stats(hidden)
+        hat, _ = norm_stats(hidden)
         normed = (hat * gain_two + shift_two).astype(BF)
         n2_ref[rows, :] = normed
         logits = pltpu.roll(dot(normed, w_ref[:, RV_AT:PACK]), LANES - A_EXP, 1)
@@ -251,16 +270,10 @@
         return 0
 
     lax.fori_loop(0, tok // BLOCK, finish, 0)
-
-    def gather(e, _):
-        slots_ref[e] = dot(one_hot(rank_t_ref, e, capacity), n2_ref[...]).astype(BF)
-        return 0
-
-    lax.fori_loop(0, experts, gather, 0)
+    gather_slots(experts, capacity, rank_t_ref, n2_ref, slots_refs)
 
 
 def expert_kernel(parts, x_ref, up_ref, down_ref, out_ref, act_ref, slope_ref):
-    width = up_ref.shape[2]
     rows = x_ref[...]
 
     def part(c, total):
@@ -284,14 +297,53 @@
     out_ref[...] = total.astype(BF)
 
 
+def combine_sums(experts, capacity, h, rank, back_ref, fgate, cot, halt_row, lane, sums):
+    branch, with_cot, with_row = sums
+    size = capacity // HALVES
+    place = lax.broadcasted_iota(jnp.int32, (BLOCK, size), 1) + h * size
+    for e in range(experts):
+        hot = jnp.where(place == rank[:, e : e + 1], 1.0, 0.0).astype(BF)
+        came = dot(hot, back_ref[e])
+        branch = branch + fgate[:, e : e + 1] * came
+        one = jnp.sum(came * cot, axis=1, keepdims=True)
+        two = jnp.sum(came * halt_row, axis=1, keepdims=True)
+        with_cot = with_cot + jnp.where(lane == e, one, 0.0)
+        with_row = with_row + jnp.where(lane == e, two, 0.0)
+    return branch, with_cot, with_row
+
+
+def combine_first_kernel(
+    experts, capacity, back_ref, rank_ref, tail_ref, fgate_ref, cot_ref, branch_ref, wcot_ref, wrow_ref
+):
+    halt_row = vector_row(turned_tail(tail_ref[...]), A_EXP + experts, 4)
+    lane = lane_ids(BLOCK)
+
+    def block(b, _):
+        rows = pl.ds(b * BLOCK, BLOCK)
+        rank = rank_ref[rows, :].astype(jnp.int32)
+        cot = cot_ref[rows, :].astype(F32)
+        zero = jnp.zeros((BLOCK, LANES), F32)
+        sums = (jnp.zeros((BLOCK, D), F32), zero, zero)
+        sums = combine_sums(
+            experts, capacity, 0, rank, back_ref, fgate_ref[rows, :], cot, halt_row, lane, sums
+        )
+        branch_ref[rows, :], wcot_ref[rows, :], wrow_ref[rows, :] = sums
+        return 0
+
+    lax.fori_loop(0, branch_ref.shape[0] // BLOCK, block, 0)
+
+
 def combine_kernel(
     experts,
     capacity,
     back_ref,
+    branch_ref,
+    wcot_ref,
+    wrow_ref,
     rank_ref,
     rank_t_ref,
     hidden_ref,
-    w_ref,
+    tail_ref,
     meta_ref,
     fgate_ref,
     scal_ref,
@@ -301,12 +353,11 @@
     slope_ref,
     glf_ref,
     row_ref,
-    ab_ref,
-    cols_ref,
+    *rest,
 ):
+    ab_refs, cols_ref = rest[:HALVES], rest[HALVES]
     tok = hidden_ref.shape[0]
-    rows_t = transposed_tail(w_ref)
-    halt_row = vector_row(rows_t, A_EXP + experts, 4)
+    halt_row = vector_row(turned_tail(tail_ref[...]), A_EXP + experts, 4)
     lane = lane_ids(BLOCK)
     row_ref[...] = jnp.zeros(row_ref.shape, F32)
 
@@ -318,18 +369,10 @@
         scal = scal_ref[rows, :]
         active = jnp.where(meta[:, 6:7] >= STEP, 1.0, 0.0)
         cot = cot_ref[rows, :].astype(F32)
-        place = lax.broadcasted_iota(jnp.int32, (BLOCK, capacity), 1)
-        branch = jnp.zeros((BLOCK, D), F32)
-        with_cot = jnp.zeros((BLOCK, LANES), F32)
-        with_row = jnp.zeros((BLOCK, LANES), F32)
-        for e in range(experts):
-            hot = jnp.where(place == rank[:, e : e + 1], 1.0, 0.0).astype(BF)
-            came = dot(hot, back_ref[e])
-            branch = branch + fgate[:, e : e + 1] * came
-            with_cot = jnp.where(lane == e, jnp.sum(came * cot, axis=1, keepdims=True), with_cot)
-            with_row = jnp.where(
-                lane == e, jnp.sum(came * halt_row, axis=1, keepdims=True), with_row
-            )
+        sums = (branch_ref[rows, :], wcot_ref[rows, :], wrow_ref[rows, :])
+        branch, with_cot, with_row = combine_sums(
+            experts, capacity, 1, rank, back_ref, fgate, cot, halt_row, lane, sums
+        )
         z = hidden_ref[rows, :] + active * branch
         out_ref[rows, :] = z.astype(BF)
         prob = 1.0 / (1.0 + jnp.exp(-jnp.sum(z * halt_row, axis=1, keepdims=True)))
@@ -358,24 +401,24 @@
     for e in range(experts):
         rows = jnp.concatenate(
             [t[e : e + 1, :] for t in turned] + [jnp.zeros((2, tok), F32)], axis=0
-        )
-        ab_ref[e] = dot(rows.astype(BF), one_hot(rank_t_ref, e, capacity), NT).astype(BF)
+        ).astype(BF)
+        for h in range(HALVES):
+            ab_refs[h][e] = dot(rows, one_hot(rank_t_ref, e, capacity, h), NT).astype(BF)
 
 
 def data_back_kernel(
     experts, parts, cot_ref, ab_ref, tail_ref, slope_ref, up_ref, down_ref, gpre_ref, gy_ref, rows_ref
 ):
     rows = cot_ref.shape[0]
-    eye = (
-        lax.broadcasted_iota(jnp.int32, (LANES, LANES), 0)
-        == lax.broadcasted_iota(jnp.int32, (LANES, LANES), 1)
-    )
-    rows_t = dot(jnp.where(eye, 1.0, 0.0).astype(BF), tail_ref[...], NT)
-    halt_row = vector_row(rows_t, A_EXP + experts, 4)
-    ab = ab_ref[0].astype(F32)
-    live = ab[0:1, :] + ab[1:2, :] + ab[2:3, :]
-    bent = ab[3:4, :] + ab[4:5, :] + ab[5:6, :]
-    cols = jnp.transpose(jnp.concatenate([live, bent, jnp.zeros((LANES - 2, rows), F32)], axis=0))
+    halt_row = vector_row(turned_tail(tail_ref[...]), A_EXP + experts, 4)
+    cols = []
+    for i in range(ab_ref.shape[0]):
+        ab = ab_ref[i].astype(F32)
+        live = ab[0:1, :] + ab[1:2, :] + ab[2:3, :]
+        bent = ab[3:4, :] + ab[4:5, :] + ab[5:6, :]
+        filler = jnp.zeros((LANES - 2, ab.shape[1]), F32)
+        cols.append(jnp.transpose(jnp.concatenate([live, bent, filler], axis=0)))
+    cols = jnp.concatenate(cols, axis=0)
     gy = (cols[:, 0:1] * cot_ref[...].astype(F32) + cols[:, 1:2] * halt_row).astype(BF)
     gy_ref[...] = gy
     total = jnp.zeros((rows, D), F32)
@@ -386,7 +429,8 @@
     rows_ref[...] = total.astype(BF)
 
 
-def weight_back_kernel(parts, x_ref, gy_ref, gpre_ref, act_ref, gup_ref, gdown_ref, up_acc, down_acc):
+def weight_back_kernel(parts, steps, joined, *refs):
+    up_acc, down_acc = refs[-2:]
     step = pl.program_id(0)
 
     @pl.when(step == 0)
@@ -394,79 +438,74 @@
         up_acc[...] = jnp.zeros(up_acc.shape, F32)
         down_acc[...] = jnp.zeros(down_acc.shape, F32)
 
-    for c in range(parts):
-        up_acc[c] += dot(x_ref[...], gpre_ref[c], TN)
-        down_acc[c] += dot(gy_ref[...], act_ref[c], TN)
+    for h in range(HALVES):
+        x_ref, gy_ref, gpre_ref, act_ref = refs[4 * h : 4 * h + 4]
+
+        @pl.when(step // steps == h)
+        def _(x_ref=x_ref, gy_ref=gy_ref, gpre_ref=gpre_ref, act_ref=act_ref):
+            for c in range(parts):
+                up_acc[c] += dot(x_ref[...], gpre_ref[c], TN)
+                down_acc[c] += dot(gy_ref[...], act_ref[c], TN)
 
     @pl.when(step == pl.num_programs(0) - 1)
     def _():
         for c in range(parts):
-            gup_ref[c] = up_acc[c].astype(BF)
-            gdown_ref[c] = jnp.transpose(down_acc[c]).astype(BF)
-
-
-def attend_back_kernel(
+            if joined:
+                refs[-3][c, :D] = up_acc[c].astype(BF)
+                refs[-3][c, D:] = jnp.transpose(down_acc[c]).astype(BF)
+            else:
+                refs[-4][c] = up_acc[c].astype(BF)
+                refs[-3][c] = jnp.transpose(down_acc[c]).astype(BF)
+
+
+def hidden_back_kernel(
     experts,
     capacity,
-    back_ref,
+    first_ref,
+    second_ref,
     rank_ref,
     hidden_ref,
-    tok_ref,
     w_ref,
     meta_ref,
     cot_ref,
     slope_ref,
     glf_ref,
-    row_ref,
     mixed_ref,
     so_ref,
-    lse_ref,
     gates_ref,
-    slotq_ref,
-    kv_ref,
-    gin_ref,
-    pack_ref,
+    gout_ref,
     gh_ref,
-    n1_ref,
-    gx_ref,
     gslot_ref,
     gla_ref,
-    wide_ref,
-    acc_ref,
     rv_ref,
     vec_ref,
-    kx_ref,
-    vx_ref,
-    lset_ref,
-    gq_ref,
+    acc_ref,
 ):
     tok = hidden_ref.shape[0]
-    blocks = tok // BLOCK
     first = A_EXP + experts
+    size = capacity // HALVES
     rows_t = transposed_tail(w_ref)
     low_t = rows_t.astype(BF)
-    gain_one, shift_one, gain_two, shift_two, halt_row = (
-        vector_row(rows_t, first, i) for i in range(5)
-    )
+    gain_two, shift_two, halt_row = (vector_row(rows_t, first, i) for i in (2, 3, 4))
     lane = lane_ids(BLOCK)
     upper = lane >= HEAD
     lane_half = jnp.where(upper, 1, 0)
     vec_ref[...] = jnp.zeros(vec_ref.shape, F32)
-    vec_ref[4:5, :] = row_ref[0:1, :]
     acc_ref[...] = jnp.zeros(acc_ref.shape, F32)
     rv_ref[...] = jnp.zeros(rv_ref.shape, F32)
 
-    def hidden_back(b, _):
+    def block(b, _):
         rows = pl.ds(b * BLOCK, BLOCK)
         meta = meta_ref[rows, :]
         rank = rank_ref[rows, :].astype(jnp.int32)
         active = jnp.where(meta[:, 6:7] >= STEP, 1.0, 0.0)
-        place = lax.broadcasted_iota(jnp.int32, (BLOCK, capacity), 1)
+        place = lax.broadcasted_iota(jnp.int32, (BLOCK, size), 1)
         glf_high, glf_low = split_two(glf_ref[rows, :])
         grad = dot(glf_high, low_t) + dot(glf_low, low_t)
-        for e in range(experts):
-            hot = jnp.where(place == rank[:, e : e + 1], 1.0, 0.0).astype(BF)
-            grad = grad + dot(hot, back_ref[e])
+        for h, back_ref in enumerate((first_ref, second_ref)):
+            for e in range(experts):
+                hot = jnp.where(place + h * size == rank[:, e : e + 1], 1.0, 0.0).astype(BF)
+                grad = grad + dot(hot, back_ref[e])
         hat, inv = norm_stats(hidden_ref[rows, :])
         normed = (hat * gain_two + shift_two).astype(BF)
         rv_ref[...] += dot(normed, glf_high, TN) + dot(normed, glf_low, TN)
@@ -496,16 +535,59 @@
             value = gates[:, k : k + 1] * (grads[k] - weighted)
             gla = jnp.where(lane == meta[:, k : k + 1], value, gla)
         gla_ref[rows, :] = gla
-        kv = kv_ref[rows, :].astype(F32)
-        swapped = pltpu.roll(kv, HEAD, 1)
-        kx_ref[0, rows, :] = jnp.where(upper, 0.0, kv).astype(BF)
-        kx_ref[1, rows, :] = jnp.where(upper, swapped, 0.0).astype(BF)
-        vx_ref[0, rows, :] = jnp.where(upper, 0.0, swapped).astype(BF)
-        vx_ref[1, rows, :] = jnp.where(upper, kv, 0.0).astype(BF)
         return 0
 
-    lax.fori_loop(0, blocks, hidden_back, 0)
-    pack_ref[:, WIDTH:KV_AT] = acc_ref[...].astype(BF)
+    lax.fori_loop(0, tok // BLOCK, block, 0)
+    gout_ref[...] = acc_ref[...].astype(BF)
+
+
+def input_back_kernel(
+    experts,
+    tok_ref,
+    w_ref,
+    meta_ref,
+    gh_ref,
+    gslot_ref,
+    gla_ref,
+    rvin_ref,
+    vecin_ref,
+    halt_ref,
+    lse_ref,
+    slotq_ref,
+    kv_ref,
+    gin_ref,
+    pack_ref,
+    gx_ref,
+    wide_ref,
+    acc_ref,
+    rv_ref,
+    vec_ref,
+    kx_ref,
+    vx_ref,
+    lset_ref,
+    gq_ref,
+):
+    tok = tok_ref.shape[0]
+    blocks = tok // BLOCK
+    first = A_EXP + experts
+    rows_t = transposed_tail(w_ref)
+    low_t = rows_t.astype(BF)
+    gain_one, shift_one = (vector_row(rows_t, first, i) for i in range(2))
+    lane = lane_ids(BLOCK)
+    upper = lane >= HEAD
+    lane_half = jnp.where(upper, 1, 0)
+    all_upper = lane_ids(tok) >= HEAD
+    vec_ref[...] = jnp.zeros(vec_ref.shape, F32)
+    vec_ref[2:4, :] = vecin_ref[2:4, :]
+    vec_ref[4:5, :] = halt_ref[0:1, :]
+    acc_ref[...] = jnp.zeros(acc_ref.shape, F32)
+    rv_ref[...] = rvin_ref[...]
+    kv = kv_ref[...].astype(F32)
+    swapped = pltpu.roll(kv, HEAD, 1)
+    kx_ref[0] = jnp.where(all_upper, 0.0, kv).astype(BF)
+    kx_ref[1] = jnp.where(all_upper, swapped, 0.0).astype(BF)
+    vx_ref[0] = jnp.where(all_upper, 0.0, swapped).astype(BF)
+    vx_ref[1] = jnp.where(all_upper, kv, 0.0).astype(BF)
     lset_ref[...] = jnp.transpose(lse_ref[...])
 
     above = lax.broadcasted_iota(jnp.int32, (BLOCK, BLOCK), 0) <= lax.broadcasted_iota(
@@ -538,8 +620,6 @@
 
         lax.fori_loop(0, A_TOP // 2, pair, 0)
 
-    acc_ref[...] = jnp.zeros(acc_ref.shape, F32)
-
     def input_back(b, gkv_sum):
         rows = pl.ds(b * BLOCK, BLOCK)
         meta = meta_ref[rows, :]
@@ -567,12 +647,10 @@
 
     gkv_sum = lax.fori_loop(0, blocks, input_back, jnp.zeros((D, LANES), F32))
     pack_ref[:, :WIDTH] = acc_ref[...].astype(BF)
-    pack_ref[:, KV_AT:RV_AT] = gkv_sum.astype(BF)
-    turned = jnp.transpose(vec_ref[...])
-    turned = pltpu.roll(turned, first, 1)
-    wide_lane = lane_ids(D)
-    tail = jnp.where(wide_lane < first, rv_ref[...], turned)
-    pack_ref[:, RV_AT:PACK] = tail.astype(BF)
+    pack_ref[:, WIDTH : WIDTH + LANES] = gkv_sum.astype(BF)
+    turned = pltpu.roll(jnp.transpose(vec_ref[...]), first, 1)
+    tail = jnp.where(lane_ids(D) < first, rv_ref[...], turned)
+    pack_ref[:, WIDTH + LANES :] = tail.astype(BF)
 
 
 VMEM_LIMIT = 60 * 1024 * 1024
@@ -586,10 +664,9 @@
     return [pl.BlockSpec(memory_space=pltpu.VMEM)] * count
 
 
-def call(kernel, name, inputs, outs, scratch=()):
+def call(kernel, inputs, outs, scratch=()):
     return pl.pallas_call(
         kernel,
-        name=name,
         out_shape=outs,
         in_specs=in_vmem(len(inputs)),
         out_specs=in_vmem(len(outs)),
@@ -598,8 +675,41 @@
     )(*inputs)
 
 
-def constant_spec(shape):
-    return pl.BlockSpec(shape, lambda s: (0,) * len(shape), pipeline_mode=pl.Buffered(1))
+def constant_spec(shape, middle=0):
+    return pl.BlockSpec(shape, lambda s: (0, middle, 0), pipeline_mode=pl.Buffered(1))
+
+
+def gather_pieces(pack, shape):
+    groups, experts, _ = shape
+    if experts != 8 or groups != 4:
+        own = lax.all_gather(pack, "dp", axis=0, tiled=False)
+        every = lax.all_gather(own, "fsdp", axis=0, tiled=False)
+        return [every.transpose(1, 0, 2, 3).reshape(D, PACK)]
+
+    own = [pack]
+    for d in range(1, groups):
+        pairs = [((i + d) % groups, i) for i in range(groups)]
+        own.append(lax.ppermute(pack, "dp", pairs))
+    own = jnp.stack(own)
+
+    def swap(values, m):
+        return lax.ppermute(values, "fsdp", [(i, i ^ m) for i in range(experts)])
+
+    along, across = swap(own, 2), swap(own, 4)
+    low = swap(along[: groups // 2], 4)
+    high = swap(across[groups // 2 :], 2)
+    return [
+        own,
+        swap(own, 1),
+        along,
+        swap(along, 1),
+        across,
+        swap(across, 1),
+        low,
+        high,
+        swap(low, 1),
+        swap(high, 1),
+    ]
 
 
 def on_device(
@@ -628,31 +738,39 @@
     tail = jnp.concatenate([router, vectors.T], axis=1)
     tail = jnp.pad(tail, ((0, 0), (0, LANES - tail.shape[1])))
     pack = jnp.concatenate([w_query, w_out.T, w_kv, tail], axis=1)
-    pack = lax.all_gather(pack, "dp", axis=0, tiled=False)
-    pack = lax.all_gather(pack, "fsdp", axis=0, tiled=False)
-    weights = pack.transpose(1, 0, 2, 3).reshape(D, PACK)
-    whole_up = lax.all_gather(w_up[0], "dp", axis=0, tiled=False)
-    whole_down = lax.all_gather(w_down[0], "dp", axis=0, tiled=False)
+    shape = (groups, experts, shard)
+    pieces = gather_pieces(pack, shape)
+    joined = slice_width == D
+    if joined:
+        expert_pack = jnp.concatenate([w_up[0], w_down[0]], axis=0)
+        whole_up = whole_down = lax.all_gather(expert_pack, "dp", axis=0, tiled=False)
+    else:
+        whole_up = lax.all_gather(w_up[0], "dp", axis=0, tiled=False)
+        whole_down = lax.all_gather(w_down[0], "dp", axis=0, tiled=False)
 
     meta = jnp.concatenate([attn_routes, ffn_routes, depths[:, None], depths[:, None]], axis=1)
     scal = jnp.stack([halt_in, cot_halt], axis=1)
-
-    rank, rank_t, cot_slots = call(
+    half = capacity // HALVES
+    half_slots = slots // HALVES
+    slot_shape = whole((experts, half, D), BF)
+
+    rank, rank_t, *cot_slots = call(
         partial(slots_kernel, experts, capacity),
-        "slots",
         (meta, cot_out),
+        (whole((tok, LANES), F32), whole((LANES, tok), jnp.int32)) + (slot_shape,) * HALVES,
+    )
+
+    def exchange(values):
+        return lax.all_to_all(values, "fsdp", split_axis=0, concat_axis=0, tiled=True)
+
+    *pieces, cot_first = lax.optimization_barrier((*pieces, cot_slots[0]))
+    owned_cot = [exchange(cot_first)]
+
+    weights, slotq, kv, so, lse, gates, mixed, hidden, fgate, *n2_slots = call(
+        partial(attend_kernel, experts, capacity, shape),
+        (tokens, meta, rank_t, *pieces),
         (
-            whole((tok, LANES), F32),
-            whole((LANES, tok), jnp.int32),
-            whole((experts, capacity, D), BF),
-        ),
-    )
-
-    slotq, kv, so, lse, gates, mixed, hidden, fgate, n2_slots = call(
-        partial(attend_kernel, experts, capacity),
-        "attend",
-        (tokens, weights, meta, rank_t),
-        (
+            whole((D, PACK), BF),
             whole((2, tok, LANES), BF),
             whole((tok, LANES), BF),
             whole((2, tok, LANES), F32),
@@ -661,117 +779,174 @@
             whole((tok, WIDTH), BF),
             whole((tok, D), F32),
             whole((tok, LANES), F32),
-            whole((experts, capacity, D), BF),
-        ),
+        )
+        + (slot_shape,) * HALVES,
         (
             pltpu.VMEM((2, tok, LANES), BF),
             pltpu.VMEM((2, tok, LANES), BF),
             pltpu.VMEM((tok, D), BF),
         ),
     )
-
-    def exchange(values):
-        return lax.all_to_all(values, "fsdp", split_axis=0, concat_axis=0, tiled=True)
-
-    owned_cot = exchange(cot_slots).reshape(slots, D)
-    owned = exchange(n2_slots).reshape(slots, D)
-
-    row_spec = pl.BlockSpec((capacity, D), lambda s: (s, 0))
-    wide_spec = pl.BlockSpec((groups, capacity, slice_width), lambda s: (0, s, 0))
+    n2_slots[0], owned_cot[0] = lax.optimization_barrier((n2_slots[0], owned_cot[0]))
+
     up_spec = constant_spec((groups, D, slice_width))
-    down_spec = constant_spec((groups, slice_width, D))
+    down_spec = constant_spec((groups, slice_width, D), 1 if joined else 0)
     params = pltpu.CompilerParams(vmem_limit_bytes=VMEM_LIMIT)
-    wide = whole((groups, slots, slice_width), BF)
-    owned_out, act, slope = pl.pallas_call(
-        partial(expert_kernel, groups),
-        name="expert",
-        grid=(experts,),
-        out_shape=(whole((slots, D), BF), wide, wide),
-        in_specs=[row_spec, up_spec, down_spec],
-        out_specs=[row_spec, wide_spec, wide_spec],
+    wide = whole((groups, half_slots, slice_width), BF)
+    narrow = whole((half_slots, D), BF)
+    step_rows = max(half, min(512, half_slots))
+    step_spec = pl.BlockSpec((step_rows, D), lambda s: (s, 0))
+    step_wide = pl.BlockSpec((groups, step_rows, slice_width), lambda s: (0, s, 0))
+
+    owned = []
+    for h in range(HALVES):
+        owned.append(exchange(n2_slots[h]).reshape(half_slots, D))
+        if h + 1 < HALVES:
+            n2_slots[h + 1], owned[h] = lax.optimization_barrier((n2_slots[h + 1], owned[h]))
+    outs, acts, slopes = [], [], []
+    for h in range(HALVES):
+        out, act, slope = pl.pallas_call(
+            partial(expert_kernel, groups),
+            grid=(half_slots // step_rows,),
+            out_shape=(narrow, wide, wide),
+            in_specs=[step_spec, up_spec, down_spec],
+            out_specs=[step_spec, step_wide, step_wide],
+            compiler_params=params,
+        )(owned[h], whole_up, whole_down)
+        outs.append(out)
+        acts.append(act)
+        slopes.append(slope)
+    back = [exchange(out.reshape(experts, half, D)) for out in outs]
+
+    tail_spec = pl.BlockSpec((D, LANES), lambda s: (0, RV_AT // LANES))
+    full = pl.BlockSpec(memory_space=pltpu.VMEM)
+    sums = pl.pallas_call(
+        partial(combine_first_kernel, experts, capacity),
+        name="combine_first",
+        grid=(1,),
+        out_shape=(whole((tok, D), F32), whole((tok, LANES), F32), whole((tok, LANES), F32)),
+        in_specs=[full, full, tail_spec, full, full],
+        out_specs=[full] * 3,
         compiler_params=params,
-    )(owned, whole_up, whole_down)
-
-    back = exchange(owned_out.reshape(experts, capacity, D))
-    block_out, halt_wide, halt_slope, glf, halt_grad, ab = call(
+    )(back[0], rank, weights, fgate, cot_out)
+    back[1], cot_second = lax.optimization_barrier((back[1], cot_slots[1]))
+    owned_cot.append(exchange(cot_second))
+    ab_shape = whole((experts, 8, half), BF)
+    block_out, halt_wide, halt_slope, glf, halt_grad, *ab = pl.pallas_call(
         partial(combine_kernel, experts, capacity),
-        "combine",
-        (back, rank, rank_t, hidden, weights, meta, fgate, scal, cot_out),
-        (
+        name="combine",
+        grid=(1,),
+        out_shape=(
             whole((tok, D), BF),
             whole((tok, LANES), F32),
             whole((tok, LANES), F32),
             whole((tok, LANES), F32),
             whole((8, D), F32),
-            whole((experts, 8, capacity), BF),
-        ),
-        (pltpu.VMEM((6, tok, LANES), BF),),
-    )
+        )
+        + (ab_shape,) * HALVES,
+        in_specs=[full] * 7 + [tail_spec] + [full] * 4,
+        out_specs=[full] * (5 + HALVES),
+        scratch_shapes=[pltpu.VMEM((6, tok, LANES), BF)],
+        compiler_params=params,
+    )(back[1], *sums, rank, rank_t, hidden, weights, meta, fgate, scal, cot_out)
     halt_out = halt_wide[:, 0]
-    owned_ab = exchange(ab)
-
-    gpre, gy, owned_rows = pl.pallas_call(
-        partial(data_back_kernel, experts, groups),
-        name="data_back",
-        grid=(experts,),
-        out_shape=(wide, whole((slots, D), BF), whole((slots, D), BF)),
-        in_specs=[
-            row_spec,
-            pl.BlockSpec((1, 8, capacity), lambda s: (s, 0, 0)),
-            pl.BlockSpec((D, LANES), lambda s: (0, RV_AT // LANES)),
-            wide_spec,
-            up_spec,
-            down_spec,
-        ],
-        out_specs=[wide_spec, row_spec, row_spec],
+    owned_ab = exchange(jnp.concatenate(ab, axis=1))
+    owned_ab = [owned_ab[:, 8 * h : 8 * h + 8] for h in range(HALVES)]
+
+    together = step_rows // half if half % LANES == 0 else 1
+    row_spec = pl.BlockSpec((together * half, D), lambda s: (s, 0))
+    wide_spec = pl.BlockSpec((groups, together * half, slice_width), lambda s: (0, s, 0))
+    gys, gpres, rows_back = [], [], []
+    for h in range(HALVES):
+        gpre, gy, owned_rows = pl.pallas_call(
+            partial(data_back_kernel, experts, groups),
+            grid=(experts // together,),
+            out_shape=(wide, narrow, narrow),
+            in_specs=[
+                row_spec,
+                pl.BlockSpec((together, 8, half), lambda s: (s, 0, 0)),
+                tail_spec,
+                wide_spec,
+                up_spec,
+                down_spec,
+            ],
+            out_specs=[wide_spec, row_spec, row_spec],
+            compiler_params=params,
+        )(owned_cot[h].reshape(half_slots, D), owned_ab[h], weights, slopes[h], whole_up, whole_down)
+        gys.append(gy)
+        gpres.append(gpre)
+        rows_back.append(exchange(owned_rows.reshape(experts, half, D)))
+
+    steps = half_slots // step_rows
+    specs, inputs = [], []
+    for h in range(HALVES):
+
+        def at(s, h=h):
+            return jnp.clip(s - h * steps, 0, steps - 1)
+
+        narrow_at = pl.BlockSpec((step_rows, D), lambda s, at=at: (at(s), 0))
+        wide_at = pl.BlockSpec((groups, step_rows, slice_width), lambda s, at=at: (0, at(s), 0))
+        specs += [narrow_at, narrow_at, wide_at, wide_at]
+        inputs += [owned[h], gys[h], gpres[h], acts[h]]
+    if joined:
+        grad_shapes = [(groups, 2 * D, D)]
+    else:
+        grad_shapes = [(groups, D, slice_width), (groups, slice_width, D)]
+    expert_grads = pl.pallas_call(
+        partial(weight_back_kernel, groups, steps, joined),
+        name="weight_back",
+        grid=(HALVES * steps,),
+        out_shape=[whole(g, BF) for g in grad_shapes],
+        in_specs=specs,
+        out_specs=[constant_spec(g) for g in grad_shapes],
+        scratch_shapes=[pltpu.VMEM((groups, D, slice_width), F32)] * 2,
         compiler_params=params,
-    )(owned_cot, owned_ab, weights, slope, whole_up, whole_down)
-    rows_back = exchange(owned_rows.reshape(experts, capacity, D))
-
-    grad_up, grad_down = pl.pallas_call(
-        partial(weight_back_kernel, groups),
-        name="weight_back",
-        grid=(experts,),
-        out_shape=(whole((groups, D, slice_width), BF), whole((groups, slice_width, D), BF)),
-        in_specs=[row_spec, row_spec, wide_spec, wide_spec],
-        out_specs=[constant_spec((groups, D, slice_width)), constant_spec((groups, slice_width, D))],
-        scratch_shapes=[
-            pltpu.VMEM((groups, D, slice_width), F32),
-            pltpu.VMEM((groups, D, slice_width), F32),
-        ],
-        compiler_params=params,
-    )(owned, gy, gpre, act)
-    part_up = lax.psum_scatter(grad_up, "dp", scatter_dimension=0, tiled=True).astype(F32)
-    part_down = lax.psum_scatter(grad_down, "dp", scatter_dimension=0, tiled=True).astype(F32)
-
-    grad_in, grads = call(
-        partial(attend_back_kernel, experts, capacity),
-        "attend_back",
+    )(*inputs)
+    expert_grads = [
+        lax.psum_scatter(g, "dp", scatter_dimension=0, tiled=True).astype(F32) for g in expert_grads
+    ]
+    if joined:
+        part_up, part_down = expert_grads[0][:, :D], expert_grads[0][:, D:]
+    else:
+        part_up, part_down = expert_grads
+
+    grad_out, gh, gslot, gla, rv, vec = call(
+        partial(hidden_back_kernel, experts, capacity),
         (
-            rows_back,
+            *rows_back,
             rank,
             hidden,
-            tokens,
             weights,
             meta,
             cot_out,
             halt_slope,
             glf,
-            halt_grad,
             mixed,
             so,
-            lse,
             gates,
-            slotq,
-            kv,
         ),
-        (whole((tok, D), BF), whole((D, PACK), BF)),
         (
-            pltpu.VMEM((tok, D), F32),
-            pltpu.VMEM((8, LANES), F32),
+            whole((D, WIDTH), BF),
+            whole((tok, D), F32),
+            whole((2, tok, LANES), BF),
+            whole((tok, LANES), F32),
+            whole((D, LANES), F32),
+            whole((8, D), F32),
+        ),
+        (pltpu.VMEM((D, WIDTH), F32),),
+    )
+
+    def reduced(grads):
+        sent = grads.reshape(groups, experts, shard, grads.shape[1]).transpose(1, 0, 2, 3)
+        return jnp.sum(exchange(sent).astype(F32), axis=0).astype(BF)
+
+    part_out = reduced(grad_out)
+    grad_in, grads = call(
+        partial(input_back_kernel, experts),
+        (tokens, weights, meta, gh, gslot, gla, rv, vec, halt_grad, lse, slotq, kv),
+        (whole((tok, D), BF), whole((D, WIDTH + 2 * LANES), BF)),
+        (
             pltpu.VMEM((2, 2, tok, LANES), F32),
-            pltpu.VMEM((2, tok, LANES), BF),
-            pltpu.VMEM((tok, LANES), F32),
             pltpu.VMEM((BLOCK, WIDTH), BF),
             pltpu.VMEM((D, WIDTH), F32),
             pltpu.VMEM((D, LANES), F32),
@@ -782,22 +957,20 @@
             pltpu.VMEM((2, tok, LANES), F32),
         ),
     )
-
-    sent = grads.reshape(groups, experts, shard, PACK).transpose(1, 0, 2, 3)
-    came = exchange(sent)
-    half = jnp.sum(came.astype(F32), axis=0).astype(BF)
-    came = lax.all_to_all(half, "dp", split_axis=0, concat_axis=0, tiled=True)
+    part = jnp.concatenate([reduced(grads), part_out], axis=2)
+    came = lax.all_to_all(part, "dp", split_axis=0, concat_axis=0, tiled=True)
     total = jnp.sum(came.astype(F32), axis=0)
-    routers = A_EXP + experts
+    kv_end = WIDTH + LANES
+    router_end = kv_end + A_EXP + experts
     return (
         block_out,
         halt_out,
         grad_in,
         total[:, :WIDTH],
-        total[:, WIDTH:KV_AT].T,
-        total[:, KV_AT:RV_AT],
-        total[:, RV_AT : RV_AT + routers],
-        total[:, RV_AT + routers : RV_AT + routers + 5].T,
+        total[:, WIDTH + 2 * LANES :].T,
+        total[:, WIDTH:kv_end],
+        total[:, kv_end:router_end],
+        total[:, router_end : router_end + 5].T,
         part_up,
         part_down,
     )
@@ -821,6 +994,7 @@
         P(both, None),
         P(both),
     )
+
     return jax.shard_map(
         on_device,
         mesh=mesh,

time: 556 us -> 483 us (0.87)
  waiting for transfers between devices: 149 us -> 68.7 us
  blocking collectives: 122 us -> 69.2 us
  Pallas kernels: 211 us -> 243 us
  starting transfers between devices: 27.3 us -> 51.2 us
  local copies, waits for them, and re-layouts: 13.5 us -> 20.6 us
    all_gather x3 -> x1, waiting for transfers between devices: 74.5 us -> 0.02 us  [on_device(): lax.all_gather(expert_pack, 'dp', axis=0, tiled=False)]
    all_to_all x3, blocking collectives: 106 us -> 69.2 us  [exchange(): lax.all_to_all(values, 'fsdp', split_axis=0, concat_axis=0, tiled=True)]
    pallas_call x7 -> x11, Pallas kernels: 211 us -> 243 us  [the longest x4 91.7 us: call(): pl.pallas_call(kernel, out_shape=outs, in_specs=in_vmem(len(inputs)), out...]
    all_to_all x3 -> x8, waiting for transfers between devices: 67.1 us -> 43.8 us  [exchange(): lax.all_to_all(values, 'fsdp', split_axis=0, concat_axis=0, tiled=True)]
    all_to_all x3 -> x8, starting transfers between devices: 13.8 us -> 31.3 us  [exchange(): lax.all_to_all(values, 'fsdp', split_axis=0, concat_axis=0, tiled=True)]
    all_gather x1 -> x0, blocking collectives: 16.9 us -> none  [on_device(): pack = lax.all_gather(pack, 'dp', axis=0, tiled=False)]
    ppermute x0 -> x12, waiting for transfers between devices: none -> 16 us  [the longest x9 9.36 us: swap(): return lax.ppermute(values, 'fsdp', [(i, i ^ m) for i in range(experts)])]
    ppermute x0 -> x12, starting transfers between devices: none -> 13 us  [the longest x9 6.81 us: swap(): return lax.ppermute(values, 'fsdp', [(i, i ^ m) for i in range(experts)])]
  transfers between devices with their start and end apart: 9 -> 23, of which waited for: 6 -> 10; matrix products, arithmetic and copies ran while one was open for 3% -> 3% of each run, Pallas kernels for 20% -> 47%
where the time goes in v2:
time: 483 us; the launch traced here: 474 us
  Pallas kernels  243 us (50%)
  blocking collectives  69.2 us (14%)
  waiting for transfers between devices  68.7 us (14%)
  starting transfers between devices  51.2 us (11%)
  local copies, waits for them, and re-layouts  20.6 us (4%)
  between operations  14.6 us (3%)
  other arithmetic  6.75 us (1%)
    pallas_call x4, Pallas kernels, call(): pl.pallas_call(kernel, out_shape=outs, in_specs=in_vmem(len(inputs)), out...  91.7 us
    all_to_all x3, blocking collectives, exchange(): lax.all_to_all(values, 'fsdp', split_axis=0, concat_axis=0, tiled=True)  69.2 us
    pallas_call x2, Pallas kernels, on_device(): pl.pallas_call(partial(expert_kernel, groups), grid=(half_slots // step_r...  56.3 us
    all_to_all x8, waiting for transfers between devices, exchange(): lax.all_to_all(values, 'fsdp', split_axis=0, concat_axis=0, tiled=True)  43.8 us
    pallas_call x2, Pallas kernels, on_device(): pl.pallas_call(partial(data_back_kernel, experts, groups), grid=(experts...  31.6 us
    all_to_all x8, starting transfers between devices, exchange(): lax.all_to_all(values, 'fsdp', split_axis=0, concat_axis=0, tiled=True)  31.3 us
    pallas_call x1, Pallas kernels, on_device(): pl.pallas_call(partial(weight_back_kernel, groups, steps, joined), name='...  27.2 us
    pallas_call x1, Pallas kernels, on_device(): pl.pallas_call(partial(combine_kernel, experts, capacity), name='combine'...  21.4 us
  transfers between devices with their start and end apart: 23, of which 10 were waited for; matrix products, arithmetic and copies ran while one was open for 3% of the time, Pallas kernels for 47%

profile of v2, /device:TPU:0, one launch (start us, length us, event | category | flops | bytes accessed | tf_op | source)
XLA Modules:
  0.0 473.8 jit_solution(16307135379144734473)
XLA Ops:
  15.8 4.9 %collective-permute-done.1 = bf16[16,3328]{1,0:T(8,128)(2,1)S(1)} collective-permute-done((bf16[16,3328]{1,0:T(8,128)(2,1)S(1)}, bf16[16,3328]{1,0:T(8,128)(2,1)S(1)}, u32[]{:S(2)}, u32[]{:S(2)}) %collective-permute-start.1) | collective-permute-done | bytes 106528 | tf_op jit(solution)/shard_map/ppermute | solution.py:692
  28.0 5.3 %collective-permute-done.6.refs_7_ = bf16[4,16,3328]{2,1,0:T(8,128)(2,1)S(1)} collective-permute-done((bf16[4,16,3328]{2,1,0:T(8,128)(2,1)S(1)}, bf16[4,16,3328]{2,1,0:T(8,128)(2,1)S(1)}, u32[]{:S(2)}, u32[]{:S(2)}) %collective-permute-start.6) | collective-permute-done | bytes 426016 | tf_op jit(solution)/shard_map/ppermute | solution.py:696
  42.0 9.7 %shard_map.213 = (f32[1024,128]{1,0:T(8,128)}, s32[128,1024]{1,0:T(8,128)}, bf16[8,256,512]{2,1,0:T(8,128)(2,1)}, bf16[8,256,512]{2,1,0:T(8,128)(2,1)}) custom-call(s32[1024,8]{1,0:T(8,128)} %copy.57.meta_ref.refs_1_, bf16[1024,512]{1,0:T(8,128)(2,1)} %cot_ref.7), custom_call_target="tpu_custom_call" | custom-call | tf_op jit(solution)/shard_map/pallas_call | solution.py:668
  56.5 33.8 %shard_map.214 = (bf16[512,3328]{1,0:T(8,128)(2,1)}, bf16[2,1024,128]{2,1,0:T(8,128)(2,1)}, bf16[1024,128]{1,0:T(8,128)(2,1)}, f32[2,1024,128]{2,1,0:T(8,128)}, ...) custom-call(bf16[1024,512]{1,0:T(8,128)(2,1)} %tok_ref.1, ...), custom_call_target="tpu_custom_call" | custom-call | tf_op jit(solution)/shard_map/pallas_call | solution.py:668
  90.4 30.9 %all_to_all.60 = bf16[8,256,512]{2,1,0:T(8,128)(2,1)} all-to-all(bf16[8,256,512]{2,1,0:T(8,128)(2,1)} %get-tuple-element.87), channel_id=1, replica_groups=mesh['dp'=4,'fsdp'=8] {'fsdp'}, dimensions={0} | all-to-all | bytes 4194304 | tf_op jit(solution)/shard_map/all_to_all | solution.py:764
  125.1 28.1 %shard_map.216 = (bf16[2048,512]{1,0:T(8,128)(2,1)}, bf16[4,2048,512]{2,1,0:T(8,128)(2,1)}, bf16[4,2048,512]{2,1,0:T(8,128)(2,1)}) custom-call(bf16[2048,512]{1,0:T(8,128)(2,1)} %bitcast.41, bf16[4,1024,512]{2,1,0:T(8,128)(2,1)} %bitcast.33, bf16[4,1024,512]{2,1,0:T(8,128)(2,1)} %bitcast.34), custom_call_target="tpu_custom_call" | custom-call | tf_op jit(solution)/shard_map/pallas_call | solution.py:808
  154.5 4.3 all-to-all-start.4
  158.9 28.2 %shard_map.215 = (bf16[2048,512]{1,0:T(8,128)(2,1)}, bf16[4,2048,512]{2,1,0:T(8,128)(2,1)}, bf16[4,2048,512]{2,1,0:T(8,128)(2,1)}) custom-call(bf16[2048,512]{1,0:T(8,128)(2,1)} %bitcast.43, bf16[4,1024,512]{2,1,0:T(8,128)(2,1)} %bitcast.35, bf16[4,1024,512]{2,1,0:T(8,128)(2,1)} %bitcast.36), custom_call_target="tpu_custom_call" | custom-call | tf_op jit(solution)/shard_map/pallas_call | solution.py:808
  187.1 4.5 all-to-all-start.3
  192.7 14.7 %combine_first.1 = (f32[1024,512]{1,0:T(8,128)}, f32[1024,128]{1,0:T(8,128)}, f32[1024,128]{1,0:T(8,128)}) custom-call(bf16[8,256,512]{2,1,0:T(8,128)(2,1)} %all-to-all-done.4.back_ref, f32[1024,128]{1,0:T(8,128)} %get-tuple-element.94.rank_ref, bf16[512,3328]{1,0:T(8,128)(2,1)} %get-tuple-element.95.tail_ref.w_ref, ...), custom_call_target="tpu_custom_call" | custom-call | tf_op jit(solution)/shard_map/combine_first/pallas_call | solution.py:823
  207.4 10.8 %all-to-all-done.3.back_ref = bf16[8,256,512]{2,1,0:T(8,128)(2,1)S(1)} async-done(((bf16[8,256,512]{2,1,0:T(8,128)(2,1)}), bf16[8,256,512]{2,1,0:T(8,128)(2,1)S(1)}, u32[]{:S(2)}, u32[]{:S(2)}) %all-to-all-start.3) | async-done | bytes 2097184 | tf_op jit(solution)/shard_map/all_to_all | solution.py:764
  219.6 21.4 %combine.1 = (bf16[1024,512]{1,0:T(8,128)(2,1)}, f32[1024,128]{1,0:T(8,128)}, f32[1024,128]{1,0:T(8,128)}, f32[1024,128]{1,0:T(8,128)}, f32[8,512]{1,0:T(8,128)}...) custom-call(bf16[8,256,512]{2,1,0:T(8,128)(2,1)} %copy-done.2, f32[1024,512]{1,0:T(8,128)} %get-tuple-element.97.branch_ref, ...), custom_call_target="tpu_custom_call" | custom-call | tf_op jit(solution)/shard_map/combine/pallas_call | solution.py:835
  241.7 7.4 %all_to_all.61 = bf16[8,16,256]{2,1,0:T(8,128)(2,1)S(1)} all-to-all(bf16[8,16,256]{2,1,0:T(8,128)(2,1)S(1)} %pad_maximum_fusion.4), channel_id=1, replica_groups=mesh['dp'=4,'fsdp'=8] {'fsdp'}, dimensions={0} | all-to-all | bytes 131072 | tf_op jit(solution)/shard_map/all_to_all | solution.py:764
  253.3 15.8 %shard_map.217 = (bf16[4,2048,512]{2,1,0:T(8,128)(2,1)}, bf16[2048,512]{1,0:T(8,128)(2,1)}, bf16[2048,512]{1,0:T(8,128)(2,1)}) custom-call(bf16[2048,512]{1,0:T(8,128)(2,1)} %bitcast.45, bf16[8,8,256]{2,1,0:T(8,128)(2,1)} %get-tuple-element.181.ab_ref, bf16[512,3328]{1,0:T(8,128)(2,1)} %get-tuple-element.95.tail_ref.w_ref, ...), custom_call_target="tpu_custom_call" | custom-call | tf_op jit(solution)/shard_map/pallas_call | solution.py:861
  269.1 10.1 %all-to-all-done.7 = bf16[8,256,512]{2,1,0:T(8,128)(2,1)S(1)} async-done(((bf16[8,256,512]{2,1,0:T(8,128)(2,1)}), bf16[8,256,512]{2,1,0:T(8,128)(2,1)S(1)}, u32[]{:S(2)}, u32[]{:S(2)}) %all-to-all-start.7) | async-done | bytes 2097184 | tf_op jit(solution)/shard_map/all_to_all | solution.py:764
  284.7 15.8 %shard_map.218 = (bf16[4,2048,512]{2,1,0:T(8,128)(2,1)}, bf16[2048,512]{1,0:T(8,128)(2,1)}, bf16[2048,512]{1,0:T(8,128)(2,1)}) custom-call(bf16[2048,512]{1,0:T(8,128)(2,1)} %bitcast.46, bf16[8,8,256]{2,1,0:T(8,128)(2,1)} %get-tuple-element.180.ab_ref, bf16[512,3328]{1,0:T(8,128)(2,1)} %get-tuple-element.95.tail_ref.w_ref, ...), custom_call_target="tpu_custom_call" | custom-call | tf_op jit(solution)/shard_map/pallas_call | solution.py:861
  300.5 27.2 %weight_back.1 = bf16[4,1024,512]{2,1,0:T(8,128)(2,1)} custom-call(bf16[2048,512]{1,0:T(8,128)(2,1)} %bitcast.42, bf16[2048,512]{1,0:T(8,128)(2,1)} %get-tuple-element.128.refs_1_, bf16[4,2048,512]{2,1,0:T(8,128)(2,1)} %get-tuple-element.129.refs_2_, bf16[4,2048,512]{2,1,0:T(8,128)(2,1)} %get-tuple-element.130.refs_3_, bf16[2048,512]{1,0:T(8,128)(2,1)} %bitcast.44, ...), custom_call_target="tpu_custom_call" | custom-call | tf_op jit(solution)/shard_map/weight_back/pallas_call | solution.py:895
  327.7 30.9 %all_to_all.62.second_ref = bf16[8,256,512]{2,1,0:T(8,128)(2,1)} all-to-all(bf16[8,256,512]{2,1,0:T(8,128)(2,1)} %bitcast.48), channel_id=1, replica_groups=mesh['dp'=4,'fsdp'=8] {'fsdp'}, dimensions={0} | all-to-all | bytes 4194304 | tf_op jit(solution)/shard_map/all_to_all | solution.py:764
  358.6 21.6 %shard_map.219 = (bf16[512,1536]{1,0:T(8,128)(2,1)}, f32[1024,512]{1,0:T(8,128)}, bf16[2,1024,128]{2,1,0:T(8,128)(2,1)}, f32[1024,128]{1,0:T(8,128)}, f32[512,128]{1,0:T(8,128)}, /*index=5*/f32[8,512]{1,0:T(8,128)}) custom-call(bf16[8,256,512]{2,1,0:T(8,128)(2,1)} %copy-done.1, bf16[8,256,512]{2,1,0:T(8,128)(2,1)} %all_to_all.62.second_ref, ...), custom_call_target="tpu_custom_call" | custom-call | tf_op jit(solution)/shard_map/pallas_call | solution.py:668
  386.7 26.5 %shard_map.220 = (bf16[1024,512]{1,0:T(8,128)(2,1)}, bf16[512,1792]{1,0:T(8,128)(2,1)}) custom-call(bf16[1024,512]{1,0:T(8,128)(2,1)} %tok_ref.1, bf16[512,3328]{1,0:T(8,128)(2,1)} %get-tuple-element.95.tail_ref.w_ref, s32[1024,8]{1,0:T(8,128)} %copy.57.meta_ref.refs_1_, f32[1024,512]{1,0:T(8,128)} %get-tuple-element.116.gh_ref, ...), custom_call_target="tpu_custom_call" | custom-call | tf_op jit(solution)/shard_map/pallas_call | solution.py:668
  416.2 4.2 all-to-all-start.9
  421.3 22.9 %all-to-all-done.9 = bf16[8,4,16,1792]{3,2,1,0:T(8,128)(2,1)S(1)} async-done(((bf16[8,4,16,1792]{3,2,1,0:T(8,128)(2,1)}), bf16[8,4,16,1792]{3,2,1,0:T(8,128)(2,1)S(1)}, u32[]{:S(2)}, u32[]{:S(2)}) %all-to-all-start.9) | async-done | bytes 1835040 | tf_op jit(solution)/shard_map/all_to_all | solution.py:764
  445.3 6.4 %all-to-all-start.11 = ((bf16[4,16,3328]{2,1,0:T(8,128)(2,1)}), bf16[4,16,3328]{2,1,0:T(8,128)(2,1)S(1)}, u32[]{:S(2)}, u32[]{:S(2)}) async-start(bf16[4,16,3328]{2,1,0:T(8,128)(2,1)} %pad_maximum_fusion.2), calls=%async_computation.11 | async-start | bytes 851968 | tf_op jit(solution)/shard_map/all_to_all | solution.py:961
  452.5 8.8 %all-to-all-done.11 = bf16[4,16,3328]{2,1,0:T(8,128)(2,1)S(1)} async-done(((bf16[4,16,3328]{2,1,0:T(8,128)(2,1)}), bf16[4,16,3328]{2,1,0:T(8,128)(2,1)S(1)}, u32[]{:S(2)}, u32[]{:S(2)}) %all-to-all-start.11) | async-done | bytes 426016 | tf_op jit(solution)/shard_map/all_to_all | solution.py:961
  (106 shorter events, 65.0 us)
Async XLA Ops:
  7.2 117.9 %all-gather.3.cloned.1.call-start = ((), (), s32[]{:S(2)}) async-start(), calls=%async_computation.14 | async-start | bytes 5242880 | tf_op jit(solution)/shard_map/all_gather | solution.py:746
  9.6 11.1 %collective-permute-start.1 = (bf16[16,3328]{1,0:T(8,128)(2,1)S(1)}, bf16[16,3328]{1,0:T(8,128)(2,1)S(1)}, u32[]{:S(2)}, u32[]{:S(2)}) collective-permute-start(bf16[16,3328]{1,0:T(8,128)(2,1)S(1)} %get-tuple-element.179), channel_id=1, source_target_pairs={{16,0},{24,8},{0,16},{8,24},{17,1},{25,9},{1,17},{9,25},{18,2},{26... | collective-permute-start | bytes 319496 | tf_op jit(solution)/shard_map/ppermute | solution.py:692
  13.7 6.9 %collective-permute-start = (bf16[16,3328]{1,0:T(8,128)(2,1)S(1)}, bf16[16,3328]{1,0:T(8,128)(2,1)S(1)}, u32[]{:S(2)}, u32[]{:S(2)}) collective-permute-start(bf16[16,3328]{1,0:T(8,128)(2,1)S(1)} %get-tuple-element.179), channel_id=1, source_target_pairs={{8,0},{16,8},{24,16},{0,24},{9,1},{17,9},{25,17},{1,25},{10,2},{18... | collective-permute-start | bytes 319496 | tf_op jit(solution)/shard_map/ppermute | solution.py:692
  15.1 7.3 %collective-permute-start.2 = (bf16[16,3328]{1,0:T(8,128)(2,1)S(1)}, bf16[16,3328]{1,0:T(8,128)(2,1)S(1)}, u32[]{:S(2)}, u32[]{:S(2)}) collective-permute-start(bf16[16,3328]{1,0:T(8,128)(2,1)S(1)} %get-tuple-element.179), channel_id=1, source_target_pairs={{24,0},{0,8},{8,16},{16,24},{25,1},{1,9},{9,17},{17,25},{26,2},{2,... | collective-permute-start | bytes 319496 | tf_op jit(solution)/shard_map/ppermute | solution.py:692
  22.5 10.8 %collective-permute-start.6 = (bf16[4,16,3328]{2,1,0:T(8,128)(2,1)S(1)}, bf16[4,16,3328]{2,1,0:T(8,128)(2,1)S(1)}, u32[]{:S(2)}, u32[]{:S(2)}) collective-permute-start(bf16[4,16,3328]{2,1,0:T(8,128)(2,1)S(1)} %pad_maximum_fusion.1.refs_3_), channel_id=1, source_target_pairs={{0,4},{1,5},{2,6},{3,7},{4,0},{5,1},{6,2},{7,3},{8,12},{9,13},{10,... | collective-permute-start | bytes 1277960 | tf_op jit(solution)/shard_map/ppermute | solution.py:696
  24.1 10.8 %collective-permute-start.4 = (bf16[4,16,3328]{2,1,0:T(8,128)(2,1)S(1)}, bf16[4,16,3328]{2,1,0:T(8,128)(2,1)S(1)}, u32[]{:S(2)}, u32[]{:S(2)}) collective-permute-start(bf16[4,16,3328]{2,1,0:T(8,128)(2,1)S(1)} %pad_maximum_fusion.1.refs_3_), channel_id=1, source_target_pairs={{0,2},{1,3},{2,0},{3,1},{4,6},{5,7},{6,4},{7,5},{8,10},{9,11},{10,... | collective-permute-start | bytes 1277960 | tf_op jit(solution)/shard_map/ppermute | solution.py:696
  27.9 23.8 %collective-permute-start.3 = (bf16[4,16,3328]{2,1,0:T(8,128)(2,1)S(1)}, bf16[4,16,3328]{2,1,0:T(8,128)(2,1)S(1)}, u32[]{:S(2)}, u32[]{:S(2)}) collective-permute-start(bf16[4,16,3328]{2,1,0:T(8,128)(2,1)S(1)} %pad_maximum_fusion.1.refs_3_), channel_id=1, source_target_pairs={{0,1},{1,0},{2,3},{3,2},{4,5},{5,4},{6,7},{7,6},{8,9},{9,8},{10,11... | collective-permute-start | bytes 1277960 | tf_op jit(solution)/shard_map/ppermute | solution.py:696
  33.3 5.9 %collective-permute-start.9 = (bf16[2,16,3328]{2,1,0:T(8,128)(2,1)S(1)}, bf16[2,16,3328]{2,1,0:T(8,128)(2,1)S(1)}, u32[]{:S(2)}, u32[]{:S(2)}) collective-permute-start(bf16[2,16,3328]{2,1,0:T(8,128)(2,1)S(1)} %slice.49), channel_id=1, source_target_pairs={{0,2},{1,3},{2,0},{3,1},{4,6},{5,7},{6,4},{7,5},{8,10},{9,11},{10,... | collective-permute-start | bytes 638984 | tf_op jit(solution)/shard_map/ppermute | solution.py:696
  35.0 6.0 %collective-permute-start.8 = (bf16[2,16,3328]{2,1,0:T(8,128)(2,1)S(1)}, bf16[2,16,3328]{2,1,0:T(8,128)(2,1)}, u32[]{:S(2)}, u32[]{:S(2)}) collective-permute-start(bf16[2,16,3328]{2,1,0:T(8,128)(2,1)S(1)} %slice.48), channel_id=1, source_target_pairs={{0,4},{1,5},{2,6},{3,7},{4,0},{5,1},{6,2},{7,3},{8,12},{9,13},{10,... | collective-permute-start | bytes 638984 | tf_op jit(solution)/shard_map/ppermute | solution.py:696
  36.5 15.2 %collective-permute-start.7 = (bf16[4,16,3328]{2,1,0:T(8,128)(2,1)S(1)}, bf16[4,16,3328]{2,1,0:T(8,128)(2,1)S(1)}, u32[]{:S(2)}, u32[]{:S(2)}) collective-permute-start(bf16[4,16,3328]{2,1,0:T(8,128)(2,1)S(1)} %collective-permute-done.6.refs_7_), channel_id=1, source_target_pairs={{0,1},{1,0},{2,3},{3,2},{4,5},{5,4},{6,7},{7,6},{8,9},{9,8},{10,11... | collective-permute-start | bytes 1277960 | tf_op jit(solution)/shard_map/ppermute | solution.py:696
  36.5 15.2 %collective-permute-start.5 = (bf16[4,16,3328]{2,1,0:T(8,128)(2,1)S(1)}, bf16[4,16,3328]{2,1,0:T(8,128)(2,1)S(1)}, u32[]{:S(2)}, u32[]{:S(2)}) collective-permute-start(bf16[4,16,3328]{2,1,0:T(8,128)(2,1)S(1)} %collective-permute-done.4.refs_5_), channel_id=1, source_target_pairs={{0,1},{1,0},{2,3},{3,2},{4,5},{5,4},{6,7},{7,6},{8,9},{9,8},{10,11... | collective-permute-start | bytes 1277960 | tf_op jit(solution)/shard_map/ppermute | solution.py:696
  39.2 12.4 %collective-permute-start.11 = (bf16[2,16,3328]{2,1,0:T(8,128)(2,1)S(1)}, bf16[2,16,3328]{2,1,0:T(8,128)(2,1)S(1)}, u32[]{:S(2)}, u32[]{:S(2)}) collective-permute-start(bf16[2,16,3328]{2,1,0:T(8,128)(2,1)S(1)} %collective-permute-done.9.refs_10_), channel_id=1, source_target_pairs={{0,1},{1,0},{2,3},{3,2},{4,5},{5,4},{6,7},{7,6},{8,9},{9,8},{10,11... | collective-permute-start | bytes 638984 | tf_op jit(solution)/shard_map/ppermute | solution.py:696
  41.0 10.7 %collective-permute-start.10 = (bf16[2,16,3328]{2,1,0:T(8,128)(2,1)}, bf16[2,16,3328]{2,1,0:T(8,128)(2,1)S(1)}, u32[]{:S(2)}, u32[]{:S(2)}) collective-permute-start(bf16[2,16,3328]{2,1,0:T(8,128)(2,1)} %collective-permute-done.8.refs_9_), channel_id=1, source_target_pairs={{0,1},{1,0},{2,3},{3,2},{4,5},{5,4},{6,7},{7,6},{8,9},{9,8},{10,11... | collective-permute-start | bytes 638984 | tf_op jit(solution)/shard_map/ppermute | solution.py:696
  52.9 37.4 %all-to-all-start = ((bf16[8,256,512]{2,1,0:T(8,128)(2,1)}), bf16[8,256,512]{2,1,0:T(8,128)(2,1)S(1)}, u32[]{:S(2)}, u32[]{:S(2)}) async-start(bf16[8,256,512]{2,1,0:T(8,128)(2,1)} %get-tuple-element.86), calls=%async_computation | async-start | bytes 4194304 | tf_op jit(solution)/shard_map/all_to_all | solution.py:764
  90.4 30.9 %copy-start.3 = (bf16[8,256,512]{2,1,0:T(8,128)(2,1)}, bf16[8,256,512]{2,1,0:T(8,128)(2,1)S(1)}, u32[]{:S(2)}) copy-start(bf16[8,256,512]{2,1,0:T(8,128)(2,1)S(1)} %all-to-all-done) | copy-start | bytes 6291460
  121.3 31.9 %all-to-all-start.2 = ((bf16[8,256,512]{2,1,0:T(8,128)(2,1)}), bf16[8,256,512]{2,1,0:T(8,128)(2,1)S(1)}, u32[]{:S(2)}, u32[]{:S(2)}) async-start(bf16[8,256,512]{2,1,0:T(8,128)(2,1)} %get-tuple-element.88), calls=%async_computation.2 | async-start | bytes 4194304 | tf_op jit(solution)/shard_map/all_to_all | solution.py:764
  154.5 32.5 %all-to-all-start.4 = ((bf16[8,256,512]{2,1,0:T(8,128)(2,1)}), bf16[8,256,512]{2,1,0:T(8,128)(2,1)}, u32[]{:S(2)}, u32[]{:S(2)}) async-start(bf16[8,256,512]{2,1,0:T(8,128)(2,1)} %bitcast.50), calls=%async_computation.4 | async-start | bytes 4194304 | tf_op jit(solution)/shard_map/all_to_all | solution.py:764
  187.1 31.1 %all-to-all-start.3 = ((bf16[8,256,512]{2,1,0:T(8,128)(2,1)}), bf16[8,256,512]{2,1,0:T(8,128)(2,1)S(1)}, u32[]{:S(2)}, u32[]{:S(2)}) async-start(bf16[8,256,512]{2,1,0:T(8,128)(2,1)} %bitcast.49), calls=%async_computation.3 | async-start | bytes 4194304 | tf_op jit(solution)/shard_map/all_to_all | solution.py:764
  249.1 30.2 %all-to-all-start.7 = ((bf16[8,256,512]{2,1,0:T(8,128)(2,1)}), bf16[8,256,512]{2,1,0:T(8,128)(2,1)S(1)}, u32[]{:S(2)}, u32[]{:S(2)}) async-start(bf16[8,256,512]{2,1,0:T(8,128)(2,1)} %get-tuple-element.108), calls=%async_computation.7 | async-start | bytes 4194304 | tf_op jit(solution)/shard_map/all_to_all | solution.py:764
  280.6 47.1 %all-to-all-start.6 = ((bf16[8,256,512]{2,1,0:T(8,128)(2,1)}), bf16[8,256,512]{2,1,0:T(8,128)(2,1)S(1)}, u32[]{:S(2)}, u32[]{:S(2)}) async-start(bf16[8,256,512]{2,1,0:T(8,128)(2,1)} %bitcast.47), calls=%async_computation.6 | async-start | bytes 4194304 | tf_op jit(solution)/shard_map/all_to_all | solution.py:764
  284.2 179.8 %reduce-scatter.2.cloned.1.call-start = ((), (), s32[]{:S(2)}) async-start(), calls=%async_computation.13 | async-start | bytes 5242880 | tf_op jit(solution)/shard_map/reduce_scatter | solution.py:906
  383.0 33.3 %all-to-all-start.10 = ((bf16[8,4,16,1536]{3,2,1,0:T(8,128)(2,1)}), bf16[8,4,16,1536]{3,2,1,0:T(8,128)(2,1)S(1)}, u32[]{:S(2)}, u32[]{:S(2)}) async-start(bf16[8,4,16,1536]{3,2,1,0:T(8,128)(2,1)} %bitcast.32), calls=%async_computation.10 | async-start | bytes 3145728 | tf_op jit(solution)/shard_map/all_to_all | solution.py:764
  416.2 28.0 %all-to-all-start.9 = ((bf16[8,4,16,1792]{3,2,1,0:T(8,128)(2,1)}), bf16[8,4,16,1792]{3,2,1,0:T(8,128)(2,1)S(1)}, u32[]{:S(2)}, u32[]{:S(2)}) async-start(bf16[8,4,16,1792]{3,2,1,0:T(8,128)(2,1)} %bitcast.31), calls=%async_computation.9 | async-start | bytes 3670016 | tf_op jit(solution)/shard_map/all_to_all | solution.py:764
  445.3 16.0 %all-to-all-start.11 = ((bf16[4,16,3328]{2,1,0:T(8,128)(2,1)}), bf16[4,16,3328]{2,1,0:T(8,128)(2,1)S(1)}, u32[]{:S(2)}, u32[]{:S(2)}) async-start(bf16[4,16,3328]{2,1,0:T(8,128)(2,1)} %pad_maximum_fusion.2), calls=%async_computation.11 | async-start | bytes 851968 | tf_op jit(solution)/shard_map/all_to_all | solution.py:961
  (20 other events, 227.6 us)
Sparse Core Ops, SparseCore 0:
  28.0 80.2 all-gather.2
  327.8 79.7 reduce-scatter.1

commit v3 on v2

--- a/solution.py
+++ b/solution.py
@@ -31,17 +31,18 @@
 NT = (((1,), (1,)), ((), ()))
 TN = (((0,), (0,)), ((), ()))
 
-TAIL_P = 0.3
-TAIL = (
-    0.11962930113077164,
-    0.1207539290189743,
-    0.09991367161273956,
-    0.12856101989746094,
-    -0.053682513535022736,
-    0.20635227859020233,
-    -0.15720237791538239,
-    0.03567460551857948,
+ROOT_MAX = 31.36
+ROOT = (
+    0.7978849411010742,
+    0.03633308410644531,
+    -3.259496588725597e-05,
+    -5.530620546778664e-05,
+    3.964748430007603e-06,
+    -1.3226379280695255e-07,
+    1.756186418511163e-09,
 )
+BELL = -0.7213475204444817
+BELL_SCALE = 0.3989422804014327
 
 
 def dot(a, b, dims=NN):
@@ -87,8 +88,9 @@
     return high, (values - high.astype(F32)).astype(BF)
 
 
-def slots_kernel(experts, capacity, meta_ref, cot_ref, rank_ref, rank_t_ref, *slots_refs):
-    tok = cot_ref.shape[0]
+def ranks_kernel(capacity, meta_ref, rank_ref, rank_t_ref, place_ref):
+    tok = meta_ref.shape[0]
+    size = capacity // HALVES
     tri = lax.broadcasted_iota(jnp.int32, (BLOCK, BLOCK), 0) >= lax.broadcasted_iota(
         jnp.int32, (BLOCK, BLOCK), 1
     )
@@ -102,26 +104,46 @@
         ones = jnp.where(pick, 1.0, 0.0)
         count = dot(tri, ones.astype(BF)) + carry
         carry = count[BLOCK - 1 :, :]
-        rank_ref[rows, :] = jnp.where(pick, count - 1.0, -1.0)
-    rank_t_ref[...] = jnp.transpose(rank_ref[...]).astype(jnp.int32)
-
-    gather_slots(experts, capacity, rank_t_ref, cot_ref, slots_refs)
-
-
-def gather_slots(experts, capacity, rank_t_ref, rows_ref, slots_refs):
-    def gather(e, _):
-        for h in range(HALVES):
-            hot = one_hot(rank_t_ref, e, capacity, h)
-            slots_refs[h][e] = dot(hot, rows_ref[...]).astype(BF)
+        rank = jnp.where(pick, count - 1.0, -1.0)
+        rank_ref[rows, :] = rank
+        place = jnp.full((BLOCK, LANES), -1, jnp.int32)
+        for k in range(F_TOP):
+            route = meta[:, 4 + k : 5 + k]
+            mine = jnp.sum(jnp.where(lane == route, rank, 0.0), axis=1, keepdims=True)
+            mine = mine.astype(jnp.int32)
+            for h in range(HALVES):
+                within = mine - h * size
+                dest = jnp.where((within >= 0) & (within < size), route * size + within, -1)
+                place = jnp.where(lane == F_TOP * h + k, dest, place)
+        place_ref[rows, :] = place
+    rank_t_ref[...] = jnp.transpose(rank_ref[...])[: rank_t_ref.shape[0], :].astype(jnp.int32)
+
+
+def gather_kernel(experts, starts, rank_t_ref, rows_ref, *slots_refs):
+    tok = rows_ref.shape[0]
+
+    def gather(pair, _):
+        hots, targets = [], []
+        for e in (2 * pair, 2 * pair + 1):
+            row = rank_t_ref[pl.ds(e, 1), :]
+            for start, slots_ref in zip(starts, slots_refs):
+                size = slots_ref.shape[1]
+                place = lax.broadcasted_iota(jnp.int32, (size, tok), 0) + start
+                hots.append(jnp.where(place == row, 1.0, 0.0).astype(BF))
+                targets.append((slots_ref, e, size))
+        rows = dot(jnp.concatenate(hots, axis=0), rows_ref[...]).astype(BF)
+        at = 0
+        for slots_ref, e, size in targets:
+            slots_ref[e] = rows[at : at + size]
+            at += size
         return 0
 
-    lax.fori_loop(0, experts, gather, 0)
-
-
-def one_hot(rank_t_ref, e, capacity, h):
-    size = capacity // HALVES
-    row = rank_t_ref[pl.ds(e, 1), :] - h * size
-    place = lax.broadcasted_iota(jnp.int32, (size, row.shape[1]), 0)
+    lax.fori_loop(0, experts // 2, gather, 0)
+
+
+def one_hot(rank_t_ref, e, capacity):
+    row = rank_t_ref[pl.ds(e, 1), :]
+    place = lax.broadcasted_iota(jnp.int32, (capacity, row.shape[1]), 0)
     return jnp.where(place == row, 1.0, 0.0).astype(BF)
 
 
@@ -166,12 +188,11 @@
             w_ref[rows, :] = block
 
 
-def attend_kernel(experts, capacity, shape, *refs):
-    tok_ref, meta_ref, rank_t_ref = refs[:3]
-    slots_refs, refs = refs[-3 - HALVES : -3], refs[3 : -3 - HALVES] + refs[-3:]
-    pieces, refs = refs[:-12], refs[-12:]
+def attend_kernel(experts, shape, *refs):
+    tok_ref, meta_ref = refs[:2]
+    pieces, refs = refs[2:-12], refs[-12:]
     w_ref, slotq_ref, kv_ref, so_ref, lse_ref, gates_ref, mixed_ref, hidden_ref, fgate_ref = refs[:9]
-    kx_ref, vx_ref, n2_ref = refs[9:]
+    n2_ref, kx_ref, vx_ref = refs[9:]
     place_pieces(shape, pieces, w_ref)
     tok = tok_ref.shape[0]
     first = A_EXP + experts
@@ -262,75 +283,108 @@
         hat, _ = norm_stats(hidden)
         normed = (hat * gain_two + shift_two).astype(BF)
         n2_ref[rows, :] = normed
-        logits = pltpu.roll(dot(normed, w_ref[:, RV_AT:PACK]), LANES - A_EXP, 1)
-        named = (lane == meta[:, 4:5]) | (lane == meta[:, 5:6])
-        top = jnp.max(jnp.where(named, logits, NEG), axis=1, keepdims=True)
-        raised = jnp.where(named, jnp.exp(jnp.where(named, logits, NEG) - top), 0.0)
-        fgate_ref[rows, :] = raised * (1.0 / jnp.sum(raised, axis=1, keepdims=True))
+        logits = dot(normed, w_ref[:, RV_AT:PACK])
+        first_logit, second_logit = (
+            jnp.sum(
+                jnp.where(lane == meta[:, 4 + k : 5 + k] + A_EXP, logits, 0.0), axis=1, keepdims=True
+            )
+            for k in range(F_TOP)
+        )
+        top = jnp.maximum(first_logit, second_logit)
+        first_raised, second_raised = jnp.exp(first_logit - top), jnp.exp(second_logit - top)
+        scale = 1.0 / (first_raised + second_raised)
+        fgate_ref[rows, :] = jnp.where(lane == 0, first_raised * scale, second_raised * scale)
         return 0
 
     lax.fori_loop(0, tok // BLOCK, finish, 0)
-    gather_slots(experts, capacity, rank_t_ref, n2_ref, slots_refs)
-
-
-def expert_kernel(parts, x_ref, up_ref, down_ref, out_ref, act_ref, slope_ref):
-    rows = x_ref[...]
-
-    def part(c, total):
-        pre = dot(rows, up_ref[c])
-        size = jnp.abs(pre)
-        bell = jnp.exp(pre * pre * -0.5)
-        inv = 1.0 / (1.0 + TAIL_P * size)
-        tail = TAIL[-1] * inv
-        for coef in TAIL[-2::-1]:
-            tail = (tail + coef) * inv
-        tail = tail * bell
-        phi = jnp.where(pre >= 0.0, 1.0 - tail, tail)
+
+
+def expert_kernel(parts, x_ref, up_ref, down_ref, out_ref, act_ref, slope_ref, total_ref):
+    total_ref[...] = jnp.zeros(total_ref.shape, F32)
+
+    def part(c, _):
+        pre = dot(x_ref[...], up_ref[c])
+        square = pre * pre
+        short = jnp.minimum(square, ROOT_MAX)
+        root = ROOT[-1] * short
+        for coef in ROOT[-2:0:-1]:
+            root = (root + coef) * short
+        phi = 0.5 + 0.5 * jnp.tanh(pre * (root + ROOT[0]))
         act = (pre * phi).astype(BF)
         act_ref[c] = act
-        slope_ref[c] = (phi + pre * bell * 0.3989422804014327).astype(BF)
-        return total + dot(act, down_ref[c])
-
-    total = part(0, jnp.zeros(out_ref.shape, F32))
-    for c in range(1, parts):
-        total = part(c, total)
-    out_ref[...] = total.astype(BF)
-
-
-def combine_sums(experts, capacity, h, rank, back_ref, fgate, cot, halt_row, lane, sums):
-    branch, with_cot, with_row = sums
-    size = capacity // HALVES
-    place = lax.broadcasted_iota(jnp.int32, (BLOCK, size), 1) + h * size
-    for e in range(experts):
-        hot = jnp.where(place == rank[:, e : e + 1], 1.0, 0.0).astype(BF)
-        came = dot(hot, back_ref[e])
-        branch = branch + fgate[:, e : e + 1] * came
+        bell = jnp.exp2(square * BELL)
+        slope_ref[c] = (phi + (pre * BELL_SCALE) * bell).astype(BF)
+        total_ref[...] += dot(act, down_ref[c])
+        return 0
+
+    lax.fori_loop(0, parts, part, 0, unroll=2)
+    out_ref[...] = total_ref[...].astype(BF)
+
+
+def combine_sums(h, place, back_ref, fgate, cot, halt_row, lane, branch, cols):
+    slot = lax.broadcasted_iota(jnp.int32, (BLOCK, back_ref.shape[0]), 1)
+    for k in range(F_TOP):
+        at = F_TOP * h + k
+        hot = jnp.where(slot == place[:, at : at + 1], 1.0, 0.0).astype(BF)
+        came = dot(hot, back_ref[...])
+        branch = branch + fgate[:, k : k + 1] * came
         one = jnp.sum(came * cot, axis=1, keepdims=True)
         two = jnp.sum(came * halt_row, axis=1, keepdims=True)
-        with_cot = with_cot + jnp.where(lane == e, one, 0.0)
-        with_row = with_row + jnp.where(lane == e, two, 0.0)
-    return branch, with_cot, with_row
+        cols = cols + jnp.where(lane == k, one, jnp.where(lane == F_TOP + k, two, 0.0))
+    return branch, cols
+
+
+def split_three(values):
+    high = values.astype(BF).astype(F32)
+    middle = (values - high).astype(BF).astype(F32)
+    return high, middle, values - high - middle
 
 
 def combine_first_kernel(
-    experts, capacity, back_ref, rank_ref, tail_ref, fgate_ref, cot_ref, branch_ref, wcot_ref, wrow_ref
+    experts,
+    back_ref,
+    place_ref,
+    tail_ref,
+    meta_ref,
+    fgate_ref,
+    cot_ref,
+    branch_ref,
+    cols_ref,
+    live_ref,
+    dense_ref,
 ):
     halt_row = vector_row(turned_tail(tail_ref[...]), A_EXP + experts, 4)
     lane = lane_ids(BLOCK)
 
     def block(b, _):
         rows = pl.ds(b * BLOCK, BLOCK)
-        rank = rank_ref[rows, :].astype(jnp.int32)
-        cot = cot_ref[rows, :].astype(F32)
-        zero = jnp.zeros((BLOCK, LANES), F32)
-        sums = (jnp.zeros((BLOCK, D), F32), zero, zero)
-        sums = combine_sums(
-            experts, capacity, 0, rank, back_ref, fgate_ref[rows, :], cot, halt_row, lane, sums
+        meta = meta_ref[rows, :]
+        fgate = fgate_ref[rows, :]
+        branch, cols = combine_sums(
+            0,
+            place_ref[rows, :],
+            back_ref,
+            fgate,
+            cot_ref[rows, :].astype(F32),
+            halt_row,
+            lane,
+            jnp.zeros((BLOCK, D), F32),
+            jnp.zeros((BLOCK, LANES), F32),
         )
-        branch_ref[rows, :], wcot_ref[rows, :], wrow_ref[rows, :] = sums
+        branch_ref[rows, :] = branch
+        cols_ref[rows, :] = cols
+        active = jnp.where(meta[:, 6:7] >= STEP, 1.0, 0.0)
+        dense = jnp.zeros((BLOCK, LANES), F32)
+        for k in range(F_TOP):
+            named = lane == meta[:, 4 + k : 5 + k]
+            dense = jnp.where(named, active * fgate[:, k : k + 1], dense)
+        dense_ref[rows, :] = dense
         return 0
 
     lax.fori_loop(0, branch_ref.shape[0] // BLOCK, block, 0)
+    turned = jnp.transpose(dense_ref[...])[: live_ref.shape[1], :]
+    for index, part in enumerate(split_three(turned)):
+        live_ref[index] = part.astype(BF)
 
 
 def combine_kernel(
@@ -338,9 +392,9 @@
     capacity,
     back_ref,
     branch_ref,
-    wcot_ref,
-    wrow_ref,
-    rank_ref,
+    cols_ref,
+    live_ref,
+    place_ref,
     rank_t_ref,
     hidden_ref,
     tail_ref,
@@ -353,73 +407,83 @@
     slope_ref,
     glf_ref,
     row_ref,
-    *rest,
+    ab_ref,
+    kept_ref,
 ):
-    ab_refs, cols_ref = rest[:HALVES], rest[HALVES]
-    tok = hidden_ref.shape[0]
+    step = pl.program_id(0)
     halt_row = vector_row(turned_tail(tail_ref[...]), A_EXP + experts, 4)
     lane = lane_ids(BLOCK)
-    row_ref[...] = jnp.zeros(row_ref.shape, F32)
-
-    def block(b, _):
-        rows = pl.ds(b * BLOCK, BLOCK)
-        meta = meta_ref[rows, :]
-        rank = rank_ref[rows, :].astype(jnp.int32)
-        fgate = fgate_ref[rows, :]
-        scal = scal_ref[rows, :]
-        active = jnp.where(meta[:, 6:7] >= STEP, 1.0, 0.0)
-        cot = cot_ref[rows, :].astype(F32)
-        sums = (branch_ref[rows, :], wcot_ref[rows, :], wrow_ref[rows, :])
-        branch, with_cot, with_row = combine_sums(
-            experts, capacity, 1, rank, back_ref, fgate, cot, halt_row, lane, sums
-        )
-        z = hidden_ref[rows, :] + active * branch
-        out_ref[rows, :] = z.astype(BF)
-        prob = 1.0 / (1.0 + jnp.exp(-jnp.sum(z * halt_row, axis=1, keepdims=True)))
-        halt_in, cot_halt = scal[:, 0:1], scal[:, 1:2]
-        room = active * (1.0 - halt_in) * prob
-        slope = cot_halt * room * (1.0 - prob)
-        halt_ref[rows, :] = jnp.broadcast_to(halt_in + room, (BLOCK, LANES))
-        slope_ref[rows, :] = jnp.broadcast_to(slope, (BLOCK, LANES))
-        row_ref[0:1, :] += jnp.sum(slope * z, axis=0, keepdims=True)
-        gfg = active * (with_cot + slope * with_row)
-        inner = jnp.sum(fgate * gfg, axis=1, keepdims=True)
-        glf_ref[rows, :] = pltpu.roll(fgate * (gfg - inner), A_EXP, 1)
-        live = active * fgate
-        bent = live * slope
-        for index, part in enumerate((live, bent)):
-            high = part.astype(BF)
-            rest = part - high.astype(F32)
-            middle = rest.astype(BF)
-            cols_ref[3 * index, rows, :] = high
-            cols_ref[3 * index + 1, rows, :] = middle
-            cols_ref[3 * index + 2, rows, :] = (rest - middle.astype(F32)).astype(BF)
-        return 0
-
-    lax.fori_loop(0, tok // BLOCK, block, 0)
-    turned = [jnp.transpose(cols_ref[i].astype(F32)) for i in range(6)]
-    for e in range(experts):
-        rows = jnp.concatenate(
-            [t[e : e + 1, :] for t in turned] + [jnp.zeros((2, tok), F32)], axis=0
-        ).astype(BF)
-        for h in range(HALVES):
-            ab_refs[h][e] = dot(rows, one_hot(rank_t_ref, e, capacity, h), NT).astype(BF)
-
-
-def data_back_kernel(
-    experts, parts, cot_ref, ab_ref, tail_ref, slope_ref, up_ref, down_ref, gpre_ref, gy_ref, rows_ref
-):
-    rows = cot_ref.shape[0]
+
+    @pl.when(step == 0)
+    def _():
+        row_ref[...] = jnp.zeros(row_ref.shape, F32)
+
+    meta = meta_ref[...]
+    fgate = fgate_ref[...]
+    scal = scal_ref[...]
+    active = jnp.where(meta[:, 6:7] >= STEP, 1.0, 0.0)
+    branch, cols = combine_sums(
+        1,
+        place_ref[...],
+        back_ref,
+        fgate,
+        cot_ref[...].astype(F32),
+        halt_row,
+        lane,
+        branch_ref[...],
+        cols_ref[...],
+    )
+    z = hidden_ref[...] + active * branch
+    out_ref[...] = z.astype(BF)
+    prob = 1.0 / (1.0 + jnp.exp(-jnp.sum(z * halt_row, axis=1, keepdims=True)))
+    halt_in, cot_halt = scal[:, 0:1], scal[:, 1:2]
+    room = active * (1.0 - halt_in) * prob
+    slope = cot_halt * room * (1.0 - prob)
+    halt_ref[...] = jnp.broadcast_to(halt_in + room, (BLOCK, LANES))
+    wide_slope = jnp.broadcast_to(slope, (BLOCK, LANES))
+    slope_ref[...] = wide_slope
+    kept_ref[pl.ds(step * BLOCK, BLOCK), :] = wide_slope
+    row_ref[0:1, :] += jnp.sum(slope * z, axis=0, keepdims=True)
+    gfg = [active * (cols[:, k : k + 1] + slope * cols[:, 2 + k : 3 + k]) for k in range(F_TOP)]
+    inner = fgate[:, 0:1] * gfg[0] + fgate[:, 1:2] * gfg[1]
+    glf = jnp.zeros((BLOCK, LANES), F32)
+    for k in range(F_TOP):
+        value = fgate[:, k : k + 1] * (gfg[k] - inner)
+        glf = jnp.where(lane == meta[:, 4 + k : 5 + k] + A_EXP, value, glf)
+    glf_ref[...] = glf
+
+    @pl.when(step == pl.num_programs(0) - 1)
+    def _():
+        slopes = [part[:1, :] for part in split_three(jnp.transpose(kept_ref[...]))]
+        low = [live_ref[i].astype(F32) for i in range(3)]
+        tok = kept_ref.shape[0]
+        for e in range(experts):
+            rows = [part[e : e + 1, :] for part in low] + slopes + [jnp.zeros((2, tok), F32)]
+            rows = jnp.concatenate(rows, axis=0).astype(BF)
+            ab_ref[e] = dot(rows, one_hot(rank_t_ref, e, capacity), NT).astype(BF)
+
+
+def data_back_kernel(experts, parts, h, *refs):
+    cot_refs, refs = refs[:-8], refs[-8:]
+    ab_ref, tail_ref, slope_ref, up_ref, down_ref, gpre_ref, gy_ref, rows_ref = refs
+    size = ab_ref.shape[2] // HALVES
+    count = ab_ref.shape[0]
+    rows = count * size
     halt_row = vector_row(turned_tail(tail_ref[...]), A_EXP + experts, 4)
     cols = []
-    for i in range(ab_ref.shape[0]):
-        ab = ab_ref[i].astype(F32)
+    cots = []
+    for i in range(count):
+        ab = ab_ref[i].astype(F32)[:, h * size : (h + 1) * size]
         live = ab[0:1, :] + ab[1:2, :] + ab[2:3, :]
-        bent = ab[3:4, :] + ab[4:5, :] + ab[5:6, :]
-        filler = jnp.zeros((LANES - 2, ab.shape[1]), F32)
-        cols.append(jnp.transpose(jnp.concatenate([live, bent, filler], axis=0)))
+        slope = ab[3:4, :] + ab[4:5, :] + ab[5:6, :]
+        filler = jnp.zeros((LANES - 2, size), F32)
+        cols.append(jnp.transpose(jnp.concatenate([live, slope, filler], axis=0)))
+        for ref in cot_refs:
+            part = ref.shape[0] // count
+            cots.append(ref[i * part : (i + 1) * part, :].astype(F32))
     cols = jnp.concatenate(cols, axis=0)
-    gy = (cols[:, 0:1] * cot_ref[...].astype(F32) + cols[:, 1:2] * halt_row).astype(BF)
+    cots = jnp.concatenate(cots, axis=0)
+    gy = (cols[:, 0:1] * (cots + cols[:, 1:2] * halt_row)).astype(BF)
     gy_ref[...] = gy
     total = jnp.zeros((rows, D), F32)
     for c in range(parts):
@@ -458,6 +522,18 @@
                 refs[-3][c] = jnp.transpose(down_acc[c]).astype(BF)
 
 
+def store_grads(ref, values, start):
+    columns = slice(start, start + values.shape[1])
+    if len(ref.shape) == 2:
+        ref[:, columns] = values
+        return
+    experts, groups, shard, _ = ref.shape
+    for e in range(experts):
+        for g in range(groups):
+            at = (g * experts + e) * shard
+            ref[e, g, :, columns] = values[at : at + shard]
+
+
 def hidden_back_kernel(
     experts,
     capacity,
@@ -466,6 +542,7 @@
     rank_ref,
     hidden_ref,
     w_ref,
+    tail_ref,
     meta_ref,
     cot_ref,
     slope_ref,
@@ -481,64 +558,65 @@
     vec_ref,
     acc_ref,
 ):
-    tok = hidden_ref.shape[0]
+    step = pl.program_id(0)
     first = A_EXP + experts
     size = capacity // HALVES
-    rows_t = transposed_tail(w_ref)
+    rows_t = turned_tail(tail_ref[...])
     low_t = rows_t.astype(BF)
     gain_two, shift_two, halt_row = (vector_row(rows_t, first, i) for i in (2, 3, 4))
     lane = lane_ids(BLOCK)
     upper = lane >= HEAD
     lane_half = jnp.where(upper, 1, 0)
-    vec_ref[...] = jnp.zeros(vec_ref.shape, F32)
-    acc_ref[...] = jnp.zeros(acc_ref.shape, F32)
-    rv_ref[...] = jnp.zeros(rv_ref.shape, F32)
-
-    def block(b, _):
-        rows = pl.ds(b * BLOCK, BLOCK)
-        meta = meta_ref[rows, :]
-        rank = rank_ref[rows, :].astype(jnp.int32)
-        active = jnp.where(meta[:, 6:7] >= STEP, 1.0, 0.0)
-        place = lax.broadcasted_iota(jnp.int32, (BLOCK, size), 1)
-        glf_high, glf_low = split_two(glf_ref[rows, :])
-        grad = dot(glf_high, low_t) + dot(glf_low, low_t)
-        for h, back_ref in enumerate((first_ref, second_ref)):
-            for e in range(experts):
-                hot = jnp.where(place + h * size == rank[:, e : e + 1], 1.0, 0.0).astype(BF)
-                grad = grad + dot(hot, back_ref[e])
-        hat, inv = norm_stats(hidden_ref[rows, :])
-        normed = (hat * gain_two + shift_two).astype(BF)
-        rv_ref[...] += dot(normed, glf_high, TN) + dot(normed, glf_low, TN)
-        vec_ref[2:3, :] += jnp.sum(grad * hat, axis=0, keepdims=True)
-        vec_ref[3:4, :] += jnp.sum(grad, axis=0, keepdims=True)
-        gz = cot_ref[rows, :].astype(F32) + slope_ref[rows, 0:1] * halt_row
-        gh = gz + norm_back(grad, hat, inv, gain_two)
-        gh_ref[rows, :] = gh
-        ga = (active * gh).astype(BF)
-        acc_ref[...] += dot(ga, mixed_ref[rows, :], TN)
-        gm = dot(ga, w_ref[:, WIDTH:KV_AT])
-        gates = gates_ref[rows, :]
-        weighted = jnp.zeros((BLOCK, 1), F32)
-        grads = []
-        picked = [select_heads(gm, meta[:, k : k + 1], lane_half) for k in range(A_TOP)]
-        for j in range(A_TOP // 2):
-            both = jnp.where(upper, picked[2 * j + 1], picked[2 * j])
-            prod = both * so_ref[j, rows, :]
-            scale = jnp.where(upper, gates[:, 2 * j + 1 : 2 * j + 2], gates[:, 2 * j : 2 * j + 1])
-            gslot_ref[j, rows, :] = (both * scale).astype(BF)
-            grads.append(jnp.sum(jnp.where(upper, 0.0, prod), axis=1, keepdims=True))
-            grads.append(jnp.sum(jnp.where(upper, prod, 0.0), axis=1, keepdims=True))
-        for k in range(A_TOP):
-            weighted = weighted + gates[:, k : k + 1] * grads[k]
-        gla = jnp.zeros((BLOCK, LANES), F32)
-        for k in range(A_TOP):
-            value = gates[:, k : k + 1] * (grads[k] - weighted)
-            gla = jnp.where(lane == meta[:, k : k + 1], value, gla)
-        gla_ref[rows, :] = gla
-        return 0
-
-    lax.fori_loop(0, tok // BLOCK, block, 0)
-    gout_ref[...] = acc_ref[...].astype(BF)
+
+    @pl.when(step == 0)
+    def _():
+        vec_ref[...] = jnp.zeros(vec_ref.shape, F32)
+        acc_ref[...] = jnp.zeros(acc_ref.shape, F32)
+        rv_ref[...] = jnp.zeros(rv_ref.shape, F32)
+
+    meta = meta_ref[...]
+    rank = rank_ref[...].astype(jnp.int32)
+    active = jnp.where(meta[:, 6:7] >= STEP, 1.0, 0.0)
+    place = lax.broadcasted_iota(jnp.int32, (BLOCK, size), 1)
+    glf_high, glf_low = split_two(glf_ref[...])
+    grad = dot(glf_high, low_t) + dot(glf_low, low_t)
+    for h, back_ref in enumerate((first_ref, second_ref)):
+        for e in range(experts):
+            hot = jnp.where(place + h * size == rank[:, e : e + 1], 1.0, 0.0).astype(BF)
+            grad = grad + dot(hot, back_ref[e])
+    hat, inv = norm_stats(hidden_ref[...])
+    normed = (hat * gain_two + shift_two).astype(BF)
+    rv_ref[...] += dot(normed, glf_high, TN) + dot(normed, glf_low, TN)
+    vec_ref[2:3, :] += jnp.sum(grad * hat, axis=0, keepdims=True)
+    vec_ref[3:4, :] += jnp.sum(grad, axis=0, keepdims=True)
+    gz = cot_ref[...].astype(F32) + slope_ref[:, 0:1] * halt_row
+    gh = gz + norm_back(grad, hat, inv, gain_two)
+    gh_ref[...] = gh
+    ga = (active * gh).astype(BF)
+    acc_ref[...] += dot(ga, mixed_ref[...], TN)
+    gm = dot(ga, w_ref[...])
+    gates = gates_ref[...]
+    weighted = jnp.zeros((BLOCK, 1), F32)
+    grads = []
+    picked = [select_heads(gm, meta[:, k : k + 1], lane_half) for k in range(A_TOP)]
+    for j in range(A_TOP // 2):
+        both = jnp.where(upper, picked[2 * j + 1], picked[2 * j])
+        prod = both * so_ref[j]
+        scale = jnp.where(upper, gates[:, 2 * j + 1 : 2 * j + 2], gates[:, 2 * j : 2 * j + 1])
+        gslot_ref[j] = (both * scale).astype(BF)
+        grads.append(jnp.sum(jnp.where(upper, 0.0, prod), axis=1, keepdims=True))
+        grads.append(jnp.sum(jnp.where(upper, prod, 0.0), axis=1, keepdims=True))
+    for k in range(A_TOP):
+        weighted = weighted + gates[:, k : k + 1] * grads[k]
+    gla = jnp.zeros((BLOCK, LANES), F32)
+    for k in range(A_TOP):
+        value = gates[:, k : k + 1] * (grads[k] - weighted)
+        gla = jnp.where(lane == meta[:, k : k + 1], value, gla)
+    gla_ref[...] = gla
+
+    @pl.when(step == pl.num_programs(0) - 1)
+    def _():
+        store_grads(gout_ref, acc_ref[...].astype(BF), 0)
 
 
 def input_back_kernel(
@@ -646,11 +724,11 @@
         return gkv_sum + dot(normed, gkv, TN)
 
     gkv_sum = lax.fori_loop(0, blocks, input_back, jnp.zeros((D, LANES), F32))
-    pack_ref[:, :WIDTH] = acc_ref[...].astype(BF)
-    pack_ref[:, WIDTH : WIDTH + LANES] = gkv_sum.astype(BF)
+    store_grads(pack_ref, acc_ref[...].astype(BF), 0)
+    store_grads(pack_ref, gkv_sum.astype(BF), WIDTH)
     turned = pltpu.roll(jnp.transpose(vec_ref[...]), first, 1)
     tail = jnp.where(lane_ids(D) < first, rv_ref[...], turned)
-    pack_ref[:, WIDTH + LANES :] = tail.astype(BF)
+    store_grads(pack_ref, tail.astype(BF), WIDTH + LANES)
 
 
 VMEM_LIMIT = 60 * 1024 * 1024
@@ -695,7 +773,8 @@
     def swap(values, m):
         return lax.ppermute(values, "fsdp", [(i, i ^ m) for i in range(experts)])
 
-    along, across = swap(own, 2), swap(own, 4)
+    along = swap(own, 2)
+    across = swap(own, 4)
     low = swap(along[: groups // 2], 4)
     high = swap(across[groups // 2 :], 2)
     return [
@@ -752,23 +831,30 @@
     scal = jnp.stack([halt_in, cot_halt], axis=1)
     half = capacity // HALVES
     half_slots = slots // HALVES
-    slot_shape = whole((experts, half, D), BF)
-
-    rank, rank_t, *cot_slots = call(
-        partial(slots_kernel, experts, capacity),
-        (meta, cot_out),
-        (whole((tok, LANES), F32), whole((LANES, tok), jnp.int32)) + (slot_shape,) * HALVES,
+
+    rank, rank_t, place = call(
+        partial(ranks_kernel, capacity),
+        (meta,),
+        (whole((tok, LANES), F32), whole((experts, tok), jnp.int32), whole((tok, LANES), jnp.int32)),
     )
 
+    def gather_rows(rows, starts):
+        ends = starts[1:] + (capacity if len(starts) > 1 else starts[0] + half,)
+        shapes = [whole((experts, end - start, D), BF) for start, end in zip(starts, ends)]
+        return call(partial(gather_kernel, experts, starts), (rank_t, rows), shapes)
+
+    cot_slots = gather_rows(cot_out, (0, half, half + half // 2))
+
     def exchange(values):
-        return lax.all_to_all(values, "fsdp", split_axis=0, concat_axis=0, tiled=True)
-
-    *pieces, cot_first = lax.optimization_barrier((*pieces, cot_slots[0]))
+        came = lax.all_to_all(values, "fsdp", split_axis=0, concat_axis=0, tiled=True)
+        return came
+
+    *pieces, cot_first, scal = lax.optimization_barrier((*pieces, cot_slots[0], scal))
     owned_cot = [exchange(cot_first)]
 
-    weights, slotq, kv, so, lse, gates, mixed, hidden, fgate, *n2_slots = call(
-        partial(attend_kernel, experts, capacity, shape),
-        (tokens, meta, rank_t, *pieces),
+    weights, slotq, kv, so, lse, gates, mixed, hidden, fgate, normed_two = call(
+        partial(attend_kernel, experts, shape),
+        (tokens, meta, *pieces),
         (
             whole((D, PACK), BF),
             whole((2, tok, LANES), BF),
@@ -779,14 +865,11 @@
             whole((tok, WIDTH), BF),
             whole((tok, D), F32),
             whole((tok, LANES), F32),
-        )
-        + (slot_shape,) * HALVES,
-        (
-            pltpu.VMEM((2, tok, LANES), BF),
-            pltpu.VMEM((2, tok, LANES), BF),
-            pltpu.VMEM((tok, D), BF),
+            whole((tok, D), BF),
         ),
+        (pltpu.VMEM((2, tok, LANES), BF), pltpu.VMEM((2, tok, LANES), BF)),
     )
+    n2_slots = [gather_rows(normed_two, (h * half,))[0] for h in range(HALVES)]
     n2_slots[0], owned_cot[0] = lax.optimization_barrier((n2_slots[0], owned_cot[0]))
 
     up_spec = constant_spec((groups, D, slice_width))
@@ -811,47 +894,74 @@
             out_shape=(narrow, wide, wide),
             in_specs=[step_spec, up_spec, down_spec],
             out_specs=[step_spec, step_wide, step_wide],
+            scratch_shapes=[pltpu.VMEM((step_rows, D), F32)],
             compiler_params=params,
         )(owned[h], whole_up, whole_down)
         outs.append(out)
         acts.append(act)
         slopes.append(slope)
-    back = [exchange(out.reshape(experts, half, D)) for out in outs]
+    back = []
+    for h in range(HALVES):
+        back.append(exchange(outs[h].reshape(experts, half, D)).reshape(half_slots, D))
 
     tail_spec = pl.BlockSpec((D, LANES), lambda s: (0, RV_AT // LANES))
     full = pl.BlockSpec(memory_space=pltpu.VMEM)
     sums = pl.pallas_call(
-        partial(combine_first_kernel, experts, capacity),
+        partial(combine_first_kernel, experts),
         name="combine_first",
         grid=(1,),
-        out_shape=(whole((tok, D), F32), whole((tok, LANES), F32), whole((tok, LANES), F32)),
-        in_specs=[full, full, tail_spec, full, full],
+        out_shape=(
+            whole((tok, D), F32),
+            whole((tok, LANES), F32),
+            whole((3, max(16, experts), tok), BF),
+        ),
+        in_specs=[full, full, tail_spec, full, full, full],
         out_specs=[full] * 3,
+        scratch_shapes=[pltpu.VMEM((tok, LANES), F32)],
         compiler_params=params,
-    )(back[0], rank, weights, fgate, cot_out)
+    )(back[0], place, weights, meta, fgate, cot_out)
     back[1], cot_second = lax.optimization_barrier((back[1], cot_slots[1]))
     owned_cot.append(exchange(cot_second))
-    ab_shape = whole((experts, 8, half), BF)
-    block_out, halt_wide, halt_slope, glf, halt_grad, *ab = pl.pallas_call(
+
+    def tokens_of(width):
+        return pl.BlockSpec((BLOCK, width), lambda b: (b, 0))
+
+    block_out, halt_wide, halt_slope, glf, halt_grad, ab = pl.pallas_call(
         partial(combine_kernel, experts, capacity),
         name="combine",
-        grid=(1,),
+        grid=(tok // BLOCK,),
         out_shape=(
             whole((tok, D), BF),
             whole((tok, LANES), F32),
             whole((tok, LANES), F32),
             whole((tok, LANES), F32),
             whole((8, D), F32),
-        )
-        + (ab_shape,) * HALVES,
-        in_specs=[full] * 7 + [tail_spec] + [full] * 4,
-        out_specs=[full] * (5 + HALVES),
-        scratch_shapes=[pltpu.VMEM((6, tok, LANES), BF)],
+            whole((experts, 8, capacity), BF),
+        ),
+        in_specs=[
+            full,
+            tokens_of(D),
+            tokens_of(LANES),
+            full,
+            tokens_of(LANES),
+            full,
+            tokens_of(D),
+            tail_spec,
+            tokens_of(meta.shape[1]),
+            tokens_of(LANES),
+            tokens_of(2),
+            tokens_of(D),
+        ],
+        out_specs=[tokens_of(D)] + [tokens_of(LANES)] * 3 + [full] * 2,
+        scratch_shapes=[pltpu.VMEM((tok, LANES), F32)],
         compiler_params=params,
-    )(back[1], *sums, rank, rank_t, hidden, weights, meta, fgate, scal, cot_out)
+    )(back[1], *sums, place, rank_t, hidden, weights, meta, fgate, scal, cot_out)
     halt_out = halt_wide[:, 0]
-    owned_ab = exchange(jnp.concatenate(ab, axis=1))
-    owned_ab = [owned_ab[:, 8 * h : 8 * h + 8] for h in range(HALVES)]
+    ab, owned_cot[1] = lax.optimization_barrier((ab, owned_cot[1]))
+    owned_ab = exchange(ab)
+    owned_ab, cot_third = lax.optimization_barrier((owned_ab, cot_slots[2]))
+    owned_cot.append(exchange(cot_third))
+    cot_parts = [owned_cot[:1], owned_cot[1:]]
 
     together = step_rows // half if half % LANES == 0 else 1
     row_spec = pl.BlockSpec((together * half, D), lambda s: (s, 0))
@@ -859,12 +969,12 @@
     gys, gpres, rows_back = [], [], []
     for h in range(HALVES):
         gpre, gy, owned_rows = pl.pallas_call(
-            partial(data_back_kernel, experts, groups),
+            partial(data_back_kernel, experts, groups, h),
             grid=(experts // together,),
             out_shape=(wide, narrow, narrow),
             in_specs=[
-                row_spec,
-                pl.BlockSpec((together, 8, half), lambda s: (s, 0, 0)),
+                *(pl.BlockSpec((together * part.shape[1], D), lambda s: (s, 0)) for part in cot_parts[h]),
+                pl.BlockSpec((together, 8, capacity), lambda s: (s, 0, 0)),
                 tail_spec,
                 wide_spec,
                 up_spec,
@@ -872,7 +982,14 @@
             ],
             out_specs=[wide_spec, row_spec, row_spec],
             compiler_params=params,
-        )(owned_cot[h].reshape(half_slots, D), owned_ab[h], weights, slopes[h], whole_up, whole_down)
+        )(
+            *(part.reshape(-1, D) for part in cot_parts[h]),
+            owned_ab,
+            weights,
+            slopes[h],
+            whole_up,
+            whole_down,
+        )
         gys.append(gy)
         gpres.append(gpre)
         rows_back.append(exchange(owned_rows.reshape(experts, half, D)))
@@ -910,41 +1027,67 @@
     else:
         part_up, part_down = expert_grads
 
-    grad_out, gh, gslot, gla, rv, vec = call(
+    ordered = shard % 16 == 0
+
+    def grads_shape(width):
+        return whole((experts, groups, shard, width) if ordered else (D, width), BF)
+
+    pair_spec = pl.BlockSpec((2, BLOCK, LANES), lambda b: (0, b, 0))
+    grad_out, gh, gslot, gla, rv, vec = pl.pallas_call(
         partial(hidden_back_kernel, experts, capacity),
-        (
-            *rows_back,
-            rank,
-            hidden,
-            weights,
-            meta,
-            cot_out,
-            halt_slope,
-            glf,
-            mixed,
-            so,
-            gates,
-        ),
-        (
-            whole((D, WIDTH), BF),
+        name="hidden_back",
+        grid=(tok // BLOCK,),
+        out_shape=(
+            grads_shape(WIDTH),
             whole((tok, D), F32),
             whole((2, tok, LANES), BF),
             whole((tok, LANES), F32),
             whole((D, LANES), F32),
             whole((8, D), F32),
         ),
-        (pltpu.VMEM((D, WIDTH), F32),),
+        in_specs=[
+            full,
+            full,
+            tokens_of(LANES),
+            tokens_of(D),
+            pl.BlockSpec((D, WIDTH), lambda b: (0, 1), pipeline_mode=pl.Buffered(1)),
+            tail_spec,
+            tokens_of(meta.shape[1]),
+            tokens_of(D),
+            tokens_of(LANES),
+            tokens_of(LANES),
+            tokens_of(WIDTH),
+            pair_spec,
+            tokens_of(LANES),
+        ],
+        out_specs=[full, tokens_of(D), pair_spec, tokens_of(LANES), full, full],
+        scratch_shapes=[pltpu.VMEM((D, WIDTH), F32)],
+        compiler_params=params,
+    )(
+        *rows_back,
+        rank,
+        hidden,
+        weights,
+        weights,
+        meta,
+        cot_out,
+        halt_slope,
+        glf,
+        mixed,
+        so,
+        gates,
     )
 
-    def reduced(grads):
-        sent = grads.reshape(groups, experts, shard, grads.shape[1]).transpose(1, 0, 2, 3)
+    def reduced(sent):
+        if not ordered:
+            sent = sent.reshape(groups, experts, shard, sent.shape[1]).transpose(1, 0, 2, 3)
         return jnp.sum(exchange(sent).astype(F32), axis=0).astype(BF)
 
     part_out = reduced(grad_out)
     grad_in, grads = call(
         partial(input_back_kernel, experts),
         (tokens, weights, meta, gh, gslot, gla, rv, vec, halt_grad, lse, slotq, kv),
-        (whole((tok, D), BF), whole((D, WIDTH + 2 * LANES), BF)),
+        (whole((tok, D), BF), grads_shape(WIDTH + 2 * LANES)),
         (
             pltpu.VMEM((2, 2, tok, LANES), F32),
             pltpu.VMEM((BLOCK, WIDTH), BF),

time: 483 us -> 502 us (1.039)
  the two profiles are of different devices: /device:TPU:0 before, /device:TPU:2 now
where the time goes in v3:
time: 502 us; the launch traced here: 492 us
  Pallas kernels  234 us (47%)
  waiting for transfers between devices  122 us (24%)
  starting transfers between devices  61.9 us (12%)
  blocking collectives  37.7 us (8%)
  local copies, waits for them, and re-layouts  15.2 us (3%)
  between operations  14.8 us (3%)
  other arithmetic  5.97 us (1%)
    all_to_all x10, waiting for transfers between devices, exchange(): lax.all_to_all(values, 'fsdp', split_axis=0, concat_axis=0, tiled=True)  91.5 us
    pallas_call x6, Pallas kernels, call(): pl.pallas_call(kernel, out_shape=outs, in_specs=in_vmem(len(inputs)), out...  76.7 us
    pallas_call x2, Pallas kernels, on_device(): pl.pallas_call(partial(expert_kernel, groups), grid=(half_slots // step_r...  52.9 us
    all_to_all x10, starting transfers between devices, exchange(): lax.all_to_all(values, 'fsdp', split_axis=0, concat_axis=0, tiled=True)  47.2 us
    all_to_all x2, blocking collectives, exchange(): lax.all_to_all(values, 'fsdp', split_axis=0, concat_axis=0, tiled=True)  37.7 us
    pallas_call x2, Pallas kernels, on_device(): pl.pallas_call(partial(data_back_kernel, experts, groups, h), grid=(exper...  31.6 us
    pallas_call x1, Pallas kernels, on_device(): pl.pallas_call(partial(weight_back_kernel, groups, steps, joined), name='...  27.2 us
    pallas_call x1, Pallas kernels, on_device(): pl.pallas_call(partial(hidden_back_kernel, experts, capacity), name='hidd...  19.9 us
  transfers between devices with their start and end apart: 25, of which 10 were waited for; matrix products, arithmetic and copies ran while one was open for 2% of the time, Pallas kernels for 42%

profile of v3, /device:TPU:2, one launch (start us, length us, event | category | flops | bytes accessed | tf_op | source)
XLA Modules:
  0.0 491.7 jit_solution(14636304847049485045)
XLA Ops:
  14.3 6.7 %collective-permute-done.1 = bf16[16,3328]{1,0:T(8,128)(2,1)S(1)} collective-permute-done((bf16[16,3328]{1,0:T(8,128)(2,1)S(1)}, bf16[16,3328]{1,0:T(8,128)(2,1)S(1)}, u32[]{:S(2)}, u32[]{:S(2)}) %collective-permute-start.1) | collective-permute-done | bytes 106528 | tf_op jit(solution)/shard_map/ppermute | solution.py:770
  25.5 6.4 %collective-permute-done.6.refs_6_ = bf16[4,16,3328]{2,1,0:T(8,128)(2,1)S(1)} collective-permute-done((bf16[4,16,3328]{2,1,0:T(8,128)(2,1)S(1)}, bf16[4,16,3328]{2,1,0:T(8,128)(2,1)S(1)}, u32[]{:S(2)}, u32[]{:S(2)}) %collective-permute-start.6) | collective-permute-done | bytes 426016 | tf_op jit(solution)/shard_map/ppermute | solution.py:774
  45.3 8.2 %shard_map.214 = (bf16[8,256,512]{2,1,0:T(8,128)(2,1)}, bf16[8,128,512]{2,1,0:T(8,128)(2,1)}, bf16[8,128,512]{2,1,0:T(8,128)(2,1)}) custom-call(s32[8,1024]{1,0:T(8,128)} %get-tuple-element.77.rank_t_ref, bf16[1024,512]{1,0:T(8,128)(2,1)} %cot_ref.5), custom_call_target="tpu_custom_call" | custom-call | tf_op jit(solution)/shard_map/pallas_call | solution.py:746
  58.7 26.5 %shard_map.215 = (bf16[512,3328]{1,0:T(8,128)(2,1)}, bf16[2,1024,128]{2,1,0:T(8,128)(2,1)}, bf16[1024,128]{1,0:T(8,128)(2,1)}, f32[2,1024,128]{2,1,0:T(8,128)}, ...) custom-call(bf16[1024,512]{1,0:T(8,128)(2,1)} %tok_ref.1, ...), custom_call_target="tpu_custom_call" | custom-call | tf_op jit(solution)/shard_map/pallas_call | solution.py:746
  85.2 5.4 %shard_map.217 = bf16[8,256,512]{2,1,0:T(8,128)(2,1)} custom-call(s32[8,1024]{1,0:T(8,128)} %get-tuple-element.77.rank_t_ref, bf16[1024,512]{1,0:T(8,128)(2,1)} %get-tuple-element.89.rows_ref), custom_call_target="tpu_custom_call" | custom-call | tf_op jit(solution)/shard_map/pallas_call | solution.py:746
  96.2 5.4 %shard_map.216 = bf16[8,256,512]{2,1,0:T(8,128)(2,1)} custom-call(s32[8,1024]{1,0:T(8,128)} %get-tuple-element.77.rank_t_ref, bf16[1024,512]{1,0:T(8,128)(2,1)} %get-tuple-element.89.rows_ref), custom_call_target="tpu_custom_call" | custom-call | tf_op jit(solution)/shard_map/pallas_call | solution.py:746
  101.6 19.7 %all-to-all-done.1 = bf16[8,256,512]{2,1,0:T(8,128)(2,1)S(1)} async-done(((bf16[8,256,512]{2,1,0:T(8,128)(2,1)}), bf16[8,256,512]{2,1,0:T(8,128)(2,1)S(1)}, u32[]{:S(2)}, u32[]{:S(2)}) %all-to-all-start.1) | async-done | bytes 2097184 | tf_op jit(solution)/shard_map/all_to_all | solution.py:849
  122.6 5.9 %all-to-all-start.2 = ((bf16[8,256,512]{2,1,0:T(8,128)(2,1)}), bf16[8,256,512]{2,1,0:T(8,128)(2,1)}, u32[]{:S(2)}, u32[]{:S(2)}) async-start(bf16[8,256,512]{2,1,0:T(8,128)(2,1)} %shard_map.216), calls=%async_computation.2 | async-start | bytes 4194304 | tf_op jit(solution)/shard_map/all_to_all | solution.py:849
  128.5 25.2 %all-to-all-done.2 = bf16[8,256,512]{2,1,0:T(8,128)(2,1)} async-done(((bf16[8,256,512]{2,1,0:T(8,128)(2,1)}), bf16[8,256,512]{2,1,0:T(8,128)(2,1)}, u32[]{:S(2)}, u32[]{:S(2)}) %all-to-all-start.2) | async-done | bytes 2097184 | tf_op jit(solution)/shard_map/all_to_all | solution.py:849
  153.8 26.5 %shard_map.218 = (bf16[2048,512]{1,0:T(8,128)(2,1)}, bf16[4,2048,512]{2,1,0:T(8,128)(2,1)}, bf16[4,2048,512]{2,1,0:T(8,128)(2,1)}) custom-call(bf16[2048,512]{1,0:T(8,128)(2,1)} %bitcast.10.x_ref.refs_4_, bf16[4,1024,512]{2,1,0:T(8,128)(2,1)} %bitcast.28, bf16[4,1024,512]{2,1,0:T(8,128)(2,1)} %bitcast.29), custom_call_target="tpu_custom_call" | custom-call | tf_op jit(solution)/shard_map/pallas_call | solution.py:891
  185.3 26.4 %shard_map.219 = (bf16[2048,512]{1,0:T(8,128)(2,1)}, bf16[4,2048,512]{2,1,0:T(8,128)(2,1)}, bf16[4,2048,512]{2,1,0:T(8,128)(2,1)}) custom-call(bf16[2048,512]{1,0:T(8,128)(2,1)} %bitcast.36, bf16[4,1024,512]{2,1,0:T(8,128)(2,1)} %bitcast.30, bf16[4,1024,512]{2,1,0:T(8,128)(2,1)} %bitcast.31), custom_call_target="tpu_custom_call" | custom-call | tf_op jit(solution)/shard_map/pallas_call | solution.py:891
  217.5 25.2 %all-to-all-done.4 = bf16[8,256,512]{2,1,0:T(8,128)(2,1)} async-done(((bf16[8,256,512]{2,1,0:T(8,128)(2,1)}), bf16[8,256,512]{2,1,0:T(8,128)(2,1)}, u32[]{:S(2)}, u32[]{:S(2)}) %all-to-all-start.4) | async-done | bytes 2097184 | tf_op jit(solution)/shard_map/all_to_all | solution.py:849
  248.7 9.8 %combine_first.1 = (f32[1024,512]{1,0:T(8,128)}, f32[1024,128]{1,0:T(8,128)}, bf16[3,16,1024]{2,1,0:T(8,128)(2,1)}) custom-call(bf16[2048,512]{1,0:T(8,128)(2,1)} %bitcast.17.back_ref, s32[1024,128]{1,0:T(8,128)} %get-tuple-element.98.place_ref, bf16[512,3328]{1,0:T(8,128)(2,1)} %get-tuple-element.99.tail_ref.refs_2_.refs_3_.w_ref, ...), custom_call_target="tpu_custom_call" | custom-call | tf_op jit(solution)/shard_map/combine_first/pallas_call | solution.py:909
  258.6 15.7 %combine.1 = (bf16[1024,512]{1,0:T(8,128)(2,1)}, f32[1024,128]{1,0:T(8,128)}, f32[1024,128]{1,0:T(8,128)}, f32[1024,128]{1,0:T(8,128)}, f32[8,512]{1,0:T(8,128)}, /*index=5*/bf16[8,8,512]{2,1,0:T(8,128)(2,1)}) custom-call(bf16[2048,512]{1,0:T(8,128)(2,1)} %bitcast.38, f32[1024,512]{1,0:T(8,128)} %get-tuple-element.101.branch_ref, ...), custom_call_target="tpu_custom_call" | custom-call | tf_op jit(solution)/shard_map/combine/pallas_call | solution.py:929
  274.3 7.9 %all_to_all.65.refs_1_.refs_2_ = bf16[8,8,512]{2,1,0:T(8,128)(2,1)} all-to-all(bf16[8,8,512]{2,1,0:T(8,128)(2,1)} %get-tuple-element.111), channel_id=1, replica_groups=mesh['dp'=4,'fsdp'=8] {'fsdp'}, dimensions={0} | all-to-all | bytes 131072 | tf_op jit(solution)/shard_map/all_to_all | solution.py:849
  287.4 15.8 %shard_map.220 = (bf16[4,2048,512]{2,1,0:T(8,128)(2,1)}, bf16[2048,512]{1,0:T(8,128)(2,1)}, bf16[2048,512]{1,0:T(8,128)(2,1)}) custom-call(bf16[2048,512]{1,0:T(8,128)(2,1)} %bitcast.39, bf16[8,8,512]{2,1,0:T(8,128)(2,1)} %all_to_all.65.refs_1_.refs_2_, bf16[512,3328]{1,0:T(8,128)(2,1)} %get-tuple-element.99.tail_ref.refs_2_.refs_3_.w_ref, ...), custom_call_target="tpu_custom_call" | custom-call | tf_op jit(solution)/shard_map/pallas_call | solution.py:971
  308.4 15.8 %shard_map.221 = (bf16[4,2048,512]{2,1,0:T(8,128)(2,1)}, bf16[2048,512]{1,0:T(8,128)(2,1)}, bf16[2048,512]{1,0:T(8,128)(2,1)}) custom-call(bf16[1024,512]{1,0:T(8,128)(2,1)} %bitcast.40, bf16[1024,512]{1,0:T(8,128)(2,1)} %bitcast.41, bf16[8,8,512]{2,1,0:T(8,128)(2,1)} %all_to_all.65.refs_1_.refs_2_, ...), custom_call_target="tpu_custom_call" | custom-call | tf_op jit(solution)/shard_map/pallas_call | solution.py:971
  324.2 27.2 %weight_back.1 = bf16[4,1024,512]{2,1,0:T(8,128)(2,1)} custom-call(bf16[2048,512]{1,0:T(8,128)(2,1)} %bitcast.37, bf16[2048,512]{1,0:T(8,128)(2,1)} %get-tuple-element.138.refs_1_, bf16[4,2048,512]{2,1,0:T(8,128)(2,1)} %get-tuple-element.139.refs_2_, bf16[4,2048,512]{2,1,0:T(8,128)(2,1)} %get-tuple-element.140.refs_3_, ...), custom_call_target="tpu_custom_call" | custom-call | tf_op jit(solution)/shard_map/weight_back/pallas_call | solution.py:1012
  351.4 29.8 %all_to_all.66.second_ref = bf16[8,256,512]{2,1,0:T(8,128)(2,1)} all-to-all(bf16[8,256,512]{2,1,0:T(8,128)(2,1)} %bitcast.43), channel_id=1, replica_groups=mesh['dp'=4,'fsdp'=8] {'fsdp'}, dimensions={0} | all-to-all | bytes 4194304 | tf_op jit(solution)/shard_map/all_to_all | solution.py:849
  381.2 19.9 %hidden_back.1 = (bf16[8,4,16,1536]{3,2,1,0:T(8,128)(2,1)}, f32[1024,512]{1,0:T(8,128)}, bf16[2,1024,128]{2,1,0:T(8,128)(2,1)}, f32[1024,128]{1,0:T(8,128)}, f32[512,128]{1,0:T(8,128)}, /*index=5*/f32[8,512]{1,0:T(8,128)}) custom-call(bf16[8,256,512]{2,1,0:T(8,128)(2,1)} %copy-done.1, bf16[8,256,512]{2,1,0:T(8,128)(2,1)} %all_to_all.66.second_ref, ...), custom_call_target="tpu_custom_call" | custom-call | tf_op jit(solution)/shard_map/hidden_back/pallas_call | solution.py:1036
  406.1 26.5 %shard_map.222 = (bf16[1024,512]{1,0:T(8,128)(2,1)}, bf16[8,4,16,1792]{3,2,1,0:T(8,128)(2,1)}) custom-call(bf16[1024,512]{1,0:T(8,128)(2,1)} %tok_ref.1, bf16[512,3328]{1,0:T(8,128)(2,1)} %get-tuple-element.99.tail_ref.refs_2_.refs_3_.w_ref, s32[1024,8]{1,0:T(8,128)} %copy.54.meta_ref.refs_1_, f32[1024,512]{1,0:T(8,128)} %get-tuple-element.126.gh_ref, ...), custom_call_target="tpu_custom_call" | custom-call | tf_op jit(solution)/shard_map/pallas_call | solution.py:746
  437.8 21.4 %all-to-all-done.10 = bf16[8,4,16,1792]{3,2,1,0:T(8,128)(2,1)S(1)} async-done(((bf16[8,4,16,1792]{3,2,1,0:T(8,128)(2,1)}), bf16[8,4,16,1792]{3,2,1,0:T(8,128)(2,1)S(1)}, u32[]{:S(2)}, u32[]{:S(2)}) %all-to-all-start.10) | async-done | bytes 1835040 | tf_op jit(solution)/shard_map/all_to_all | solution.py:849
  460.2 6.2 %all-to-all-start.12 = ((bf16[4,16,3328]{2,1,0:T(8,128)(2,1)}), bf16[4,16,3328]{2,1,0:T(8,128)(2,1)S(1)}, u32[]{:S(2)}, u32[]{:S(2)}) async-start(bf16[4,16,3328]{2,1,0:T(8,128)(2,1)} %pad_maximum_fusion.2), calls=%async_computation.12 | async-start | bytes 851968 | tf_op jit(solution)/shard_map/all_to_all | solution.py:1104
  467.2 11.8 %all-to-all-done.12 = bf16[4,16,3328]{2,1,0:T(8,128)(2,1)S(1)} async-done(((bf16[4,16,3328]{2,1,0:T(8,128)(2,1)}), bf16[4,16,3328]{2,1,0:T(8,128)(2,1)S(1)}, u32[]{:S(2)}, u32[]{:S(2)}) %all-to-all-start.12) | async-done | bytes 426016 | tf_op jit(solution)/shard_map/all_to_all | solution.py:1104
  (110 shorter events, 81.7 us)
Async XLA Ops:
  7.2 121.3 %all-gather.3.cloned.1.call-start = ((), (), s32[]{:S(2)}) async-start(), calls=%async_computation.15 | async-start | bytes 5242880 | tf_op jit(solution)/shard_map/all_gather | solution.py:825
  9.6 11.3 %collective-permute-start.1 = (bf16[16,3328]{1,0:T(8,128)(2,1)S(1)}, bf16[16,3328]{1,0:T(8,128)(2,1)S(1)}, u32[]{:S(2)}, u32[]{:S(2)}) collective-permute-start(bf16[16,3328]{1,0:T(8,128)(2,1)S(1)} %get-tuple-element.189), channel_id=1, source_target_pairs={{16,0},{24,8},{0,16},{8,24},{17,1},{25,9},{1,17},{9,25},{18,2},{26... | collective-permute-start | bytes 319496 | tf_op jit(solution)/shard_map/ppermute | solution.py:770
  12.3 8.7 %collective-permute-start = (bf16[16,3328]{1,0:T(8,128)(2,1)S(1)}, bf16[16,3328]{1,0:T(8,128)(2,1)S(1)}, u32[]{:S(2)}, u32[]{:S(2)}) collective-permute-start(bf16[16,3328]{1,0:T(8,128)(2,1)S(1)} %get-tuple-element.189), channel_id=1, source_target_pairs={{8,0},{16,8},{24,16},{0,24},{9,1},{17,9},{25,17},{1,25},{10,2},{18... | collective-permute-start | bytes 319496 | tf_op jit(solution)/shard_map/ppermute | solution.py:770
  13.6 7.3 %collective-permute-start.2 = (bf16[16,3328]{1,0:T(8,128)(2,1)S(1)}, bf16[16,3328]{1,0:T(8,128)(2,1)S(1)}, u32[]{:S(2)}, u32[]{:S(2)}) collective-permute-start(bf16[16,3328]{1,0:T(8,128)(2,1)S(1)} %get-tuple-element.189), channel_id=1, source_target_pairs={{24,0},{0,8},{8,16},{16,24},{25,1},{1,9},{9,17},{17,25},{26,2},{2,... | collective-permute-start | bytes 319496 | tf_op jit(solution)/shard_map/ppermute | solution.py:770
  21.1 10.8 %collective-permute-start.6 = (bf16[4,16,3328]{2,1,0:T(8,128)(2,1)S(1)}, bf16[4,16,3328]{2,1,0:T(8,128)(2,1)S(1)}, u32[]{:S(2)}, u32[]{:S(2)}) collective-permute-start(bf16[4,16,3328]{2,1,0:T(8,128)(2,1)S(1)} %pad_maximum_fusion.1.refs_2_), channel_id=1, source_target_pairs={{0,4},{1,5},{2,6},{3,7},{4,0},{5,1},{6,2},{7,3},{8,12},{9,13},{10,... | collective-permute-start | bytes 1277960 | tf_op jit(solution)/shard_map/ppermute | solution.py:774
  22.7 10.9 %collective-permute-start.4 = (bf16[4,16,3328]{2,1,0:T(8,128)(2,1)S(1)}, bf16[4,16,3328]{2,1,0:T(8,128)(2,1)S(1)}, u32[]{:S(2)}, u32[]{:S(2)}) collective-permute-start(bf16[4,16,3328]{2,1,0:T(8,128)(2,1)S(1)} %pad_maximum_fusion.1.refs_2_), channel_id=1, source_target_pairs={{0,2},{1,3},{2,0},{3,1},{4,6},{5,7},{6,4},{7,5},{8,10},{9,11},{10,... | collective-permute-start | bytes 1277960 | tf_op jit(solution)/shard_map/ppermute | solution.py:774
  33.5 6.0 %collective-permute-start.8 = (bf16[2,16,3328]{2,1,0:T(8,128)(2,1)S(1)}, bf16[2,16,3328]{2,1,0:T(8,128)(2,1)}, u32[]{:S(2)}, u32[]{:S(2)}) collective-permute-start(bf16[2,16,3328]{2,1,0:T(8,128)(2,1)S(1)} %slice.40), channel_id=1, source_target_pairs={{0,4},{1,5},{2,6},{3,7},{4,0},{5,1},{6,2},{7,3},{8,12},{9,13},{10,... | collective-permute-start | bytes 638984 | tf_op jit(solution)/shard_map/ppermute | solution.py:774
  34.1 19.4 %collective-permute-start.3 = (bf16[4,16,3328]{2,1,0:T(8,128)(2,1)S(1)}, bf16[4,16,3328]{2,1,0:T(8,128)(2,1)S(1)}, u32[]{:S(2)}, u32[]{:S(2)}) collective-permute-start(bf16[4,16,3328]{2,1,0:T(8,128)(2,1)S(1)} %pad_maximum_fusion.1.refs_2_), channel_id=1, source_target_pairs={{0,1},{1,0},{2,3},{3,2},{4,5},{5,4},{6,7},{7,6},{8,9},{9,8},{10,11... | collective-permute-start | bytes 1277960 | tf_op jit(solution)/shard_map/ppermute | solution.py:774
  34.1 19.5 %collective-permute-start.7 = (bf16[4,16,3328]{2,1,0:T(8,128)(2,1)S(1)}, bf16[4,16,3328]{2,1,0:T(8,128)(2,1)S(1)}, u32[]{:S(2)}, u32[]{:S(2)}) collective-permute-start(bf16[4,16,3328]{2,1,0:T(8,128)(2,1)S(1)} %collective-permute-done.6.refs_6_), channel_id=1, source_target_pairs={{0,1},{1,0},{2,3},{3,2},{4,5},{5,4},{6,7},{7,6},{8,9},{9,8},{10,11... | collective-permute-start | bytes 1277960 | tf_op jit(solution)/shard_map/ppermute | solution.py:774
  34.6 19.0 %collective-permute-start.5 = (bf16[4,16,3328]{2,1,0:T(8,128)(2,1)S(1)}, bf16[4,16,3328]{2,1,0:T(8,128)(2,1)S(1)}, u32[]{:S(2)}, u32[]{:S(2)}) collective-permute-start(bf16[4,16,3328]{2,1,0:T(8,128)(2,1)S(1)} %collective-permute-done.4.refs_4_), channel_id=1, source_target_pairs={{0,1},{1,0},{2,3},{3,2},{4,5},{5,4},{6,7},{7,6},{8,9},{9,8},{10,11... | collective-permute-start | bytes 1277960 | tf_op jit(solution)/shard_map/ppermute | solution.py:774
  37.8 15.8 %collective-permute-start.11 = (bf16[2,16,3328]{2,1,0:T(8,128)(2,1)S(1)}, bf16[2,16,3328]{2,1,0:T(8,128)(2,1)S(1)}, u32[]{:S(2)}, u32[]{:S(2)}) collective-permute-start(bf16[2,16,3328]{2,1,0:T(8,128)(2,1)S(1)} %collective-permute-done.9.refs_9_), channel_id=1, source_target_pairs={{0,1},{1,0},{2,3},{3,2},{4,5},{5,4},{6,7},{7,6},{8,9},{9,8},{10,11... | collective-permute-start | bytes 638984 | tf_op jit(solution)/shard_map/ppermute | solution.py:774
  39.6 14.0 %collective-permute-start.10 = (bf16[2,16,3328]{2,1,0:T(8,128)(2,1)}, bf16[2,16,3328]{2,1,0:T(8,128)(2,1)S(1)}, u32[]{:S(2)}, u32[]{:S(2)}) collective-permute-start(bf16[2,16,3328]{2,1,0:T(8,128)(2,1)} %collective-permute-done.8.refs_8_), channel_id=1, source_target_pairs={{0,1},{1,0},{2,3},{3,2},{4,5},{5,4},{6,7},{7,6},{8,9},{9,8},{10,11... | collective-permute-start | bytes 638984 | tf_op jit(solution)/shard_map/ppermute | solution.py:774
  54.7 35.9 %all-to-all-start = ((bf16[8,256,512]{2,1,0:T(8,128)(2,1)}), bf16[8,256,512]{2,1,0:T(8,128)(2,1)S(1)}, u32[]{:S(2)}, u32[]{:S(2)}) async-start(bf16[8,256,512]{2,1,0:T(8,128)(2,1)} %get-tuple-element.90), calls=%async_computation | async-start | bytes 4194304 | tf_op jit(solution)/shard_map/all_to_all | solution.py:849
  92.0 29.3 %all-to-all-start.1 = ((bf16[8,256,512]{2,1,0:T(8,128)(2,1)}), bf16[8,256,512]{2,1,0:T(8,128)(2,1)S(1)}, u32[]{:S(2)}, u32[]{:S(2)}) async-start(bf16[8,256,512]{2,1,0:T(8,128)(2,1)} %shard_map.217), calls=%async_computation.1 | async-start | bytes 4194304 | tf_op jit(solution)/shard_map/all_to_all | solution.py:849
  122.6 31.1 %all-to-all-start.2 = ((bf16[8,256,512]{2,1,0:T(8,128)(2,1)}), bf16[8,256,512]{2,1,0:T(8,128)(2,1)}, u32[]{:S(2)}, u32[]{:S(2)}) async-start(bf16[8,256,512]{2,1,0:T(8,128)(2,1)} %shard_map.216), calls=%async_computation.2 | async-start | bytes 4194304 | tf_op jit(solution)/shard_map/all_to_all | solution.py:849
  180.2 31.4 %all-to-all-start.3 = ((bf16[8,256,512]{2,1,0:T(8,128)(2,1)}), bf16[8,256,512]{2,1,0:T(8,128)(2,1)S(1)}, u32[]{:S(2)}, u32[]{:S(2)}) async-start(bf16[8,256,512]{2,1,0:T(8,128)(2,1)} %bitcast.45), calls=%async_computation.3 | async-start | bytes 4194304 | tf_op jit(solution)/shard_map/all_to_all | solution.py:849
  213.0 29.7 %all-to-all-start.4 = ((bf16[8,256,512]{2,1,0:T(8,128)(2,1)}), bf16[8,256,512]{2,1,0:T(8,128)(2,1)}, u32[]{:S(2)}, u32[]{:S(2)}) async-start(bf16[8,256,512]{2,1,0:T(8,128)(2,1)} %bitcast.44), calls=%async_computation.4 | async-start | bytes 4194304 | tf_op jit(solution)/shard_map/all_to_all | solution.py:849
  242.7 31.6 %all-to-all-start.5 = ((bf16[8,128,512]{2,1,0:T(8,128)(2,1)}), bf16[8,128,512]{2,1,0:T(8,128)(2,1)S(1)}, u32[]{:S(2)}, u32[]{:S(2)}) async-start(bf16[8,128,512]{2,1,0:T(8,128)(2,1)} %get-tuple-element.110), calls=%async_computation.5 | async-start | bytes 2097152 | tf_op jit(solution)/shard_map/all_to_all | solution.py:849
  282.2 21.0 %all-to-all-start.8 = ((bf16[8,128,512]{2,1,0:T(8,128)(2,1)}), bf16[8,128,512]{2,1,0:T(8,128)(2,1)S(1)}, u32[]{:S(2)}, u32[]{:S(2)}) async-start(bf16[8,128,512]{2,1,0:T(8,128)(2,1)} %get-tuple-element.117), calls=%async_computation.8 | async-start | bytes 2097152 | tf_op jit(solution)/shard_map/all_to_all | solution.py:849
  304.2 47.3 %all-to-all-start.7 = ((bf16[8,256,512]{2,1,0:T(8,128)(2,1)}), bf16[8,256,512]{2,1,0:T(8,128)(2,1)S(1)}, u32[]{:S(2)}, u32[]{:S(2)}) async-start(bf16[8,256,512]{2,1,0:T(8,128)(2,1)} %bitcast.42), calls=%async_computation.7 | async-start | bytes 4194304 | tf_op jit(solution)/shard_map/all_to_all | solution.py:849
  308.4 173.3 %reduce-scatter.2.cloned.1.call-start = ((), (), s32[]{:S(2)}) async-start(), calls=%async_computation.14 | async-start | bytes 5242880 | tf_op jit(solution)/shard_map/reduce_scatter | solution.py:1023
  401.1 31.5 %all-to-all-start.11 = ((bf16[8,4,16,1536]{3,2,1,0:T(8,128)(2,1)}), bf16[8,4,16,1536]{3,2,1,0:T(8,128)(2,1)S(1)}, u32[]{:S(2)}, u32[]{:S(2)}) async-start(bf16[8,4,16,1536]{3,2,1,0:T(8,128)(2,1)} %get-tuple-element.137), calls=%async_computation.11 | async-start | bytes 3145728 | tf_op jit(solution)/shard_map/all_to_all | solution.py:849
  432.6 26.5 %all-to-all-start.10 = ((bf16[8,4,16,1792]{3,2,1,0:T(8,128)(2,1)}), bf16[8,4,16,1792]{3,2,1,0:T(8,128)(2,1)S(1)}, u32[]{:S(2)}, u32[]{:S(2)}) async-start(bf16[8,4,16,1792]{3,2,1,0:T(8,128)(2,1)} %get-tuple-element.136), calls=%async_computation.10 | async-start | bytes 3670016 | tf_op jit(solution)/shard_map/all_to_all | solution.py:849
  460.2 18.8 %all-to-all-start.12 = ((bf16[4,16,3328]{2,1,0:T(8,128)(2,1)}), bf16[4,16,3328]{2,1,0:T(8,128)(2,1)S(1)}, u32[]{:S(2)}, u32[]{:S(2)}) async-start(bf16[4,16,3328]{2,1,0:T(8,128)(2,1)} %pad_maximum_fusion.2), calls=%async_computation.12 | async-start | bytes 851968 | tf_op jit(solution)/shard_map/all_to_all | solution.py:1104
  (23 other events, 315.5 us)
Sparse Core Ops, SparseCore 0:
  25.6 81.2 all-gather.2
  351.5 79.2 reduce-scatter.1
